TPU v7x, 256 devices: a whole 4x4x8 slice. The times are simulated.
256 devices in a mesh: dom: 64 (over x, z, core), ang: 4 (over y).
Axes of the slice: x: 4, y: 4, z: 8, core: 2. Of those that a mesh axis runs over, the one named last changes fastest.
Arguments:
- incident: bfloat16 [1024, 2, 64, 512], P('dom', None, 'ang'), may hold values from -6 to 6
- response: bfloat16 [1024, 2, 512, 512], P('dom', None, None, 'ang'), may hold values from -0.25 to 0.25
- jitter: int32 [1024], P('dom'), may hold values from 0 to 63
- block_cols: int32 [512, 12], P('dom'), may hold values from 0 to 511, as said below
- block_counts: int32 [512], P('dom'), may hold values from 1 to 12
- green_blocks: bfloat16 [512, 12, 2, 128, 128], P('dom'), may hold values from -0.15625 to 0.15625
Outputs:
- near_field: float32 [2, 64, 65536], P(None, 'ang', 'dom')
Inputs may be any that keep to these rules, and one draw needn't show every extreme that they name: `block_cols`: block row r lies on device r // 8 of dom; every column block it names lies on a device at most 3 away along dom, and that distance is reached in every draw by a live entry.
All inputs are finite; a program needn't handle non-finite values.
Results may differ from a plain program's by a relative error of at most 0.0041.
Values may be sent and summed in bfloat16 or wider, within the bound.
No kernel may reach another device: no remote copies, remote signals or barrier semaphores. Data moves between devices by JAX's collectives and lax.ppermute only.
A program may use at most 64 MiB of HBM per device.

v0:
```python
import jax
import jax.numpy as jnp
from jax import lax
from jax.sharding import PartitionSpec as P

STRIDE = 64
REACH = 3


def shifted(block, axis, distance):
    devices = range(lax.axis_size(axis))
    route = [(i - distance, i) for i in devices if i - distance in devices]
    return lax.ppermute(block, axis, route)


def place(fields, starts, length):
    width = fields.shape[3]
    source = lax.broadcasted_iota(jnp.int32, (width, length), 0)
    target = lax.broadcasted_iota(jnp.int32, (width, length), 1)
    shifter = (target[None] == source[None] + starts[:, None, None]).astype(jnp.bfloat16)
    placed = jnp.einsum("dxan,dnc->dxac", fields, shifter, preferred_element_type=jnp.float32)
    return placed.astype(jnp.bfloat16)


def intersection_add(placed, stride):
    number = placed.shape[0]
    angle_rows = placed.shape[2]
    parts = placed.shape[3] // stride
    pieces = placed.reshape(number, 2, angle_rows, parts, stride)
    summed = jnp.zeros((number + parts - 1, 2, angle_rows, stride), jnp.float32)
    for part_index in range(parts):
        summed = summed.at[part_index : part_index + number].add(
            pieces[:, :, :, part_index].astype(jnp.float32)
        )
    return jnp.transpose(summed, (1, 2, 0, 3)).reshape(2, angle_rows, (number + parts - 1) * stride)


def per_device(incident, response, jitter, block_cols, block_counts, green_blocks):
    domain_width = incident.shape[3]
    panel_cols = response.shape[3]
    domains_here = incident.shape[0]
    shard_piece = lax.all_gather(incident, "ang", axis=2, tiled=True)
    real_part = jnp.einsum(
        "dan,dnc->dac", shard_piece[:, 0], response[:, 0], preferred_element_type=jnp.float32
    ) - jnp.einsum(
        "dan,dnc->dac", shard_piece[:, 1], response[:, 1], preferred_element_type=jnp.float32
    )
    imag_part = jnp.einsum(
        "dan,dnc->dac", shard_piece[:, 0], response[:, 1], preferred_element_type=jnp.float32
    ) + jnp.einsum(
        "dan,dnc->dac", shard_piece[:, 1], response[:, 0], preferred_element_type=jnp.float32
    )
    fields = jnp.stack([real_part, imag_part], 1).astype(jnp.bfloat16)
    start_cols = jitter + lax.axis_index("ang") * panel_cols
    partial_plane = intersection_add(place(fields, start_cols, domain_width + STRIDE), STRIDE)
    buffer = lax.psum_scatter(partial_plane, "ang", scatter_dimension=1, tiled=True)
    plane_width = domains_here * STRIDE
    plane = buffer[:, :, :plane_width]
    arrived = shifted(buffer[:, :, plane_width:], "dom", 1)
    plane = plane.at[:, :, :domain_width].add(arrived)
    stitched = plane.astype(jnp.bfloat16)
    block_size = green_blocks.shape[3]
    rows_here = block_cols.shape[0]
    pieces = []
    for offset_dev in range(-REACH, REACH + 1):
        if offset_dev == 0:
            pieces.append(stitched)
        else:
            pieces.append(shifted(stitched, "dom", -offset_dev))
    window = jnp.concatenate(pieces, 2)
    local_cols = block_cols - (lax.axis_index("dom") - REACH) * rows_here
    blocks = window.reshape(2, window.shape[1], window.shape[2] // block_size, block_size)
    picked = jnp.take(blocks, local_cols, axis=2)
    live = lax.broadcasted_iota(jnp.int32, block_cols.shape, 1) < block_counts[:, None]
    picked = jnp.where(live[None, None, :, :, None], picked, jnp.zeros((), picked.dtype))
    real_part = jnp.einsum(
        "arkp,rkpq->arq", picked[0], green_blocks[:, :, 0], preferred_element_type=jnp.float32
    ) - jnp.einsum(
        "arkp,rkpq->arq", picked[1], green_blocks[:, :, 1], preferred_element_type=jnp.float32
    )
    imag_part = jnp.einsum(
        "arkp,rkpq->arq", picked[0], green_blocks[:, :, 1], preferred_element_type=jnp.float32
    ) + jnp.einsum(
        "arkp,rkpq->arq", picked[1], green_blocks[:, :, 0], preferred_element_type=jnp.float32
    )
    coupled = jnp.stack([real_part, imag_part], 0)
    return coupled.reshape(2, coupled.shape[1], rows_here * block_size)


def solution(mesh):
    return jax.shard_map(
        per_device,
        mesh=mesh,
        in_specs=(
            P("dom", None, "ang", None),
            P("dom", None, None, "ang"),
            P("dom"),
            P("dom", None),
            P("dom"),
            P("dom", None, None, None, None),
        ),
        out_specs=P(None, "ang", "dom"),
        check_vma=False,
    )
```

profile of v0, /device:TPU:7, one launch (start us, length us, event | category | flops | bytes accessed | tf_op | source)
XLA Modules:
  0.0 138.6 jit_solution(16391417775437848845)
XLA Ops:
  6.5 1.9 %copy.40 = bf16[16,2,16,512]{3,2,0,1:T(8,128)(2,1)} copy(bf16[16,2,16,512]{3,2,1,0:T(8,128)(2,1)} %param.26) | data formatting | bytes 1048576 | tf_op args[0]
  8.4 0.0 all-gather.2.cloned.1.call-update
  8.5 0.0 reduce-scatter.2.cloned.1.call-start
  8.5 0.7 broadcast_add_fusion
  9.2 36.3 %all-gather.2.cloned.1.call-done = bf16[16,2,64,512]{3,2,0,1:T(8,128)(2,1)} async-done(((bf16[16,2,16,512]{3,2,0,1:T(8,128)(2,1)}), bf16[16,2,64,512]{3,2,0,1:T(8,128)(2,1)}) %all-gather.2.cloned.1.call-update) | async-done | bytes 2097168 | tf_op jit(solution)/shard_map/all_gather | solution.py:42
  45.5 2.6 %fusion.18 = f32[16,64,128]{2,1,0:T(8,128)S(1)} fusion(bf16[16,2,512,128]{3,2,1,0:T(8,128)(2,1)} %param.27, bf16[16,2,64,512]{3,2,0,1:T(8,128)(2,1)} %all-gather.2.cloned.1.call-done), kind=kOutput, calls=%fused_computation.19 | convolution fusion | flops 134217728 | bytes 3670016 | tf_op jit(solution)/shard_map/dan,dnc->dac/dot_general | solution.py:45
  48.1 2.5 %fusion.16 = f32[16,64,128]{2,1,0:T(8,128)S(1)} fusion(bf16[16,2,512,128]{3,2,1,0:T(8,128)(2,1)} %param.27, bf16[16,2,64,512]{3,2,0,1:T(8,128)(2,1)} %all-gather.2.cloned.1.call-done), kind=kOutput, calls=%fused_computation.17 | convolution fusion | flops 134217728 | bytes 3670016 | tf_op jit(solution)/shard_map/dan,dnc->dac/dot_general | solution.py:48
  50.7 0.1 copy-done.4
  50.8 0.5 fusion.43
  51.3 0.5 fusion.46
  51.8 1.3 fusion.24
  53.1 4.2 %copy.44 = bf16[16,2,64,576]{2,3,1,0:T(8,128)(2,1)} copy(bf16[16,2,64,576]{3,2,1,0:T(8,128)(2,1)S(1)} %fusion.24) | data formatting | bytes 4718592 | tf_op jit(solution)/shard_map/convert_element_type | solution.py:22
  57.3 1.2 slice_bitcast_fusion.14
  58.5 0.2 pad_convert_fusion
  58.7 1.5 %fusion.80 = f32[24,2,64,64]{2,3,1,0:T(8,128)S(1)} fusion(f32[24,2,64,64]{2,3,1,0:T(8,128)S(1)} %pad_convert_fusion, bf16[16,2,64,9,64]{2,4,3,1,0:T(8,128)(2,1)} %bitcast.179), kind=kLoop, calls=%fused_computation.59 | loop fusion | flops 262144 | bytes 2359296 | tf_op jit(solution)/shard_map/scatter-add | solution.py:32
  60.2 0.3 fusion.79
  60.5 0.3 fusion.78
  60.7 0.3 fusion.77
  61.0 0.3 fusion.76
  61.3 0.3 fusion.75
  61.5 0.3 fusion.74
  61.8 0.3 fusion.73
  62.1 0.5 copy.53
  62.6 1.3 reshape.388
  64.0 24.1 %reduce-scatter.2.cloned.1.call-done = f32[2,16,1536]{2,1,0:T(8,128)} async-done(((f32[2,64,1536]{2,1,0:T(8,128)}), f32[2,16,1536]{2,1,0:T(8,128)}) %reduce-scatter.2.cloned.1.call-update) | async-done | bytes 196624 | tf_op jit(solution)/shard_map/reduce_scatter | solution.py:56
  88.1 0.8 slice.399
  88.9 4.9 %collective-permute-start = (f32[2,16,512]{2,1,0:T(8,128)S(1)}, f32[2,16,512]{2,1,0:T(8,128)S(1)}, u32[]{:S(2)}, u32[]{:S(2)}) collective-permute-start(f32[2,16,512]{2,1,0:T(8,128)S(1)} %slice.399), channel_id=1, source_target_pairs={{0,4},{4,8},{8,12},{12,16},{16,20},{20,24},{24,28},{28,32},{32,36}... | collective-permute-start | bytes 196616 | tf_op jit(solution)/shard_map/ppermute | solution.py:13
  93.8 0.1 compare_and_fusion
  93.9 0.1 reshape.400
  94.0 0.9 slice.397
  94.9 0.2 collective-permute-done
  95.1 0.8 fusion.82
  95.9 5.2 %collective-permute-start.1 = (bf16[2,16,1024]{2,1,0:T(8,128)(2,1)S(1)}, bf16[2,16,1024]{2,1,0:T(8,128)(2,1)S(1)}, u32[]{:S(2)}, u32[]{:S(2)}) collective-permute-start(bf16[2,16,1024]{2,1,0:T(8,128)(2,1)S(1)} %fusion.82), channel_id=1, source_target_pairs={{0,12},{4,16},{8,20},{12,24},{16,28},{20,32},{24,36},{28,40},{32,4... | collective-permute-start | bytes 196616 | tf_op jit(solution)/shard_map/ppermute | solution.py:13
  101.2 3.2 %collective-permute-start.2 = (bf16[2,16,1024]{2,1,0:T(8,128)(2,1)S(1)}, bf16[2,16,1024]{2,1,0:T(8,128)(2,1)S(1)}, u32[]{:S(2)}, u32[]{:S(2)}) collective-permute-start(bf16[2,16,1024]{2,1,0:T(8,128)(2,1)S(1)} %fusion.82), channel_id=1, source_target_pairs={{0,8},{4,12},{8,16},{12,20},{16,24},{20,28},{24,32},{28,36},{32,40... | collective-permute-start | bytes 196616 | tf_op jit(solution)/shard_map/ppermute | solution.py:13
  104.4 2.9 %collective-permute-start.3 = (bf16[2,16,1024]{2,1,0:T(8,128)(2,1)S(1)}, bf16[2,16,1024]{2,1,0:T(8,128)(2,1)S(1)}, u32[]{:S(2)}, u32[]{:S(2)}) collective-permute-start(bf16[2,16,1024]{2,1,0:T(8,128)(2,1)S(1)} %fusion.82), channel_id=1, source_target_pairs={{0,4},{4,8},{8,12},{12,16},{16,20},{20,24},{24,28},{28,32},{32,36}... | collective-permute-start | bytes 196616 | tf_op jit(solution)/shard_map/ppermute | solution.py:13
  107.2 1.9 %collective-permute-start.4 = (bf16[2,16,1024]{2,1,0:T(8,128)(2,1)S(1)}, bf16[2,16,1024]{2,1,0:T(8,128)(2,1)S(1)}, u32[]{:S(2)}, u32[]{:S(2)}) collective-permute-start(bf16[2,16,1024]{2,1,0:T(8,128)(2,1)S(1)} %fusion.82), channel_id=1, source_target_pairs={{4,0},{8,4},{12,8},{16,12},{20,16},{24,20},{28,24},{32,28},{36,32}... | collective-permute-start | bytes 196616 | tf_op jit(solution)/shard_map/ppermute | solution.py:13
  109.2 3.7 %collective-permute-start.5 = (bf16[2,16,1024]{2,1,0:T(8,128)(2,1)S(1)}, bf16[2,16,1024]{2,1,0:T(8,128)(2,1)S(1)}, u32[]{:S(2)}, u32[]{:S(2)}) collective-permute-start(bf16[2,16,1024]{2,1,0:T(8,128)(2,1)S(1)} %fusion.82), channel_id=1, source_target_pairs={{8,0},{12,4},{16,8},{20,12},{24,16},{28,20},{32,24},{36,28},{40,32... | collective-permute-start | bytes 196616 | tf_op jit(solution)/shard_map/ppermute | solution.py:13
  112.9 4.5 %collective-permute-start.6 = (bf16[2,16,1024]{2,1,0:T(8,128)(2,1)S(1)}, bf16[2,16,1024]{2,1,0:T(8,128)(2,1)S(1)}, u32[]{:S(2)}, u32[]{:S(2)}) collective-permute-start(bf16[2,16,1024]{2,1,0:T(8,128)(2,1)S(1)} %fusion.82), channel_id=1, source_target_pairs={{12,0},{16,4},{20,8},{24,12},{28,16},{32,20},{36,24},{40,28},{44,3... | collective-permute-start | bytes 196616 | tf_op jit(solution)/shard_map/ppermute | solution.py:13
  117.5 2.4 %collective-permute-done.6 = bf16[2,16,1024]{2,1,0:T(8,128)(2,1)S(1)} collective-permute-done((bf16[2,16,1024]{2,1,0:T(8,128)(2,1)S(1)}, bf16[2,16,1024]{2,1,0:T(8,128)(2,1)S(1)}, u32[]{:S(2)}, u32[]{:S(2)}) %collective-permute-start.6) | collective-permute-done | bytes 65568 | tf_op jit(solution)/shard_map/ppermute | solution.py:13
  119.9 0.1 copy_bitcast_fusion
  120.0 0.7 gather_fusion
  120.7 0.1 copy.55
  120.9 0.3 select_bitcast_fusion
  121.1 2.4 %fusion.49 = f32[8,16,128]{2,1,0:T(8,128)S(1)} fusion(bf16[8,12,2,128,128]{4,3,2,1,0:T(8,128)(2,1)} %param.31, bf16[2,16,8,12,128]{4,1,3,2,0:T(8,128)(2,1)S(1)} %select_bitcast_fusion), kind=kOutput, calls=%fused_computation.36 | convolution fusion | flops 50331648 | bytes 3604480 | tf_op jit(solution)/shard_map/arkp,rkpq->arq/dot_general | solution.py:76
  123.6 2.4 %fusion.52 = f32[8,16,128]{2,1,0:T(8,128)S(1)} fusion(bf16[8,12,2,128,128]{4,3,2,1,0:T(8,128)(2,1)} %param.31, bf16[2,16,8,12,128]{4,1,3,2,0:T(8,128)(2,1)S(1)} %select_bitcast_fusion), kind=kOutput, calls=%fused_computation.37 | convolution fusion | flops 50331648 | bytes 3604480 | tf_op jit(solution)/shard_map/arkp,rkpq->arq/dot_general | solution.py:83
  126.0 2.4 %fusion.70 = f32[16,8,128]{2,0,1:T(8,128)S(1)} fusion(f32[8,16,128]{2,1,0:T(8,128)S(1)} %fusion.49, bf16[8,12,2,128,128]{4,3,2,1,0:T(8,128)(2,1)} %param.31, bf16[2,16,8,12,128]{4,1,3,2,0:T(8,128)(2,1)S(1)} %select_bitcast_fusion), kind=kOutput, calls=%fused_computation.43 | convolution fusion | flops 50348032 | bytes 3670016 | tf_op jit(solution)/shard_map/arkp,rkpq->arq/dot_general | solution.py:78
  128.5 2.4 %fusion.64 = f32[16,8,128]{2,0,1:T(8,128)S(1)} fusion(f32[8,16,128]{2,1,0:T(8,128)S(1)} %fusion.52, bf16[8,12,2,128,128]{4,3,2,1,0:T(8,128)(2,1)} %param.31, bf16[2,16,8,12,128]{4,1,3,2,0:T(8,128)(2,1)S(1)} %select_bitcast_fusion), kind=kOutput, calls=%fused_computation.41 | convolution fusion | flops 50348032 | bytes 3670016 | tf_op jit(solution)/shard_map/arkp,rkpq->arq/dot_general | solution.py:81
  131.1 0.7 pad_maximum_fusion.1
  (28 shorter events, 0.2 us)
Async XLA Ops:
  6.5 39.0 %all-gather.2.cloned.1.call-start = ((), (), s32[]{:S(2)}) async-start(), calls=%async_computation.1 | async-start | bytes 2621440 | tf_op jit(solution)/shard_map/all_gather | solution.py:42
  8.5 79.6 %reduce-scatter.2.cloned.1.call-start = ((), (), s32[]{:S(2)}) async-start(), calls=%async_computation.2 | async-start | bytes 983040 | tf_op jit(solution)/shard_map/reduce_scatter | solution.py:56
  45.5 5.1 %copy-start.3 = (bf16[16,2,512,128]{3,2,1,0:T(8,128)(2,1)S(1)}, bf16[16,2,512,128]{3,2,1,0:T(8,128)(2,1)}, u32[]{:S(2)}) copy-start(bf16[16,2,512,128]{3,2,1,0:T(8,128)(2,1)} %param.27) | copy-start | bytes 12582916
  48.1 2.7 %copy-start.4 = (bf16[16,2,64,512]{3,2,0,1:T(8,128)(2,1)S(1)}, bf16[16,2,64,512]{3,2,0,1:T(8,128)(2,1)}, u32[]{:S(2)}) copy-start(bf16[16,2,64,512]{3,2,0,1:T(8,128)(2,1)} %all-gather.2.cloned.1.call-done) | copy-start | bytes 6291460
  57.3 2.9 %copy-start = (bf16[16,2,64,576]{2,3,1,0:T(8,128)(2,1)S(1)}, bf16[16,2,64,576]{2,3,1,0:T(8,128)(2,1)}, u32[]{:S(2)}) copy-start(bf16[16,2,64,576]{2,3,1,0:T(8,128)(2,1)} %copy.44) | copy-start | bytes 7077892
  62.6 31.2 %copy-start.1 = (s32[8,12]{1,0:T(8,128)S(1)}, s32[8,12]{1,0:T(8,128)}, u32[]{:S(2)}) copy-start(s32[8,12]{1,0:T(8,128)} %param.29) | copy-start | bytes 1156
  62.6 31.2 %copy-start.2 = (s32[8]{0:T(128)S(1)}, s32[8]{0:T(128)}, u32[]{:S(2)}) copy-start(s32[8]{0:T(128)} %param.30) | copy-start | bytes 100
  88.9 6.2 %collective-permute-start = (f32[2,16,512]{2,1,0:T(8,128)S(1)}, f32[2,16,512]{2,1,0:T(8,128)S(1)}, u32[]{:S(2)}, u32[]{:S(2)}) collective-permute-start(f32[2,16,512]{2,1,0:T(8,128)S(1)} %slice.399), channel_id=1, source_target_pairs={{0,4},{4,8},{8,12},{12,16},{16,20},{20,24},{24,28},{28,32},{32,36}... | collective-permute-start | bytes 196616 | tf_op jit(solution)/shard_map/ppermute | solution.py:13
  95.9 17.0 %collective-permute-start.1 = (bf16[2,16,1024]{2,1,0:T(8,128)(2,1)S(1)}, bf16[2,16,1024]{2,1,0:T(8,128)(2,1)S(1)}, u32[]{:S(2)}, u32[]{:S(2)}) collective-permute-start(bf16[2,16,1024]{2,1,0:T(8,128)(2,1)S(1)} %fusion.82), channel_id=1, source_target_pairs={{0,12},{4,16},{8,20},{12,24},{16,28},{20,32},{24,36},{28,40},{32,4... | collective-permute-start | bytes 196616 | tf_op jit(solution)/shard_map/ppermute | solution.py:13
  101.2 16.2 %collective-permute-start.2 = (bf16[2,16,1024]{2,1,0:T(8,128)(2,1)S(1)}, bf16[2,16,1024]{2,1,0:T(8,128)(2,1)S(1)}, u32[]{:S(2)}, u32[]{:S(2)}) collective-permute-start(bf16[2,16,1024]{2,1,0:T(8,128)(2,1)S(1)} %fusion.82), channel_id=1, source_target_pairs={{0,8},{4,12},{8,16},{12,20},{16,24},{20,28},{24,32},{28,36},{32,40... | collective-permute-start | bytes 196616 | tf_op jit(solution)/shard_map/ppermute | solution.py:13
  104.4 13.1 %collective-permute-start.3 = (bf16[2,16,1024]{2,1,0:T(8,128)(2,1)S(1)}, bf16[2,16,1024]{2,1,0:T(8,128)(2,1)S(1)}, u32[]{:S(2)}, u32[]{:S(2)}) collective-permute-start(bf16[2,16,1024]{2,1,0:T(8,128)(2,1)S(1)} %fusion.82), channel_id=1, source_target_pairs={{0,4},{4,8},{8,12},{12,16},{16,20},{20,24},{24,28},{28,32},{32,36}... | collective-permute-start | bytes 196616 | tf_op jit(solution)/shard_map/ppermute | solution.py:13
  107.2 10.2 %collective-permute-start.4 = (bf16[2,16,1024]{2,1,0:T(8,128)(2,1)S(1)}, bf16[2,16,1024]{2,1,0:T(8,128)(2,1)S(1)}, u32[]{:S(2)}, u32[]{:S(2)}) collective-permute-start(bf16[2,16,1024]{2,1,0:T(8,128)(2,1)S(1)} %fusion.82), channel_id=1, source_target_pairs={{4,0},{8,4},{12,8},{16,12},{20,16},{24,20},{28,24},{32,28},{36,32}... | collective-permute-start | bytes 196616 | tf_op jit(solution)/shard_map/ppermute | solution.py:13
  109.2 8.3 %collective-permute-start.5 = (bf16[2,16,1024]{2,1,0:T(8,128)(2,1)S(1)}, bf16[2,16,1024]{2,1,0:T(8,128)(2,1)S(1)}, u32[]{:S(2)}, u32[]{:S(2)}) collective-permute-start(bf16[2,16,1024]{2,1,0:T(8,128)(2,1)S(1)} %fusion.82), channel_id=1, source_target_pairs={{8,0},{12,4},{16,8},{20,12},{24,16},{28,20},{32,24},{36,28},{40,32... | collective-permute-start | bytes 196616 | tf_op jit(solution)/shard_map/ppermute | solution.py:13
  112.9 7.0 %collective-permute-start.6 = (bf16[2,16,1024]{2,1,0:T(8,128)(2,1)S(1)}, bf16[2,16,1024]{2,1,0:T(8,128)(2,1)S(1)}, u32[]{:S(2)}, u32[]{:S(2)}) collective-permute-start(bf16[2,16,1024]{2,1,0:T(8,128)(2,1)S(1)} %fusion.82), channel_id=1, source_target_pairs={{12,0},{16,4},{20,8},{24,12},{28,16},{32,20},{36,24},{40,28},{44,3... | collective-permute-start | bytes 196616 | tf_op jit(solution)/shard_map/ppermute | solution.py:13
Sparse Core Ops, SparseCore 0:
  9.2 36.3 all-gather.1
  64.1 23.9 reduce-scatter.1
where the time goes:
time: 141 us; the launch traced here: 139 us
  waiting for transfers between devices  63.1 us (45%)
  starting transfers between devices  26.3 us (19%)
  matrix products  17.2 us (12%)
  between operations  13.8 us (10%)
  local copies, waits for them, and re-layouts  12.2 us (9%)
  other arithmetic  5.97 us (4%)
    all_gather x1, waiting for transfers between devices, per_device(): shard_piece = lax.all_gather(incident, 'ang', axis=2, tiled=True)  36.3 us
    ppermute x7, starting transfers between devices, shifted(): return lax.ppermute(block, axis, route)  26.2 us
    reduce_scatter x1, waiting for transfers between devices, per_device(): lax.psum_scatter(partial_plane, 'ang', scatter_dimension=1, tiled=True)  24.1 us
    convert_element_type x1, local copies, waits for them, and re-layouts, place(): return placed.astype(jnp.bfloat16)  4.19 us
    scatter-add x9, other arithmetic, intersection_add(): summed.at[part_index:part_index + number]  3.45 us
  transfers between devices with their start and end apart: 9, of which 4 were waited for; matrix products, arithmetic and copies ran while one was open for 1% of the time, Pallas kernels for 0%

commit v1 on v0

v1 whole, which is shorter than its diff:
```python
import functools

import jax
import jax.numpy as jnp
from jax import lax
from jax.experimental import pallas as pl
from jax.experimental.pallas import tpu as pltpu
from jax.sharding import PartitionSpec as P

LANES = 128
REACH = 3
VMEM = pl.BlockSpec(memory_space=pltpu.VMEM)
SMEM = pl.BlockSpec(memory_space=pltpu.SMEM)


def ring(block, distance):
    size = lax.axis_size("ang")
    return lax.ppermute(block, "ang", [(i, (i + distance) % size) for i in range(size)])


def to_next_domains(block, distance):
    doms, angs = lax.axis_size("dom"), lax.axis_size("ang")
    route = [
        (d * angs + a, (d + 1) * angs + (a + distance) % angs) for d in range(doms - 1) for a in range(angs)
    ]
    return lax.ppermute(block, ("dom", "ang"), route)


def facing(block, even_step):
    doms = lax.axis_size("dom")
    route = [(i, i + (even_step if i % 2 == 0 else -even_step)) for i in range(doms)]
    return lax.ppermute(block, "dom", [(s, t) for s, t in route if 0 <= t < doms])


def placed_sums(jitter_ref, pieces, response_ref):
    domains = response_ref.shape[0]
    per_piece = domains // len(pieces)
    angles = pieces[0].shape[2]
    sums = [None] * (domains // 2 + 1)
    for d in range(domains):
        wave = pieces[d // per_piece][d % per_piece].reshape(2 * angles, -1)
        panel = jnp.concatenate([response_ref[d, 0], response_ref[d, 1]], axis=1)
        product = jnp.dot(wave, panel, preferred_element_type=jnp.float32)
        real = product[:angles, :LANES] - product[angles:, LANES:]
        imag = product[:angles, LANES:] + product[angles:, :LANES]
        field = jnp.concatenate([real, imag], axis=0).astype(jnp.bfloat16).astype(jnp.float32)
        start = (d % 2) * (LANES // 2) + jitter_ref[d]
        turned = pltpu.roll(field, start, 1)
        lane = lax.broadcasted_iota(jnp.int32, turned.shape, 1)
        here = jnp.where(lane >= start, turned, 0.0)
        after = turned - here
        for block, part in ((d // 2, here), (d // 2 + 1, after)):
            sums[block] = part if sums[block] is None else sums[block] + part
    return sums


def respond_kernel(groups, halves, *refs):
    jitter_ref, response_ref = refs[0], refs[1]
    inputs = refs[2 : 2 + groups * halves]
    outputs = refs[2 + groups * halves :]
    for g in range(groups):
        sums = placed_sums(jitter_ref, inputs[g * halves : (g + 1) * halves], response_ref)
        main_ref, halo_ref = outputs[2 * g], outputs[2 * g + 1]
        for b in range(main_ref.shape[0]):
            main_ref[b] = sums[b].astype(main_ref.dtype)
        first = len(sums) - halo_ref.shape[0]
        for b in range(halo_ref.shape[0]):
            halo_ref[b] = sums[first + b].astype(halo_ref.dtype)


def respond(jitter, response, groups, main_type):
    domains, _, depth, cols = response.shape
    halves = len(groups[0])
    angles = groups[0][0].shape[2]
    main = jax.ShapeDtypeStruct((domains // 2, 2 * angles, LANES), main_type)
    halo = jax.ShapeDtypeStruct((4, 2 * angles, LANES), jnp.bfloat16)
    flops = len(groups) * domains * 2 * (2 * angles) * depth * (2 * cols)
    return pl.pallas_call(
        functools.partial(respond_kernel, len(groups), halves),
        out_shape=[main, halo] * len(groups),
        in_specs=[SMEM, VMEM] + [VMEM] * (len(groups) * halves),
        out_specs=[VMEM] * (2 * len(groups)),
        compiler_params=pltpu.CompilerParams(vmem_limit_bytes=24 * 2**20),
        cost_estimate=pl.CostEstimate(flops=flops, bytes_accessed=response.size * 2, transcendentals=0),
        name="respond",
    )(jitter, response, *[piece for group in groups for piece in group])


def stitch_kernel(*refs):
    mains, halos, (out_ref, plane, edge) = refs[:4], refs[4:8], refs[8:]
    me = lax.axis_index("ang")
    blocks = out_ref.shape[0]
    plane[...] = jnp.zeros_like(plane)
    edge[...] = jnp.zeros_like(edge)
    for step in range(4):
        owner = lax.rem(me + step, 4)
        plane[pl.ds(owner, blocks)] += mains[step][...].astype(jnp.float32)
        edge[pl.ds(owner, 4)] += halos[step][...].astype(jnp.float32)
    plane[pl.ds(0, 4)] += edge[pl.ds(3, 4)]
    out_ref[...] = plane[pl.ds(0, blocks)].astype(out_ref.dtype)


def stitch(mains, halos):
    blocks, rows, lanes = mains[0].shape
    return pl.pallas_call(
        stitch_kernel,
        out_shape=jax.ShapeDtypeStruct((blocks, rows, lanes), jnp.bfloat16),
        in_specs=[VMEM] * 8,
        out_specs=VMEM,
        scratch_shapes=[
            pltpu.VMEM((blocks + 4, rows, lanes), jnp.float32),
            pltpu.VMEM((8, rows, lanes), jnp.float32),
        ],
        compiler_params=pltpu.CompilerParams(vmem_limit_bytes=8 * 2**20),
        name="stitch",
    )(*mains, *halos)


def couple_kernel(cols_ref, counts_ref, green_ref, *refs):
    parts, out_ref, window = refs[:7], refs[7], refs[8]
    blocks, rows, lanes = parts[0].shape
    angles = rows // 2
    entries = green_ref.shape[1]
    for s in range(7):
        window[pl.ds(s * blocks, blocks)] = parts[s][...]
    dead = 7 * blocks
    window[dead] = jnp.zeros((rows, lanes), window.dtype)
    me = lax.axis_index("dom")
    odd = lax.rem(me, 2) == 1
    for r in range(green_ref.shape[0]):
        picked = []
        for k in range(entries):
            col = cols_ref[r, k]
            distance = col // blocks - me
            slot = jnp.where(odd, REACH - distance, REACH + distance)
            index = jnp.where(k < counts_ref[r], slot * blocks + col % blocks, dead)
            picked.append(window[index])
        wave = jnp.concatenate(picked, axis=1)
        green = jnp.concatenate(
            [green_ref[r, :, 0].reshape(entries * lanes, lanes), green_ref[r, :, 1].reshape(entries * lanes, lanes)],
            axis=1,
        )
        product = jnp.dot(wave, green, preferred_element_type=jnp.float32)
        at = pl.ds(r * lanes, lanes)
        out_ref[0, :, at] = product[:angles, :lanes] - product[angles:, lanes:]
        out_ref[1, :, at] = product[:angles, lanes:] + product[angles:, :lanes]


def couple(block_cols, block_counts, green, parts):
    rows_here, entries = block_cols.shape
    blocks, rows, lanes = parts[0].shape
    flops = rows_here * 2 * rows * entries * lanes * 2 * lanes
    return pl.pallas_call(
        couple_kernel,
        out_shape=jax.ShapeDtypeStruct((2, rows // 2, rows_here * lanes), jnp.float32),
        in_specs=[SMEM, SMEM, VMEM] + [VMEM] * 7,
        out_specs=VMEM,
        scratch_shapes=[pltpu.VMEM((7 * blocks + 8, rows, lanes), jnp.bfloat16)],
        compiler_params=pltpu.CompilerParams(vmem_limit_bytes=24 * 2**20),
        cost_estimate=pl.CostEstimate(flops=flops, bytes_accessed=green.size * 2, transcendentals=0),
        name="couple",
    )(block_cols, block_counts, green, *parts)


def per_device(incident, response, jitter, block_cols, block_counts, green_blocks):
    half = incident.shape[0] // 2
    low, high = incident[:half], incident[half:]
    before_low, after_high = ring(low, 1), ring(high, -1)
    before_high, after_low = ring(high, 1), ring(low, -1)
    across_low, across_high = ring(before_low, 1), ring(after_high, -1)

    own_main, own_halo = respond(jitter, response, [(incident,)], jnp.float32)
    before_main, before_halo, after_main, after_halo = respond(
        jitter, response, [(before_low, before_high), (after_low, after_high)], jnp.bfloat16
    )
    across_main, across_halo = respond(jitter, response, [(across_low, across_high)], jnp.bfloat16)

    mains = [own_main, ring(before_main, -1), ring(across_main, 2), ring(after_main, 1)]
    halos = [
        to_next_domains(own_halo, 0),
        to_next_domains(before_halo, -1),
        to_next_domains(across_halo, 2),
        to_next_domains(after_halo, 1),
    ]
    own = stitch(mains, halos)

    near = facing(own, -1)
    middle = facing(own, 2)
    far = facing(own, -3)
    other = facing(own, 1)
    other_near = facing(near, 1)
    other_middle = facing(middle, 1)
    return couple(block_cols, block_counts, green_blocks, [far, middle, near, own, other, other_near, other_middle])


def solution(mesh):
    return jax.shard_map(
        per_device,
        mesh=mesh,
        in_specs=(
            P("dom", None, "ang", None),
            P("dom", None, None, "ang"),
            P("dom"),
            P("dom", None),
            P("dom"),
            P("dom", None, None, None, None),
        ),
        out_specs=P(None, "ang", "dom"),
        check_vma=False,
    )
```

time: 141 us -> 63.7 us (0.45)
  waiting for transfers between devices: 63.1 us -> 7.31 us
  matrix products: 17.2 us -> 0 us
  starting transfers between devices: 26.3 us -> 43 us
  between operations: 13.8 us -> 0.23 us
  local copies, waits for them, and re-layouts: 12.2 us -> 4.97 us
  Pallas kernels: 0 us -> 7 us
  other arithmetic: 5.97 us -> 0.01 us
    all_gather x1 -> x0, waiting for transfers between devices: 36.3 us -> none  [per_device(): shard_piece = lax.all_gather(incident, 'ang', axis=2, tiled=True)]
    reduce_scatter x1 -> x0, waiting for transfers between devices: 24.1 us -> none  [per_device(): lax.psum_scatter(partial_plane, 'ang', scatter_dimension=1, tiled=True)]
    dot_general x9 -> x0, matrix products: 17.2 us -> none  [the longest x1 2.55 us: per_device(): jnp.einsum('dan,dnc->dac', shard_piece[:, 1], response[:, 1], preferred_e...]
    ppermute x7 -> x19, starting transfers between devices: 26.2 us -> 43 us  [the longest x4 19.4 us: to_next_domains(): return lax.ppermute(block, ('dom', 'ang'), route)]
    pallas_call x0 -> x5, Pallas kernels: none -> 7 us  [the longest x3 4.56 us: respond(): pl.pallas_call(functools.partial(respond_kernel, len(groups), halves), ou...]
    convert_element_type x2 -> x0, local copies, waits for them, and re-layouts: 5.43 us -> none  [the longest x1 4.19 us: place(): return placed.astype(jnp.bfloat16)]
    ppermute x7 -> x19, waiting for transfers between devices: 2.6 us -> 7.31 us  [the longest x9 3.04 us: ring(): lax.ppermute(block, 'ang', [(i, (i + distance) % size) for i in range(siz...]
    scatter-add x10 -> x0, other arithmetic: 4.3 us -> none  [the longest x9 3.45 us: intersection_add(): summed.at[part_index:part_index + number]]
  transfers between devices with their start and end apart: 9 -> 19, of which waited for: 4 -> 3; matrix products, arithmetic and copies ran while one was open for 1% -> 0% of each run, Pallas kernels for 0% -> 7%
where the time goes in v1:
time: 63.7 us; the launch traced here: 62.5 us
  starting transfers between devices  43 us (68%)
  waiting for transfers between devices  7.31 us (11%)
  Pallas kernels  7 us (11%)
  local copies, waits for them, and re-layouts  4.97 us (8%)
    ppermute x4, starting transfers between devices, to_next_domains(): return lax.ppermute(block, ('dom', 'ang'), route)  19.4 us
    ppermute x6, starting transfers between devices, facing(): lax.ppermute(block, 'dom', [(s, t) for s, t in route if 0 <= t < doms])  13.7 us
    ppermute x9, starting transfers between devices, ring(): lax.ppermute(block, 'ang', [(i, (i + distance) % size) for i in range(siz...  9.89 us
    pallas_call x3, Pallas kernels, respond(): pl.pallas_call(functools.partial(respond_kernel, len(groups), halves), ou...  4.56 us
    unnamed x14, local copies, waits for them, and re-layouts  3.91 us
    ppermute x9, waiting for transfers between devices, ring(): lax.ppermute(block, 'ang', [(i, (i + distance) % size) for i in range(siz...  3.04 us
    ppermute x6, waiting for transfers between devices, facing(): lax.ppermute(block, 'dom', [(s, t) for s, t in route if 0 <= t < doms])  2.97 us
    pallas_call x1, Pallas kernels, couple(): pl.pallas_call(couple_kernel, out_shape=jax.ShapeDtypeStruct((2, rows //...  2.33 us
  transfers between devices with their start and end apart: 19, of which 3 were waited for; matrix products, arithmetic and copies ran while one was open for 0% of the time, Pallas kernels for 7%

profile of v1, /device:TPU:7, one launch (start us, length us, event | category | flops | bytes accessed | tf_op | source)
XLA Modules:
  0.0 62.5 jit_solution(14709295574881094491)
XLA Ops:
  0.0 1.1 %fusion = (bf16[8,2,16,512]{3,2,1,0:T(8,128)(2,1)S(1)}, bf16[8,2,16,512]{3,2,1,0:T(8,128)(2,1)S(1)}) fusion(bf16[16,2,16,512]{3,2,1,0:T(8,128)(2,1)} %refs_2_.1), kind=kLoop, calls=%fused_computation | loop fusion | bytes 1048576 | tf_op jit(solution)/shard_map/slice | solution.py:167
  1.1 1.4 %collective-permute-start = (bf16[8,2,16,512]{3,2,1,0:T(8,128)(2,1)S(1)}, bf16[8,2,16,512]{3,2,1,0:T(8,128)(2,1)S(1)}, u32[]{:S(2)}, u32[]{:S(2)}) collective-permute-start(bf16[8,2,16,512]{3,2,1,0:T(8,128)(2,1)S(1)} %get-tuple-element.22), channel_id=1, source_target_pairs={{0,1},{1,2},{2,3},{3,0},{4,5},{5,6},{6,7},{7,4},{8,9},{9,10},{10,1... | collective-permute-start | bytes 786440 | tf_op jit(solution)/shard_map/ppermute | solution.py:18
  2.4 1.5 %collective-permute-start.3 = (bf16[8,2,16,512]{3,2,1,0:T(8,128)(2,1)S(1)}, bf16[8,2,16,512]{3,2,1,0:T(8,128)(2,1)S(1)}, u32[]{:S(2)}, u32[]{:S(2)}) collective-permute-start(bf16[8,2,16,512]{3,2,1,0:T(8,128)(2,1)S(1)} %get-tuple-element.21), channel_id=1, source_target_pairs={{0,3},{1,0},{2,1},{3,2},{4,7},{5,4},{6,5},{7,6},{8,11},{9,8},{10,9... | collective-permute-start | bytes 786440 | tf_op jit(solution)/shard_map/ppermute | solution.py:18
  4.0 0.0 collective-permute-start.1
  4.0 2.7 %collective-permute-start.2 = (bf16[8,2,16,512]{3,2,1,0:T(8,128)(2,1)S(1)}, bf16[8,2,16,512]{3,2,1,0:T(8,128)(2,1)S(1)}, u32[]{:S(2)}, u32[]{:S(2)}) collective-permute-start(bf16[8,2,16,512]{3,2,1,0:T(8,128)(2,1)S(1)} %get-tuple-element.22), channel_id=1, source_target_pairs={{0,3},{1,0},{2,1},{3,2},{4,7},{5,4},{6,5},{7,6},{8,11},{9,8},{10,9... | collective-permute-start | bytes 786440 | tf_op jit(solution)/shard_map/ppermute | solution.py:18
  6.7 3.0 %collective-permute-done.refs_2_ = bf16[8,2,16,512]{3,2,1,0:T(8,128)(2,1)S(1)} collective-permute-done((bf16[8,2,16,512]{3,2,1,0:T(8,128)(2,1)S(1)}, bf16[8,2,16,512]{3,2,1,0:T(8,128)(2,1)S(1)}, u32[]{:S(2)}, u32[]{:S(2)}) %collective-permute-start) | collective-permute-done | bytes 262176 | tf_op jit(solution)/shard_map/ppermute | solution.py:18
  9.7 0.0 collective-permute-start.5
  9.7 0.0 collective-permute-done.3.refs_5_
  9.7 2.7 %collective-permute-start.6 = (bf16[8,2,16,512]{3,2,1,0:T(8,128)(2,1)S(1)}, bf16[8,2,16,512]{3,2,1,0:T(8,128)(2,1)S(1)}, u32[]{:S(2)}, u32[]{:S(2)}) collective-permute-start(bf16[8,2,16,512]{3,2,1,0:T(8,128)(2,1)S(1)} %collective-permute-done.3.refs_5_), channel_id=1, source_target_pairs={{0,3},{1,0},{2,1},{3,2},{4,7},{5,4},{6,5},{7,6},{8,11},{9,8},{10,9... | collective-permute-start | bytes 786440 | tf_op jit(solution)/shard_map/ppermute | solution.py:18
  12.4 2.2 %copy-done = bf16[16,2,512,128]{3,2,1,0:T(8,128)(2,1)S(1)} copy-done((bf16[16,2,512,128]{3,2,1,0:T(8,128)(2,1)S(1)}, bf16[16,2,512,128]{3,2,1,0:T(8,128)(2,1)}, u32[]{:S(2)}) %copy-start) | copy-done | bytes 4194328
  14.5 1.0 %copy-done.1 = bf16[16,2,16,512]{3,2,1,0:T(8,128)(2,1)S(1)} copy-done((bf16[16,2,16,512]{3,2,1,0:T(8,128)(2,1)S(1)}, bf16[16,2,16,512]{3,2,1,0:T(8,128)(2,1)}, u32[]{:S(2)}) %copy-start.1) | copy-done | bytes 524312
  15.6 0.7 %copy-done.2 = s32[16]{0:T(128)S(1)} copy-done((s32[16]{0:T(128)S(1)}, s32[16]{0:T(128)}, u32[]{:S(2)}) %copy-start.2) | copy-done | bytes 88
  16.2 1.3 %respond.3 = (f32[8,32,128]{2,1,0:T(8,128)S(1)}, bf16[4,32,128]{2,1,0:T(8,128)(2,1)S(1)}) custom-call(s32[16]{0:T(128)S(1)} %copy-done.2, bf16[16,2,512,128]{3,2,1,0:T(8,128)(2,1)S(1)} %copy-done, bf16[16,2,16,512]{3,2,1,0:T(8,128)(2,1)S(1)} %copy-done.1), custom_call_target="tpu_custom_call" | custom-call | flops 134217728 | bytes 4194304 | tf_op jit(solution)/shard_map/respond/pallas_call | solution.py:78
  17.6 0.0 copy-start.3
  17.6 0.0 copy-start.4
  17.6 0.0 slice-start.1
  17.6 6.7 %collective-permute-start.9 = (bf16[4,32,128]{2,1,0:T(8,128)(2,1)S(1)}, bf16[4,32,128]{2,1,0:T(8,128)(2,1)S(1)}, u32[]{:S(2)}, u32[]{:S(2)}) collective-permute-start(bf16[4,32,128]{2,1,0:T(8,128)(2,1)S(1)} %get-tuple-element.17), channel_id=1, source_target_pairs={{0,4},{1,5},{2,6},{3,7},{4,8},{5,9},{6,10},{7,11},{8,12},{9,13},{1... | collective-permute-start | bytes 98312 | tf_op jit(solution)/shard_map/ppermute | solution.py:26
  24.3 0.0 collective-permute-done.1.refs_3_
  24.3 0.0 collective-permute-done.2.refs_4_
  24.3 1.9 %respond.4 = (bf16[8,32,128]{2,1,0:T(8,128)(2,1)S(1)}, bf16[4,32,128]{2,1,0:T(8,128)(2,1)S(1)}, bf16[8,32,128]{2,1,0:T(8,128)(2,1)S(1)}, bf16[4,32,128]{2,1,0:T(8,128)(2,1)S(1)}) custom-call(s32[16]{0:T(128)S(1)} %copy-done.2, bf16[16,2,512,128]{3,2,1,0:T(8,128)(2,1)S(1)} %copy-done, bf16[8,2,16,512]{3,2,1,0:T(8,128)(2,1)S(1)} %collective-permute-done.refs_2_, ...), custom_call_target="tpu_custom_call" | custom-call | flops 268435456 | bytes 4194304 | tf_op jit(solution)/shard_map/respond/pallas_call | solution.py:78
  26.2 0.4 collective-permute-start.4
  26.6 1.1 %collective-permute-start.8 = (bf16[8,32,128]{2,1,0:T(8,128)(2,1)S(1)}, bf16[8,32,128]{2,1,0:T(8,128)(2,1)S(1)}, u32[]{:S(2)}, u32[]{:S(2)}) collective-permute-start(bf16[8,32,128]{2,1,0:T(8,128)(2,1)S(1)} %get-tuple-element.16), channel_id=1, source_target_pairs={{0,1},{1,2},{2,3},{3,0},{4,5},{5,6},{6,7},{7,4},{8,9},{9,10},{10,1... | collective-permute-start | bytes 196616 | tf_op jit(solution)/shard_map/ppermute | solution.py:18
  27.8 0.0 collective-permute-done.5.refs_2_
  27.8 3.7 %collective-permute-start.10 = (bf16[4,32,128]{2,1,0:T(8,128)(2,1)S(1)}, bf16[4,32,128]{2,1,0:T(8,128)(2,1)S(1)}, u32[]{:S(2)}, u32[]{:S(2)}) collective-permute-start(bf16[4,32,128]{2,1,0:T(8,128)(2,1)S(1)} %get-tuple-element.18), channel_id=1, source_target_pairs={{0,7},{1,4},{2,5},{3,6},{4,11},{5,8},{6,9},{7,10},{8,15},{9,12},{1... | collective-permute-start | bytes 98312 | tf_op jit(solution)/shard_map/ppermute | solution.py:26
  31.5 0.0 collective-permute-done.6.refs_3_
  31.5 1.3 %respond.5 = (bf16[8,32,128]{2,1,0:T(8,128)(2,1)S(1)}, bf16[4,32,128]{2,1,0:T(8,128)(2,1)S(1)}) custom-call(s32[16]{0:T(128)S(1)} %copy-done.2, bf16[16,2,512,128]{3,2,1,0:T(8,128)(2,1)S(1)} %copy-done, bf16[8,2,16,512]{3,2,1,0:T(8,128)(2,1)S(1)} %collective-permute-done.5.refs_2_, bf16[8,2,16,512]{3,2,1,0:T(8,128)(2,1)S(1)} %collective-permute-done.6.refs_3_), custom_call_target="tpu_custom_call" | custom-call | flops 134217728 | bytes 4194304 | tf_op jit(solution)/shard_map/respond/pallas_call | solution.py:78
  32.9 0.1 collective-permute-start.7
  33.0 0.0 collective-permute-done.9.refs_4_
  33.0 3.3 %collective-permute-start.12 = (bf16[4,32,128]{2,1,0:T(8,128)(2,1)S(1)}, bf16[4,32,128]{2,1,0:T(8,128)(2,1)S(1)}, u32[]{:S(2)}, u32[]{:S(2)}) collective-permute-start(bf16[4,32,128]{2,1,0:T(8,128)(2,1)S(1)} %get-tuple-element.20), channel_id=1, source_target_pairs={{0,5},{1,6},{2,7},{3,4},{4,9},{5,10},{6,11},{7,8},{8,13},{9,14},{1... | collective-permute-start | bytes 98312 | tf_op jit(solution)/shard_map/ppermute | solution.py:26
  36.3 0.0 collective-permute-done.10.refs_5_
  36.3 5.6 %collective-permute-start.11 = (bf16[4,32,128]{2,1,0:T(8,128)(2,1)S(1)}, bf16[4,32,128]{2,1,0:T(8,128)(2,1)S(1)}, u32[]{:S(2)}, u32[]{:S(2)}) collective-permute-start(bf16[4,32,128]{2,1,0:T(8,128)(2,1)S(1)} %get-tuple-element.19), channel_id=1, source_target_pairs={{0,6},{1,7},{2,4},{3,5},{4,10},{5,11},{6,8},{7,9},{8,14},{9,15},{1... | collective-permute-start | bytes 98312 | tf_op jit(solution)/shard_map/ppermute | solution.py:26
  42.0 0.0 collective-permute-done.12.refs_7_
  42.0 0.0 collective-permute-done.4.refs_1_
  42.0 0.0 collective-permute-done.8.refs_3_
  42.0 1.3 %collective-permute-done.11.refs_6_ = bf16[4,32,128]{2,1,0:T(8,128)(2,1)S(1)} collective-permute-done((bf16[4,32,128]{2,1,0:T(8,128)(2,1)S(1)}, bf16[4,32,128]{2,1,0:T(8,128)(2,1)S(1)}, u32[]{:S(2)}, u32[]{:S(2)}) %collective-permute-start.11) | collective-permute-done | bytes 32800 | tf_op jit(solution)/shard_map/ppermute | solution.py:26
  43.3 0.0 collective-permute-done.7.refs_2_
  43.3 0.1 stitch.1.refs_3_
  43.4 4.0 %collective-permute-start.15 = (bf16[8,32,128]{2,1,0:T(8,128)(2,1)S(1)}, bf16[8,32,128]{2,1,0:T(8,128)(2,1)S(1)}, u32[]{:S(2)}, u32[]{:S(2)}) collective-permute-start(bf16[8,32,128]{2,1,0:T(8,128)(2,1)S(1)} %stitch.1.refs_3_), channel_id=1, source_target_pairs={{4,8},{8,4},{12,16},{16,12},{20,24},{24,20},{28,32},{32,28},{36,40... | collective-permute-start | bytes 196616 | tf_op jit(solution)/shard_map/ppermute | solution.py:32
  47.4 5.5 %collective-permute-start.14 = (bf16[8,32,128]{2,1,0:T(8,128)(2,1)S(1)}, bf16[8,32,128]{2,1,0:T(8,128)(2,1)S(1)}, u32[]{:S(2)}, u32[]{:S(2)}) collective-permute-start(bf16[8,32,128]{2,1,0:T(8,128)(2,1)S(1)} %stitch.1.refs_3_), channel_id=1, source_target_pairs={{0,8},{8,16},{12,4},{16,24},{20,12},{24,32},{28,20},{32,40},{36,28... | collective-permute-start | bytes 196616 | tf_op jit(solution)/shard_map/ppermute | solution.py:32
  53.0 2.4 %collective-permute-start.13 = (bf16[8,32,128]{2,1,0:T(8,128)(2,1)S(1)}, bf16[8,32,128]{2,1,0:T(8,128)(2,1)S(1)}, u32[]{:S(2)}, u32[]{:S(2)}) collective-permute-start(bf16[8,32,128]{2,1,0:T(8,128)(2,1)S(1)} %stitch.1.refs_3_), channel_id=1, source_target_pairs={{4,16},{12,24},{16,4},{20,32},{24,12},{28,40},{32,20},{36,48},{40,... | collective-permute-start | bytes 196616 | tf_op jit(solution)/shard_map/ppermute | solution.py:32
  55.4 1.2 %collective-permute-start.16 = (bf16[8,32,128]{2,1,0:T(8,128)(2,1)S(1)}, bf16[8,32,128]{2,1,0:T(8,128)(2,1)S(1)}, u32[]{:S(2)}, u32[]{:S(2)}) collective-permute-start(bf16[8,32,128]{2,1,0:T(8,128)(2,1)S(1)} %stitch.1.refs_3_), channel_id=1, source_target_pairs={{0,4},{4,0},{8,12},{12,8},{16,20},{20,16},{24,28},{28,24},{32,36},... | collective-permute-start | bytes 196616 | tf_op jit(solution)/shard_map/ppermute | solution.py:32
  56.6 0.1 collective-permute-start.17
  56.7 0.4 collective-permute-start.18
  57.1 3.0 %collective-permute-done.13.refs_0_ = bf16[8,32,128]{2,1,0:T(8,128)(2,1)S(1)} collective-permute-done((bf16[8,32,128]{2,1,0:T(8,128)(2,1)S(1)}, bf16[8,32,128]{2,1,0:T(8,128)(2,1)S(1)}, u32[]{:S(2)}, u32[]{:S(2)}) %collective-permute-start.13) | collective-permute-done | bytes 65568 | tf_op jit(solution)/shard_map/ppermute | solution.py:32
  60.1 0.0 collective-permute-done.16.refs_4_
  60.1 0.0 collective-permute-done.17.refs_5_
  60.1 0.0 collective-permute-done.18.refs_6_
  60.1 2.3 %couple.1 = f32[2,16,1024]{2,1,0:T(8,128)} custom-call(s32[8,12]{1,0:T(8,128)S(1)} %copy-done.3, s32[8]{0:T(128)S(1)} %copy-done.4, bf16[8,12,2,128,128]{4,3,2,1,0:T(8,128)(2,1)S(1)} %bitcast.1, bf16[8,32,128]{2,1,0:T(8,128)(2,1)S(1)} %collective-permute-done.13.refs_0_, bf16[8,32,128]{2,1,0:T(8,128)(2,1)S(1)} %collective-permute-done.14.refs_1_, ...), custom_call_target="tpu_custom_call" | custom-call | flops 201326592 | bytes 6291456 | tf_op jit(solution)/shard_map/couple/pallas_call | solution.py:153
  (11 shorter events, 0.0 us)
Async XLA Ops:
  1.1 8.6 %collective-permute-start = (bf16[8,2,16,512]{3,2,1,0:T(8,128)(2,1)S(1)}, bf16[8,2,16,512]{3,2,1,0:T(8,128)(2,1)S(1)}, u32[]{:S(2)}, u32[]{:S(2)}) collective-permute-start(bf16[8,2,16,512]{3,2,1,0:T(8,128)(2,1)S(1)} %get-tuple-element.22), channel_id=1, source_target_pairs={{0,1},{1,2},{2,3},{3,0},{4,5},{5,6},{6,7},{7,4},{8,9},{9,10},{10,1... | collective-permute-start | bytes 786440 | tf_op jit(solution)/shard_map/ppermute | solution.py:18
  2.4 7.2 %collective-permute-start.3 = (bf16[8,2,16,512]{3,2,1,0:T(8,128)(2,1)S(1)}, bf16[8,2,16,512]{3,2,1,0:T(8,128)(2,1)S(1)}, u32[]{:S(2)}, u32[]{:S(2)}) collective-permute-start(bf16[8,2,16,512]{3,2,1,0:T(8,128)(2,1)S(1)} %get-tuple-element.21), channel_id=1, source_target_pairs={{0,3},{1,0},{2,1},{3,2},{4,7},{5,4},{6,5},{7,6},{8,11},{9,8},{10,9... | collective-permute-start | bytes 786440 | tf_op jit(solution)/shard_map/ppermute | solution.py:18
  4.0 20.3 %collective-permute-start.1 = (bf16[8,2,16,512]{3,2,1,0:T(8,128)(2,1)S(1)}, bf16[8,2,16,512]{3,2,1,0:T(8,128)(2,1)S(1)}, u32[]{:S(2)}, u32[]{:S(2)}) collective-permute-start(bf16[8,2,16,512]{3,2,1,0:T(8,128)(2,1)S(1)} %get-tuple-element.21), channel_id=1, source_target_pairs={{0,1},{1,2},{2,3},{3,0},{4,5},{5,6},{6,7},{7,4},{8,9},{9,10},{10,1... | collective-permute-start | bytes 786440 | tf_op jit(solution)/shard_map/ppermute | solution.py:18
  4.0 20.3 %collective-permute-start.2 = (bf16[8,2,16,512]{3,2,1,0:T(8,128)(2,1)S(1)}, bf16[8,2,16,512]{3,2,1,0:T(8,128)(2,1)S(1)}, u32[]{:S(2)}, u32[]{:S(2)}) collective-permute-start(bf16[8,2,16,512]{3,2,1,0:T(8,128)(2,1)S(1)} %get-tuple-element.22), channel_id=1, source_target_pairs={{0,3},{1,0},{2,1},{3,2},{4,7},{5,4},{6,5},{7,6},{8,11},{9,8},{10,9... | collective-permute-start | bytes 786440 | tf_op jit(solution)/shard_map/ppermute | solution.py:18
  9.7 18.1 %collective-permute-start.5 = (bf16[8,2,16,512]{3,2,1,0:T(8,128)(2,1)S(1)}, bf16[8,2,16,512]{3,2,1,0:T(8,128)(2,1)S(1)}, u32[]{:S(2)}, u32[]{:S(2)}) collective-permute-start(bf16[8,2,16,512]{3,2,1,0:T(8,128)(2,1)S(1)} %collective-permute-done.refs_2_), channel_id=1, source_target_pairs={{0,1},{1,2},{2,3},{3,0},{4,5},{5,6},{6,7},{7,4},{8,9},{9,10},{10,1... | collective-permute-start | bytes 786440 | tf_op jit(solution)/shard_map/ppermute | solution.py:18
  9.7 21.8 %collective-permute-start.6 = (bf16[8,2,16,512]{3,2,1,0:T(8,128)(2,1)S(1)}, bf16[8,2,16,512]{3,2,1,0:T(8,128)(2,1)S(1)}, u32[]{:S(2)}, u32[]{:S(2)}) collective-permute-start(bf16[8,2,16,512]{3,2,1,0:T(8,128)(2,1)S(1)} %collective-permute-done.3.refs_5_), channel_id=1, source_target_pairs={{0,3},{1,0},{2,1},{3,2},{4,7},{5,4},{6,5},{7,6},{8,11},{9,8},{10,9... | collective-permute-start | bytes 786440 | tf_op jit(solution)/shard_map/ppermute | solution.py:18
  12.4 2.2 %copy-start = (bf16[16,2,512,128]{3,2,1,0:T(8,128)(2,1)S(1)}, bf16[16,2,512,128]{3,2,1,0:T(8,128)(2,1)}, u32[]{:S(2)}) copy-start(bf16[16,2,512,128]{3,2,1,0:T(8,128)(2,1)} %refs_1_.5) | copy-start | bytes 12582916
  14.5 1.0 %copy-start.1 = (bf16[16,2,16,512]{3,2,1,0:T(8,128)(2,1)S(1)}, bf16[16,2,16,512]{3,2,1,0:T(8,128)(2,1)}, u32[]{:S(2)}) copy-start(bf16[16,2,16,512]{3,2,1,0:T(8,128)(2,1)} %refs_2_.1) | copy-start | bytes 1572868
  15.6 0.7 %copy-start.2 = (s32[16]{0:T(128)S(1)}, s32[16]{0:T(128)}, u32[]{:S(2)}) copy-start(s32[16]{0:T(128)} %refs_0_.5) | copy-start | bytes 196
  16.2 43.9 %slice-start = ((s8[6291456]{0:T(1024)(128)(4,1)}), s8[4194304]{0:T(1024)(128)(4,1)S(1)}, s32[]{:S(2)}) async-start(s8[6291456]{0:T(1024)(128)(4,1)} %bitcast), calls=%async_computation | async-start | bytes 8388608
  17.6 42.5 %copy-start.3 = (s32[8,12]{1,0:T(8,128)S(1)}, s32[8,12]{1,0:T(8,128)}, u32[]{:S(2)}) copy-start(s32[8,12]{1,0:T(8,128)} %cols_ref.1) | copy-start | bytes 1156
  17.6 42.5 %copy-start.4 = (s32[8]{0:T(128)S(1)}, s32[8]{0:T(128)}, u32[]{:S(2)}) copy-start(s32[8]{0:T(128)} %counts_ref.1) | copy-start | bytes 100
  17.6 42.5 %slice-start.1 = ((s8[6291456]{0:T(1024)(128)(4,1)}), s8[2097152]{0:T(1024)(128)(4,1)S(1)}, s32[]{:S(2)}) async-start(s8[6291456]{0:T(1024)(128)(4,1)} %bitcast), calls=%async_computation.1 | async-start | bytes 4194304
  17.6 15.4 %collective-permute-start.9 = (bf16[4,32,128]{2,1,0:T(8,128)(2,1)S(1)}, bf16[4,32,128]{2,1,0:T(8,128)(2,1)S(1)}, u32[]{:S(2)}, u32[]{:S(2)}) collective-permute-start(bf16[4,32,128]{2,1,0:T(8,128)(2,1)S(1)} %get-tuple-element.17), channel_id=1, source_target_pairs={{0,4},{1,5},{2,6},{3,7},{4,8},{5,9},{6,10},{7,11},{8,12},{9,13},{1... | collective-permute-start | bytes 98312 | tf_op jit(solution)/shard_map/ppermute | solution.py:26
  26.2 15.7 %collective-permute-start.4 = (bf16[8,32,128]{2,1,0:T(8,128)(2,1)S(1)}, bf16[8,32,128]{2,1,0:T(8,128)(2,1)S(1)}, u32[]{:S(2)}, u32[]{:S(2)}) collective-permute-start(bf16[8,32,128]{2,1,0:T(8,128)(2,1)S(1)} %get-tuple-element.14), channel_id=1, source_target_pairs={{0,3},{1,0},{2,1},{3,2},{4,7},{5,4},{6,5},{7,6},{8,11},{9,8},{10,9... | collective-permute-start | bytes 196616 | tf_op jit(solution)/shard_map/ppermute | solution.py:18
  26.6 15.3 %collective-permute-start.8 = (bf16[8,32,128]{2,1,0:T(8,128)(2,1)S(1)}, bf16[8,32,128]{2,1,0:T(8,128)(2,1)S(1)}, u32[]{:S(2)}, u32[]{:S(2)}) collective-permute-start(bf16[8,32,128]{2,1,0:T(8,128)(2,1)S(1)} %get-tuple-element.16), channel_id=1, source_target_pairs={{0,1},{1,2},{2,3},{3,0},{4,5},{5,6},{6,7},{7,4},{8,9},{9,10},{10,1... | collective-permute-start | bytes 196616 | tf_op jit(solution)/shard_map/ppermute | solution.py:18
  27.8 8.5 %collective-permute-start.10 = (bf16[4,32,128]{2,1,0:T(8,128)(2,1)S(1)}, bf16[4,32,128]{2,1,0:T(8,128)(2,1)S(1)}, u32[]{:S(2)}, u32[]{:S(2)}) collective-permute-start(bf16[4,32,128]{2,1,0:T(8,128)(2,1)S(1)} %get-tuple-element.18), channel_id=1, source_target_pairs={{0,7},{1,4},{2,5},{3,6},{4,11},{5,8},{6,9},{7,10},{8,15},{9,12},{1... | collective-permute-start | bytes 98312 | tf_op jit(solution)/shard_map/ppermute | solution.py:26
  32.9 10.4 %collective-permute-start.7 = (bf16[8,32,128]{2,1,0:T(8,128)(2,1)S(1)}, bf16[8,32,128]{2,1,0:T(8,128)(2,1)S(1)}, u32[]{:S(2)}, u32[]{:S(2)}) collective-permute-start(bf16[8,32,128]{2,1,0:T(8,128)(2,1)S(1)} %get-tuple-element.15), channel_id=1, source_target_pairs={{0,2},{1,3},{2,0},{3,1},{4,6},{5,7},{6,4},{7,5},{8,10},{9,11},{10,... | collective-permute-start | bytes 196616 | tf_op jit(solution)/shard_map/ppermute | solution.py:18
  33.0 9.0 %collective-permute-start.12 = (bf16[4,32,128]{2,1,0:T(8,128)(2,1)S(1)}, bf16[4,32,128]{2,1,0:T(8,128)(2,1)S(1)}, u32[]{:S(2)}, u32[]{:S(2)}) collective-permute-start(bf16[4,32,128]{2,1,0:T(8,128)(2,1)S(1)} %get-tuple-element.20), channel_id=1, source_target_pairs={{0,5},{1,6},{2,7},{3,4},{4,9},{5,10},{6,11},{7,8},{8,13},{9,14},{1... | collective-permute-start | bytes 98312 | tf_op jit(solution)/shard_map/ppermute | solution.py:26
  36.3 6.9 %collective-permute-start.11 = (bf16[4,32,128]{2,1,0:T(8,128)(2,1)S(1)}, bf16[4,32,128]{2,1,0:T(8,128)(2,1)S(1)}, u32[]{:S(2)}, u32[]{:S(2)}) collective-permute-start(bf16[4,32,128]{2,1,0:T(8,128)(2,1)S(1)} %get-tuple-element.19), channel_id=1, source_target_pairs={{0,6},{1,7},{2,4},{3,5},{4,10},{5,11},{6,8},{7,9},{8,14},{9,15},{1... | collective-permute-start | bytes 98312 | tf_op jit(solution)/shard_map/ppermute | solution.py:26
  43.4 13.2 %collective-permute-start.15 = (bf16[8,32,128]{2,1,0:T(8,128)(2,1)S(1)}, bf16[8,32,128]{2,1,0:T(8,128)(2,1)S(1)}, u32[]{:S(2)}, u32[]{:S(2)}) collective-permute-start(bf16[8,32,128]{2,1,0:T(8,128)(2,1)S(1)} %stitch.1.refs_3_), channel_id=1, source_target_pairs={{4,8},{8,4},{12,16},{16,12},{20,24},{24,20},{28,32},{32,28},{36,40... | collective-permute-start | bytes 196616 | tf_op jit(solution)/shard_map/ppermute | solution.py:32
  47.4 9.3 %collective-permute-start.14 = (bf16[8,32,128]{2,1,0:T(8,128)(2,1)S(1)}, bf16[8,32,128]{2,1,0:T(8,128)(2,1)S(1)}, u32[]{:S(2)}, u32[]{:S(2)}) collective-permute-start(bf16[8,32,128]{2,1,0:T(8,128)(2,1)S(1)} %stitch.1.refs_3_), channel_id=1, source_target_pairs={{0,8},{8,16},{12,4},{16,24},{20,12},{24,32},{28,20},{32,40},{36,28... | collective-permute-start | bytes 196616 | tf_op jit(solution)/shard_map/ppermute | solution.py:32
  53.0 7.1 %collective-permute-start.13 = (bf16[8,32,128]{2,1,0:T(8,128)(2,1)S(1)}, bf16[8,32,128]{2,1,0:T(8,128)(2,1)S(1)}, u32[]{:S(2)}, u32[]{:S(2)}) collective-permute-start(bf16[8,32,128]{2,1,0:T(8,128)(2,1)S(1)} %stitch.1.refs_3_), channel_id=1, source_target_pairs={{4,16},{12,24},{16,4},{20,32},{24,12},{28,40},{32,20},{36,48},{40,... | collective-permute-start | bytes 196616 | tf_op jit(solution)/shard_map/ppermute | solution.py:32
  55.4 4.7 %collective-permute-start.16 = (bf16[8,32,128]{2,1,0:T(8,128)(2,1)S(1)}, bf16[8,32,128]{2,1,0:T(8,128)(2,1)S(1)}, u32[]{:S(2)}, u32[]{:S(2)}) collective-permute-start(bf16[8,32,128]{2,1,0:T(8,128)(2,1)S(1)} %stitch.1.refs_3_), channel_id=1, source_target_pairs={{0,4},{4,0},{8,12},{12,8},{16,20},{20,16},{24,28},{28,24},{32,36},... | collective-permute-start | bytes 196616 | tf_op jit(solution)/shard_map/ppermute | solution.py:32
  56.6 3.5 %collective-permute-start.17 = (bf16[8,32,128]{2,1,0:T(8,128)(2,1)S(1)}, bf16[8,32,128]{2,1,0:T(8,128)(2,1)S(1)}, u32[]{:S(2)}, u32[]{:S(2)}) collective-permute-start(bf16[8,32,128]{2,1,0:T(8,128)(2,1)S(1)} %collective-permute-done.15.refs_2_), channel_id=1, source_target_pairs={{0,4},{4,0},{8,12},{12,8},{16,20},{20,16},{24,28},{28,24},{32,36},... | collective-permute-start | bytes 196616 | tf_op jit(solution)/shard_map/ppermute | solution.py:32
  56.7 3.4 %collective-permute-start.18 = (bf16[8,32,128]{2,1,0:T(8,128)(2,1)S(1)}, bf16[8,32,128]{2,1,0:T(8,128)(2,1)S(1)}, u32[]{:S(2)}, u32[]{:S(2)}) collective-permute-start(bf16[8,32,128]{2,1,0:T(8,128)(2,1)S(1)} %collective-permute-done.14.refs_1_), channel_id=1, source_target_pairs={{0,4},{4,0},{8,12},{12,8},{16,20},{20,16},{24,28},{28,24},{32,36},... | collective-permute-start | bytes 196616 | tf_op jit(solution)/shard_map/ppermute | solution.py:32

commit v2 on v1

v2 whole, which is shorter than its diff:
```python
import functools

import jax
import jax.numpy as jnp
from jax import lax
from jax.experimental import pallas as pl
from jax.experimental.pallas import tpu as pltpu
from jax.sharding import PartitionSpec as P

LANES = 128
REACH = 3
HALO = 4
VMEM = pl.BlockSpec(memory_space=pltpu.VMEM)
SMEM = pl.BlockSpec(memory_space=pltpu.SMEM)


def ring(block, distance):
    size = lax.axis_size("ang")
    return lax.ppermute(block, "ang", [(i, (i + distance) % size) for i in range(size)])


def facing(block, even_step):
    doms = lax.axis_size("dom")
    route = [(i, i + (even_step if i % 2 == 0 else -even_step)) for i in range(doms)]
    return lax.ppermute(block, "dom", [(s, t) for s, t in route if 0 <= t < doms])


def placed_sums(jitter_ref, pieces, response_ref):
    domains = response_ref.shape[0]
    per_piece = domains // len(pieces)
    angles = pieces[0].shape[2]
    sums = [None] * (domains // 2 + 1)
    for d in range(domains):
        wave = pieces[d // per_piece][d % per_piece].reshape(2 * angles, -1)
        panel = jnp.concatenate([response_ref[d, 0], response_ref[d, 1]], axis=1)
        product = jnp.dot(wave, panel, preferred_element_type=jnp.float32)
        real = product[:angles, :LANES] - product[angles:, LANES:]
        imag = product[:angles, LANES:] + product[angles:, :LANES]
        field = jnp.concatenate([real, imag], axis=0).astype(jnp.bfloat16).astype(jnp.float32)
        start = (d % 2) * (LANES // 2) + jitter_ref[d]
        turned = pltpu.roll(field, start, 1)
        lane = lax.broadcasted_iota(jnp.int32, turned.shape, 1)
        here = jnp.where(lane >= start, turned, 0.0)
        after = turned - here
        for block, part in ((d // 2, here), (d // 2 + 1, after)):
            sums[block] = part if sums[block] is None else sums[block] + part
    return sums


def own_kernel(chunk, jitter_ref, incident_hbm, response_hbm, sums_ref, response_ref, incident_ref, wave_sem, panel_sems):
    domains = response_ref.shape[0]
    wave_copy = pltpu.make_async_copy(incident_hbm, incident_ref, wave_sem)
    wave_copy.start()
    copies = []
    for c in range(domains // chunk):
        at = pl.ds(c * chunk, chunk)
        copies.append(pltpu.make_async_copy(response_hbm.at[at], response_ref.at[at], panel_sems.at[c]))
        copies[-1].start()
    wave_copy.wait()
    for copy in copies:
        copy.wait()
    sums = placed_sums(jitter_ref, [incident_ref], response_ref)
    for b, block in enumerate(sums):
        sums_ref[b] = block


def respond_own(jitter, incident, response):
    domains, _, depth, cols = response.shape
    angles = incident.shape[2]
    chunk = domains // 4
    hbm = pl.BlockSpec(memory_space=pltpu.HBM)
    return pl.pallas_call(
        functools.partial(own_kernel, chunk),
        out_shape=[
            jax.ShapeDtypeStruct((domains // 2 + 1, 2 * angles, LANES), jnp.float32),
            jax.ShapeDtypeStruct(response.shape, response.dtype),
        ],
        in_specs=[SMEM, hbm, hbm],
        out_specs=[VMEM, VMEM],
        scratch_shapes=[
            pltpu.VMEM(incident.shape, incident.dtype),
            pltpu.SemaphoreType.DMA,
            pltpu.SemaphoreType.DMA((domains // chunk,)),
        ],
        compiler_params=pltpu.CompilerParams(vmem_limit_bytes=16 * 2**20),
        cost_estimate=pl.CostEstimate(
            flops=domains * 8 * angles * depth * cols, bytes_accessed=4 * response.size, transcendentals=0
        ),
        name="respond_own",
    )(jitter, incident, response)


def respond_kernel(groups, halves, *refs):
    jitter_ref, response_ref = refs[0], refs[1]
    inputs = refs[2 : 2 + groups * halves]
    outputs = refs[2 + groups * halves :]
    for g in range(groups):
        sums = placed_sums(jitter_ref, inputs[g * halves : (g + 1) * halves], response_ref)
        for b, block in enumerate(sums):
            outputs[g][b] = block.astype(outputs[g].dtype)


def respond(jitter, response, groups):
    domains, _, depth, cols = response.shape
    halves = len(groups[0])
    angles = groups[0][0].shape[2]
    sums = jax.ShapeDtypeStruct((domains // 2 + 1, 2 * angles, LANES), jnp.bfloat16)
    return pl.pallas_call(
        functools.partial(respond_kernel, len(groups), halves),
        out_shape=[sums] * len(groups),
        in_specs=[SMEM, VMEM] + [VMEM] * (len(groups) * halves),
        out_specs=[VMEM] * len(groups),
        compiler_params=pltpu.CompilerParams(vmem_limit_bytes=16 * 2**20),
        cost_estimate=pl.CostEstimate(
            flops=len(groups) * domains * 8 * angles * depth * cols, bytes_accessed=2 * response.size, transcendentals=0
        ),
        name="respond",
    )(jitter, response, *[piece for group in groups for piece in group])


def stitch_kernel(*refs):
    sources, plane = refs[:4], refs[4]
    me = lax.axis_index("ang")
    plane[...] = jnp.zeros_like(plane)
    for step in range(4):
        owner = lax.rem(me + step, 4)
        plane[pl.ds(owner, sources[step].shape[0])] += sources[step][...].astype(jnp.float32)


def stitch(sources):
    blocks, rows, lanes = sources[0].shape
    return pl.pallas_call(
        stitch_kernel,
        out_shape=jax.ShapeDtypeStruct((blocks + 3, rows, lanes), jnp.float32),
        in_specs=[VMEM] * 4,
        out_specs=VMEM,
        compiler_params=pltpu.CompilerParams(vmem_limit_bytes=8 * 2**20),
        name="stitch",
    )(*sources)


def pack_kernel(mine_ref, other_ref, chip_ref, far_ref):
    odd = lax.rem(lax.axis_index("dom"), 2) == 1
    blocks = mine_ref.shape[0] - HALO

    def fill(even_ref, odd_ref, first):
        chip_ref[pl.ds(0, blocks)] = even_ref[pl.ds(0, blocks)].astype(chip_ref.dtype)
        joined = odd_ref[pl.ds(0, HALO)] + even_ref[pl.ds(blocks, HALO)]
        chip_ref[pl.ds(blocks, HALO)] = joined.astype(chip_ref.dtype)
        rest = odd_ref[pl.ds(HALO, blocks)]
        chip_ref[pl.ds(blocks + HALO, blocks)] = rest.astype(chip_ref.dtype)
        far_ref[...] = chip_ref[pl.ds(first, blocks + HALO)]

    @pl.when(odd)
    def _():
        fill(other_ref, mine_ref, blocks)

    @pl.when(jnp.logical_not(odd))
    def _():
        fill(mine_ref, other_ref, 0)


def pack(mine, other):
    total, rows, lanes = mine.shape
    blocks = total - HALO
    return pl.pallas_call(
        pack_kernel,
        out_shape=[
            jax.ShapeDtypeStruct((2 * blocks + HALO, rows, lanes), jnp.bfloat16),
            jax.ShapeDtypeStruct((blocks + HALO, rows, lanes), jnp.bfloat16),
        ],
        in_specs=[VMEM] * 2,
        out_specs=[VMEM] * 2,
        compiler_params=pltpu.CompilerParams(vmem_limit_bytes=8 * 2**20),
        name="pack",
    )(mine, other)


def couple_kernel(cols_ref, counts_ref, green_ref, chip_ref, near_ref, far_ref, swap_near_ref, swap_far_ref, out_ref, window):
    rows, lanes = chip_ref.shape[1:]
    blocks = far_ref.shape[0] - HALO
    angles = rows // 2
    entries = green_ref.shape[1]
    me = lax.axis_index("dom")
    odd = lax.rem(me, 2) == 1

    def put(slot, ref, first, halo_ref=None, halo_first=None):
        at = slot * blocks
        if halo_ref is None:
            window[pl.ds(at, blocks)] = ref[pl.ds(first, blocks)]
            return
        low = ref[pl.ds(first, HALO)].astype(jnp.float32)
        halo = halo_ref[pl.ds(halo_first, HALO)].astype(jnp.float32)
        window[pl.ds(at, HALO)] = (low + halo).astype(window.dtype)
        window[pl.ds(at + HALO, blocks - HALO)] = ref[pl.ds(first + HALO, blocks - HALO)]

    def fill(left_ref, right_ref, left_far_ref):
        put(1, left_ref, 0, left_far_ref, blocks)
        put(2, left_ref, blocks)
        put(3, chip_ref, 0, left_ref, 2 * blocks)
        put(4, chip_ref, blocks)
        put(5, right_ref, 0, chip_ref, 2 * blocks)
        put(6, right_ref, blocks)

    @pl.when(odd)
    def _():
        fill(swap_near_ref, near_ref, swap_far_ref)
        put(7, far_ref, 0, near_ref, 2 * blocks)

    @pl.when(jnp.logical_not(odd))
    def _():
        fill(near_ref, swap_near_ref, far_ref)
        put(0, far_ref, 0)

    dead = 8 * blocks
    window[dead] = jnp.zeros((rows, lanes), window.dtype)
    first_col = (me - lax.rem(me, 2) - REACH) * blocks
    for r in range(green_ref.shape[0]):
        picked = []
        for k in range(entries):
            index = jnp.where(k < counts_ref[r], cols_ref[r, k] - first_col, dead)
            picked.append(window[index])
        wave = jnp.concatenate(picked, axis=1)
        green = jnp.concatenate(
            [green_ref[r, :, 0].reshape(entries * lanes, lanes), green_ref[r, :, 1].reshape(entries * lanes, lanes)],
            axis=1,
        )
        product = jnp.dot(wave, green, preferred_element_type=jnp.float32)
        at = pl.ds(r * lanes, lanes)
        out_ref[0, :, at] = product[:angles, :lanes] - product[angles:, lanes:]
        out_ref[1, :, at] = product[:angles, lanes:] + product[angles:, :lanes]


def couple(block_cols, block_counts, green, chip, near, far, swap_near, swap_far):
    rows_here, entries = block_cols.shape
    _, rows, lanes = chip.shape
    blocks = far.shape[0] - HALO
    flops = rows_here * 2 * rows * entries * lanes * 2 * lanes
    return pl.pallas_call(
        couple_kernel,
        out_shape=jax.ShapeDtypeStruct((2, rows // 2, rows_here * lanes), jnp.float32),
        in_specs=[SMEM, SMEM] + [VMEM] * 6,
        out_specs=VMEM,
        scratch_shapes=[pltpu.VMEM((8 * blocks + 8, rows, lanes), jnp.bfloat16)],
        compiler_params=pltpu.CompilerParams(vmem_limit_bytes=24 * 2**20),
        cost_estimate=pl.CostEstimate(flops=flops, bytes_accessed=green.size * 2, transcendentals=0),
        name="couple",
    )(block_cols, block_counts, green, chip, near, far, swap_near, swap_far)


def per_device(incident, response, jitter, block_cols, block_counts, green_blocks):
    half = incident.shape[0] // 2
    low, high = incident[:half], incident[half:]
    before_low, after_high = ring(low, 1), ring(high, -1)
    before_high, after_low = ring(high, 1), ring(low, -1)
    across_low, across_high = ring(before_low, 1), ring(after_high, -1)

    own, panels = respond_own(jitter, incident, response)
    before, after = respond(jitter, panels, [(before_low, before_high), (after_low, after_high)])
    (across,) = respond(jitter, panels, [(across_low, across_high)])
    mine = stitch([own, ring(before, -1), ring(across, 2), ring(after, 1)])

    chip, far = pack(mine, facing(mine, 1))
    near_in, far_in = facing(chip, -1), facing(far, -3)
    return couple(
        block_cols, block_counts, green_blocks, chip, near_in, far_in, facing(near_in, 1), facing(far_in, 1)
    )


def solution(mesh):
    return jax.shard_map(
        per_device,
        mesh=mesh,
        in_specs=(
            P("dom", None, "ang", None),
            P("dom", None, None, "ang"),
            P("dom"),
            P("dom", None),
            P("dom"),
            P("dom", None, None, None, None),
        ),
        out_specs=P(None, "ang", "dom"),
        check_vma=False,
    )
```

time: 63.7 us -> 54.9 us (0.86); the launches traced: 62.5 us -> 54.7 us
  starting transfers between devices: 43 us -> 33.1 us
  waiting for transfers between devices: 7.31 us -> 8.97 us
    ppermute x4 -> x0, starting transfers between devices: 19.4 us -> none  [to_next_domains(): return lax.ppermute(block, ('dom', 'ang'), route)]
    ppermute x6 -> x5, starting transfers between devices: 13.7 us -> 21.6 us  [facing(): lax.ppermute(block, 'dom', [(s, t) for s, t in route if 0 <= t < doms])]
    ppermute x9, waiting for transfers between devices: 3.04 us -> 6.94 us  [ring(): lax.ppermute(block, 'ang', [(i, (i + distance) % size) for i in range(siz...]
    pallas_call x1 -> x3, Pallas kernels: 0.11 us -> 1.83 us  [the longest x1 1.73 us: respond_own(): pl.pallas_call(functools.partial(own_kernel, chunk), out_shape=[jax.Shape...]
    ppermute x9, starting transfers between devices: 9.89 us -> 11.6 us  [ring(): lax.ppermute(block, 'ang', [(i, (i + distance) % size) for i in range(siz...]
    pallas_call x3 -> x2, Pallas kernels: 4.56 us -> 3.23 us  [respond(): pl.pallas_call(functools.partial(respond_kernel, len(groups), halves), ou...]
    ppermute x4 -> x0, waiting for transfers between devices: 1.3 us -> none  [to_next_domains(): return lax.ppermute(block, ('dom', 'ang'), route)]
    ppermute x6 -> x5, waiting for transfers between devices: 2.97 us -> 2.02 us  [facing(): lax.ppermute(block, 'dom', [(s, t) for s, t in route if 0 <= t < doms])]
  transfers between devices with their start and end apart: 19 -> 14, of which waited for: 3 -> 4; matrix products, arithmetic and copies ran while one was open for 0% -> 0% of each run, Pallas kernels for 7% -> 9%
where the time goes in v2:
time: 54.9 us; the launch traced here: 54.7 us
  starting transfers between devices  33.1 us (60%)
  waiting for transfers between devices  8.97 us (16%)
  Pallas kernels  7.49 us (14%)
  local copies, waits for them, and re-layouts  4.97 us (9%)
    ppermute x5, starting transfers between devices, facing(): lax.ppermute(block, 'dom', [(s, t) for s, t in route if 0 <= t < doms])  21.6 us
    ppermute x9, starting transfers between devices, ring(): lax.ppermute(block, 'ang', [(i, (i + distance) % size) for i in range(siz...  11.6 us
    ppermute x9, waiting for transfers between devices, ring(): lax.ppermute(block, 'ang', [(i, (i + distance) % size) for i in range(siz...  6.94 us
    unnamed x14, local copies, waits for them, and re-layouts  3.91 us
    pallas_call x2, Pallas kernels, respond(): pl.pallas_call(functools.partial(respond_kernel, len(groups), halves), ou...  3.23 us
    pallas_call x1, Pallas kernels, couple(): pl.pallas_call(couple_kernel, out_shape=jax.ShapeDtypeStruct((2, rows //...  2.44 us
    ppermute x5, waiting for transfers between devices, facing(): lax.ppermute(block, 'dom', [(s, t) for s, t in route if 0 <= t < doms])  2.02 us
    pallas_call x1, Pallas kernels, respond_own(): pl.pallas_call(functools.partial(own_kernel, chunk), out_shape=[jax.Shape...  1.73 us
  transfers between devices with their start and end apart: 14, of which 4 were waited for; matrix products, arithmetic and copies ran while one was open for 0% of the time, Pallas kernels for 9%

profile of v2, /device:TPU:7, one launch (start us, length us, event | category | flops | bytes accessed | tf_op | source)
XLA Modules:
  0.0 54.7 jit_solution(16121254613700482060)
XLA Ops:
  0.0 1.1 %fusion = (bf16[8,2,16,512]{3,2,1,0:T(8,128)(2,1)S(1)}, bf16[8,2,16,512]{3,2,1,0:T(8,128)(2,1)S(1)}) fusion(bf16[16,2,16,512]{3,2,1,0:T(8,128)(2,1)} %incident_hbm.1), kind=kLoop, calls=%fused_computation | loop fusion | bytes 1048576 | tf_op jit(solution)/shard_map/slice | solution.py:253
  1.1 1.4 %collective-permute-start = (bf16[8,2,16,512]{3,2,1,0:T(8,128)(2,1)S(1)}, bf16[8,2,16,512]{3,2,1,0:T(8,128)(2,1)S(1)}, u32[]{:S(2)}, u32[]{:S(2)}) collective-permute-start(bf16[8,2,16,512]{3,2,1,0:T(8,128)(2,1)S(1)} %get-tuple-element.18), channel_id=1, source_target_pairs={{0,1},{1,2},{2,3},{3,0},{4,5},{5,6},{6,7},{7,4},{8,9},{9,10},{10,1... | collective-permute-start | bytes 786440 | tf_op jit(solution)/shard_map/ppermute | solution.py:19
  2.4 1.5 %collective-permute-start.3 = (bf16[8,2,16,512]{3,2,1,0:T(8,128)(2,1)S(1)}, bf16[8,2,16,512]{3,2,1,0:T(8,128)(2,1)S(1)}, u32[]{:S(2)}, u32[]{:S(2)}) collective-permute-start(bf16[8,2,16,512]{3,2,1,0:T(8,128)(2,1)S(1)} %get-tuple-element.17), channel_id=1, source_target_pairs={{0,3},{1,0},{2,1},{3,2},{4,7},{5,4},{6,5},{7,6},{8,11},{9,8},{10,9... | collective-permute-start | bytes 786440 | tf_op jit(solution)/shard_map/ppermute | solution.py:19
  4.0 0.0 collective-permute-start.1
  4.0 2.7 %collective-permute-start.2 = (bf16[8,2,16,512]{3,2,1,0:T(8,128)(2,1)S(1)}, bf16[8,2,16,512]{3,2,1,0:T(8,128)(2,1)S(1)}, u32[]{:S(2)}, u32[]{:S(2)}) collective-permute-start(bf16[8,2,16,512]{3,2,1,0:T(8,128)(2,1)S(1)} %get-tuple-element.18), channel_id=1, source_target_pairs={{0,3},{1,0},{2,1},{3,2},{4,7},{5,4},{6,5},{7,6},{8,11},{9,8},{10,9... | collective-permute-start | bytes 786440 | tf_op jit(solution)/shard_map/ppermute | solution.py:19
  6.6 3.0 %collective-permute-done.refs_2_ = bf16[8,2,16,512]{3,2,1,0:T(8,128)(2,1)S(1)} collective-permute-done((bf16[8,2,16,512]{3,2,1,0:T(8,128)(2,1)S(1)}, bf16[8,2,16,512]{3,2,1,0:T(8,128)(2,1)S(1)}, u32[]{:S(2)}, u32[]{:S(2)}) %collective-permute-start) | collective-permute-done | bytes 262176 | tf_op jit(solution)/shard_map/ppermute | solution.py:19
  9.7 0.0 collective-permute-start.5
  9.7 0.0 collective-permute-done.3.refs_5_
  9.7 2.7 %collective-permute-start.6 = (bf16[8,2,16,512]{3,2,1,0:T(8,128)(2,1)S(1)}, bf16[8,2,16,512]{3,2,1,0:T(8,128)(2,1)S(1)}, u32[]{:S(2)}, u32[]{:S(2)}) collective-permute-start(bf16[8,2,16,512]{3,2,1,0:T(8,128)(2,1)S(1)} %collective-permute-done.3.refs_5_), channel_id=1, source_target_pairs={{0,3},{1,0},{2,1},{3,2},{4,7},{5,4},{6,5},{7,6},{8,11},{9,8},{10,9... | collective-permute-start | bytes 786440 | tf_op jit(solution)/shard_map/ppermute | solution.py:19
  12.3 0.0 copy-start
  12.3 2.2 %copy-done = bf16[16,2,512,128]{3,2,1,0:T(8,128)(2,1)S(1)} copy-done((bf16[16,2,512,128]{3,2,1,0:T(8,128)(2,1)S(1)}, bf16[16,2,512,128]{3,2,1,0:T(8,128)(2,1)}, u32[]{:S(2)}) %copy-start) | copy-done | bytes 4194328
  14.5 0.0 copy-start.1
  14.5 1.0 %copy-done.1 = bf16[16,2,16,512]{3,2,1,0:T(8,128)(2,1)S(1)} copy-done((bf16[16,2,16,512]{3,2,1,0:T(8,128)(2,1)S(1)}, bf16[16,2,16,512]{3,2,1,0:T(8,128)(2,1)}, u32[]{:S(2)}) %copy-start.1) | copy-done | bytes 524312
  15.6 0.0 copy-start.2
  15.6 0.7 %copy-done.2 = s32[16]{0:T(128)S(1)} copy-done((s32[16]{0:T(128)S(1)}, s32[16]{0:T(128)}, u32[]{:S(2)}) %copy-start.2) | copy-done | bytes 88
  16.2 0.0 slice-start
  16.2 1.7 %respond_own.1 = (f32[9,32,128]{2,1,0:T(8,128)S(1)}, bf16[16,2,512,128]{3,2,1,0:T(8,128)(2,1)S(1)}) custom-call(s32[16]{0:T(128)S(1)} %copy-done.2, bf16[16,2,16,512]{3,2,1,0:T(8,128)(2,1)S(1)} %copy-done.1, bf16[16,2,512,128]{3,2,1,0:T(8,128)(2,1)S(1)} %copy-done), custom_call_target="tpu_custom_call" | custom-call | flops 134217728 | bytes 8388608 | tf_op jit(solution)/shard_map/respond_own/pallas_call | solution.py:72
  18.0 0.0 collective-permute-done.1.refs_3_
  18.0 0.0 collective-permute-done.2.refs_4_
  18.0 0.0 slice-start.1
  18.0 0.0 copy-start.3
  18.0 0.0 copy-start.4
  18.0 1.9 %respond.2 = (bf16[9,32,128]{2,1,0:T(8,128)(2,1)S(1)}, bf16[9,32,128]{2,1,0:T(8,128)(2,1)S(1)}) custom-call(s32[16]{0:T(128)S(1)} %copy-done.2, bf16[16,2,512,128]{3,2,1,0:T(8,128)(2,1)S(1)} %get-tuple-element.12.refs_1_, bf16[8,2,16,512]{3,2,1,0:T(8,128)(2,1)S(1)} %collective-permute-done.refs_2_, ...), custom_call_target="tpu_custom_call" | custom-call | flops 268435456 | bytes 4194304 | tf_op jit(solution)/shard_map/respond/pallas_call | solution.py:108
  19.9 0.3 collective-permute-start.4
  20.2 1.3 %collective-permute-start.8 = (bf16[9,32,128]{2,1,0:T(8,128)(2,1)S(1)}, bf16[9,32,128]{2,1,0:T(8,128)(2,1)S(1)}, u32[]{:S(2)}, u32[]{:S(2)}) collective-permute-start(bf16[9,32,128]{2,1,0:T(8,128)(2,1)S(1)} %get-tuple-element.14), channel_id=1, source_target_pairs={{0,1},{1,2},{2,3},{3,0},{4,5},{5,6},{6,7},{7,4},{8,9},{9,10},{10,1... | collective-permute-start | bytes 221192 | tf_op jit(solution)/shard_map/ppermute | solution.py:19
  21.5 0.0 collective-permute-done.5.refs_2_
  21.5 0.0 collective-permute-done.6.refs_3_
  21.5 1.3 %respond.3 = bf16[9,32,128]{2,1,0:T(8,128)(2,1)S(1)} custom-call(s32[16]{0:T(128)S(1)} %copy-done.2, bf16[16,2,512,128]{3,2,1,0:T(8,128)(2,1)S(1)} %get-tuple-element.12.refs_1_, bf16[8,2,16,512]{3,2,1,0:T(8,128)(2,1)S(1)} %collective-permute-done.5.refs_2_, bf16[8,2,16,512]{3,2,1,0:T(8,128)(2,1)S(1)} %collective-permute-done.6.refs_3_), custom_call_target="tpu_custom_call" | custom-call | flops 134217728 | bytes 4194304 | tf_op jit(solution)/shard_map/respond/pallas_call | solution.py:108
  22.8 1.8 %collective-permute-start.7 = (bf16[9,32,128]{2,1,0:T(8,128)(2,1)S(1)}, bf16[9,32,128]{2,1,0:T(8,128)(2,1)S(1)}, u32[]{:S(2)}, u32[]{:S(2)}) collective-permute-start(bf16[9,32,128]{2,1,0:T(8,128)(2,1)S(1)} %respond.3), channel_id=1, source_target_pairs={{0,2},{1,3},{2,0},{3,1},{4,6},{5,7},{6,4},{7,5},{8,10},{9,11},{10,... | collective-permute-start | bytes 221192 | tf_op jit(solution)/shard_map/ppermute | solution.py:19
  24.6 0.0 collective-permute-done.4.refs_1_
  24.6 0.0 collective-permute-done.8.refs_3_
  24.6 3.9 %collective-permute-done.7.refs_2_ = bf16[9,32,128]{2,1,0:T(8,128)(2,1)S(1)} collective-permute-done((bf16[9,32,128]{2,1,0:T(8,128)(2,1)S(1)}, bf16[9,32,128]{2,1,0:T(8,128)(2,1)S(1)}, u32[]{:S(2)}, u32[]{:S(2)}) %collective-permute-start.7) | collective-permute-done | bytes 73760 | tf_op jit(solution)/shard_map/ppermute | solution.py:19
  28.5 0.1 stitch.1.mine_ref
  28.6 4.1 %collective-permute-start.9 = (f32[12,32,128]{2,1,0:T(8,128)S(1)}, f32[12,32,128]{2,1,0:T(8,128)S(1)}, u32[]{:S(2)}, u32[]{:S(2)}) collective-permute-start(f32[12,32,128]{2,1,0:T(8,128)S(1)} %stitch.1.mine_ref), channel_id=1, source_target_pairs={{0,4},{4,0},{8,12},{12,8},{16,20},{20,16},{24,28},{28,24},{32,36},... | collective-permute-start | bytes 589832 | tf_op jit(solution)/shard_map/ppermute | solution.py:25
  32.6 1.1 %collective-permute-done.9.other_ref = f32[12,32,128]{2,1,0:T(8,128)S(1)} collective-permute-done((f32[12,32,128]{2,1,0:T(8,128)S(1)}, f32[12,32,128]{2,1,0:T(8,128)S(1)}, u32[]{:S(2)}, u32[]{:S(2)}) %collective-permute-start.9) | collective-permute-done | bytes 196640 | tf_op jit(solution)/shard_map/ppermute | solution.py:25
  33.7 3.8 %collective-permute-start.10 = (bf16[20,32,128]{2,1,0:T(8,128)(2,1)S(1)}, bf16[20,32,128]{2,1,0:T(8,128)(2,1)S(1)}, u32[]{:S(2)}, u32[]{:S(2)}) collective-permute-start(bf16[20,32,128]{2,1,0:T(8,128)(2,1)S(1)} %get-tuple-element.15.chip_ref), channel_id=1, source_target_pairs={{4,8},{8,4},{12,16},{16,12},{20,24},{24,20},{28,32},{32,28},{36,40... | collective-permute-start | bytes 491528 | tf_op jit(solution)/shard_map/ppermute | solution.py:25
  37.5 3.3 %collective-permute-start.11 = (bf16[12,32,128]{2,1,0:T(8,128)(2,1)S(1)}, bf16[12,32,128]{2,1,0:T(8,128)(2,1)S(1)}, u32[]{:S(2)}, u32[]{:S(2)}) collective-permute-start(bf16[12,32,128]{2,1,0:T(8,128)(2,1)S(1)} %get-tuple-element.16), channel_id=1, source_target_pairs={{4,16},{12,24},{16,4},{20,32},{24,12},{28,40},{32,20},{36,48},{40,... | collective-permute-start | bytes 294920 | tf_op jit(solution)/shard_map/ppermute | solution.py:25
  40.8 0.0 collective-permute-done.10.near_ref
  40.8 4.5 %collective-permute-start.12 = (bf16[20,32,128]{2,1,0:T(8,128)(2,1)S(1)}, bf16[20,32,128]{2,1,0:T(8,128)(2,1)S(1)}, u32[]{:S(2)}, u32[]{:S(2)}) collective-permute-start(bf16[20,32,128]{2,1,0:T(8,128)(2,1)S(1)} %collective-permute-done.10.near_ref), channel_id=1, source_target_pairs={{0,4},{4,0},{8,12},{12,8},{16,20},{20,16},{24,28},{28,24},{32,36},... | collective-permute-start | bytes 491528 | tf_op jit(solution)/shard_map/ppermute | solution.py:25
  45.3 0.0 collective-permute-done.11.far_ref
  45.3 5.9 %collective-permute-start.13 = (bf16[12,32,128]{2,1,0:T(8,128)(2,1)S(1)}, bf16[12,32,128]{2,1,0:T(8,128)(2,1)S(1)}, u32[]{:S(2)}, u32[]{:S(2)}) collective-permute-start(bf16[12,32,128]{2,1,0:T(8,128)(2,1)S(1)} %collective-permute-done.11.far_ref), channel_id=1, source_target_pairs={{0,4},{4,0},{8,12},{12,8},{16,20},{20,16},{24,28},{28,24},{32,36},... | collective-permute-start | bytes 294920 | tf_op jit(solution)/shard_map/ppermute | solution.py:25
  51.3 0.9 %collective-permute-done.13.swap_far_ref = bf16[12,32,128]{2,1,0:T(8,128)(2,1)S(1)} collective-permute-done((bf16[12,32,128]{2,1,0:T(8,128)(2,1)S(1)}, bf16[12,32,128]{2,1,0:T(8,128)(2,1)S(1)}, u32[]{:S(2)}, u32[]{:S(2)}) %collective-permute-start.13) | collective-permute-done | bytes 98336 | tf_op jit(solution)/shard_map/ppermute | solution.py:25
  52.2 0.0 collective-permute-done.12.swap_near_ref
  52.2 0.0 slice-done
  52.2 0.0 slice-done.1
  52.2 0.0 copy-done.3
  52.2 0.0 copy-done.4
  52.2 2.4 %couple.1 = f32[2,16,1024]{2,1,0:T(8,128)} custom-call(s32[8,12]{1,0:T(8,128)S(1)} %copy-done.3, s32[8]{0:T(128)S(1)} %copy-done.4, bf16[8,12,2,128,128]{4,3,2,1,0:T(8,128)(2,1)S(1)} %bitcast.1, bf16[20,32,128]{2,1,0:T(8,128)(2,1)S(1)} %get-tuple-element.15.chip_ref, bf16[20,32,128]{2,1,0:T(8,128)(2,1)S(1)} %collective-permute-done.10.near_ref, ...), custom_call_target="tpu_custom_call" | custom-call | flops 201326592 | bytes 6291456 | tf_op jit(solution)/shard_map/couple/pallas_call | solution.py:239
  (2 shorter events, 0.0 us)
Async XLA Ops:
  1.1 8.6 %collective-permute-start = (bf16[8,2,16,512]{3,2,1,0:T(8,128)(2,1)S(1)}, bf16[8,2,16,512]{3,2,1,0:T(8,128)(2,1)S(1)}, u32[]{:S(2)}, u32[]{:S(2)}) collective-permute-start(bf16[8,2,16,512]{3,2,1,0:T(8,128)(2,1)S(1)} %get-tuple-element.18), channel_id=1, source_target_pairs={{0,1},{1,2},{2,3},{3,0},{4,5},{5,6},{6,7},{7,4},{8,9},{9,10},{10,1... | collective-permute-start | bytes 786440 | tf_op jit(solution)/shard_map/ppermute | solution.py:19
  2.4 7.2 %collective-permute-start.3 = (bf16[8,2,16,512]{3,2,1,0:T(8,128)(2,1)S(1)}, bf16[8,2,16,512]{3,2,1,0:T(8,128)(2,1)S(1)}, u32[]{:S(2)}, u32[]{:S(2)}) collective-permute-start(bf16[8,2,16,512]{3,2,1,0:T(8,128)(2,1)S(1)} %get-tuple-element.17), channel_id=1, source_target_pairs={{0,3},{1,0},{2,1},{3,2},{4,7},{5,4},{6,5},{7,6},{8,11},{9,8},{10,9... | collective-permute-start | bytes 786440 | tf_op jit(solution)/shard_map/ppermute | solution.py:19
  4.0 14.0 %collective-permute-start.1 = (bf16[8,2,16,512]{3,2,1,0:T(8,128)(2,1)S(1)}, bf16[8,2,16,512]{3,2,1,0:T(8,128)(2,1)S(1)}, u32[]{:S(2)}, u32[]{:S(2)}) collective-permute-start(bf16[8,2,16,512]{3,2,1,0:T(8,128)(2,1)S(1)} %get-tuple-element.17), channel_id=1, source_target_pairs={{0,1},{1,2},{2,3},{3,0},{4,5},{5,6},{6,7},{7,4},{8,9},{9,10},{10,1... | collective-permute-start | bytes 786440 | tf_op jit(solution)/shard_map/ppermute | solution.py:19
  4.0 14.0 %collective-permute-start.2 = (bf16[8,2,16,512]{3,2,1,0:T(8,128)(2,1)S(1)}, bf16[8,2,16,512]{3,2,1,0:T(8,128)(2,1)S(1)}, u32[]{:S(2)}, u32[]{:S(2)}) collective-permute-start(bf16[8,2,16,512]{3,2,1,0:T(8,128)(2,1)S(1)} %get-tuple-element.18), channel_id=1, source_target_pairs={{0,3},{1,0},{2,1},{3,2},{4,7},{5,4},{6,5},{7,6},{8,11},{9,8},{10,9... | collective-permute-start | bytes 786440 | tf_op jit(solution)/shard_map/ppermute | solution.py:19
  9.7 11.8 %collective-permute-start.5 = (bf16[8,2,16,512]{3,2,1,0:T(8,128)(2,1)S(1)}, bf16[8,2,16,512]{3,2,1,0:T(8,128)(2,1)S(1)}, u32[]{:S(2)}, u32[]{:S(2)}) collective-permute-start(bf16[8,2,16,512]{3,2,1,0:T(8,128)(2,1)S(1)} %collective-permute-done.refs_2_), channel_id=1, source_target_pairs={{0,1},{1,2},{2,3},{3,0},{4,5},{5,6},{6,7},{7,4},{8,9},{9,10},{10,1... | collective-permute-start | bytes 786440 | tf_op jit(solution)/shard_map/ppermute | solution.py:19
  9.7 11.8 %collective-permute-start.6 = (bf16[8,2,16,512]{3,2,1,0:T(8,128)(2,1)S(1)}, bf16[8,2,16,512]{3,2,1,0:T(8,128)(2,1)S(1)}, u32[]{:S(2)}, u32[]{:S(2)}) collective-permute-start(bf16[8,2,16,512]{3,2,1,0:T(8,128)(2,1)S(1)} %collective-permute-done.3.refs_5_), channel_id=1, source_target_pairs={{0,3},{1,0},{2,1},{3,2},{4,7},{5,4},{6,5},{7,6},{8,11},{9,8},{10,9... | collective-permute-start | bytes 786440 | tf_op jit(solution)/shard_map/ppermute | solution.py:19
  12.3 2.2 %copy-start = (bf16[16,2,512,128]{3,2,1,0:T(8,128)(2,1)S(1)}, bf16[16,2,512,128]{3,2,1,0:T(8,128)(2,1)}, u32[]{:S(2)}) copy-start(bf16[16,2,512,128]{3,2,1,0:T(8,128)(2,1)} %response_hbm.1) | copy-start | bytes 12582916
  14.5 1.0 %copy-start.1 = (bf16[16,2,16,512]{3,2,1,0:T(8,128)(2,1)S(1)}, bf16[16,2,16,512]{3,2,1,0:T(8,128)(2,1)}, u32[]{:S(2)}) copy-start(bf16[16,2,16,512]{3,2,1,0:T(8,128)(2,1)} %incident_hbm.1) | copy-start | bytes 1572868
  15.6 0.7 %copy-start.2 = (s32[16]{0:T(128)S(1)}, s32[16]{0:T(128)}, u32[]{:S(2)}) copy-start(s32[16]{0:T(128)} %refs_0_.3) | copy-start | bytes 196
  16.2 36.0 %slice-start = ((s8[6291456]{0:T(1024)(128)(4,1)}), s8[4194304]{0:T(1024)(128)(4,1)S(1)}, s32[]{:S(2)}) async-start(s8[6291456]{0:T(1024)(128)(4,1)} %bitcast), calls=%async_computation | async-start | bytes 8388608
  18.0 34.2 %slice-start.1 = ((s8[6291456]{0:T(1024)(128)(4,1)}), s8[2097152]{0:T(1024)(128)(4,1)S(1)}, s32[]{:S(2)}) async-start(s8[6291456]{0:T(1024)(128)(4,1)} %bitcast), calls=%async_computation.1 | async-start | bytes 4194304
  18.0 34.2 %copy-start.3 = (s32[8,12]{1,0:T(8,128)S(1)}, s32[8,12]{1,0:T(8,128)}, u32[]{:S(2)}) copy-start(s32[8,12]{1,0:T(8,128)} %cols_ref.1) | copy-start | bytes 1156
  18.0 34.2 %copy-start.4 = (s32[8]{0:T(128)S(1)}, s32[8]{0:T(128)}, u32[]{:S(2)}) copy-start(s32[8]{0:T(128)} %counts_ref.1) | copy-start | bytes 100
  19.9 4.6 %collective-permute-start.4 = (bf16[9,32,128]{2,1,0:T(8,128)(2,1)S(1)}, bf16[9,32,128]{2,1,0:T(8,128)(2,1)S(1)}, u32[]{:S(2)}, u32[]{:S(2)}) collective-permute-start(bf16[9,32,128]{2,1,0:T(8,128)(2,1)S(1)} %get-tuple-element.13), channel_id=1, source_target_pairs={{0,3},{1,0},{2,1},{3,2},{4,7},{5,4},{6,5},{7,6},{8,11},{9,8},{10,9... | collective-permute-start | bytes 221192 | tf_op jit(solution)/shard_map/ppermute | solution.py:19
  20.2 4.4 %collective-permute-start.8 = (bf16[9,32,128]{2,1,0:T(8,128)(2,1)S(1)}, bf16[9,32,128]{2,1,0:T(8,128)(2,1)S(1)}, u32[]{:S(2)}, u32[]{:S(2)}) collective-permute-start(bf16[9,32,128]{2,1,0:T(8,128)(2,1)S(1)} %get-tuple-element.14), channel_id=1, source_target_pairs={{0,1},{1,2},{2,3},{3,0},{4,5},{5,6},{6,7},{7,4},{8,9},{9,10},{10,1... | collective-permute-start | bytes 221192 | tf_op jit(solution)/shard_map/ppermute | solution.py:19
  22.8 5.7 %collective-permute-start.7 = (bf16[9,32,128]{2,1,0:T(8,128)(2,1)S(1)}, bf16[9,32,128]{2,1,0:T(8,128)(2,1)S(1)}, u32[]{:S(2)}, u32[]{:S(2)}) collective-permute-start(bf16[9,32,128]{2,1,0:T(8,128)(2,1)S(1)} %respond.3), channel_id=1, source_target_pairs={{0,2},{1,3},{2,0},{3,1},{4,6},{5,7},{6,4},{7,5},{8,10},{9,11},{10,... | collective-permute-start | bytes 221192 | tf_op jit(solution)/shard_map/ppermute | solution.py:19
  28.6 5.1 %collective-permute-start.9 = (f32[12,32,128]{2,1,0:T(8,128)S(1)}, f32[12,32,128]{2,1,0:T(8,128)S(1)}, u32[]{:S(2)}, u32[]{:S(2)}) collective-permute-start(f32[12,32,128]{2,1,0:T(8,128)S(1)} %stitch.1.mine_ref), channel_id=1, source_target_pairs={{0,4},{4,0},{8,12},{12,8},{16,20},{20,16},{24,28},{28,24},{32,36},... | collective-permute-start | bytes 589832 | tf_op jit(solution)/shard_map/ppermute | solution.py:25
  33.7 7.1 %collective-permute-start.10 = (bf16[20,32,128]{2,1,0:T(8,128)(2,1)S(1)}, bf16[20,32,128]{2,1,0:T(8,128)(2,1)S(1)}, u32[]{:S(2)}, u32[]{:S(2)}) collective-permute-start(bf16[20,32,128]{2,1,0:T(8,128)(2,1)S(1)} %get-tuple-element.15.chip_ref), channel_id=1, source_target_pairs={{4,8},{8,4},{12,16},{16,12},{20,24},{24,20},{28,32},{32,28},{36,40... | collective-permute-start | bytes 491528 | tf_op jit(solution)/shard_map/ppermute | solution.py:25
  37.5 7.8 %collective-permute-start.11 = (bf16[12,32,128]{2,1,0:T(8,128)(2,1)S(1)}, bf16[12,32,128]{2,1,0:T(8,128)(2,1)S(1)}, u32[]{:S(2)}, u32[]{:S(2)}) collective-permute-start(bf16[12,32,128]{2,1,0:T(8,128)(2,1)S(1)} %get-tuple-element.16), channel_id=1, source_target_pairs={{4,16},{12,24},{16,4},{20,32},{24,12},{28,40},{32,20},{36,48},{40,... | collective-permute-start | bytes 294920 | tf_op jit(solution)/shard_map/ppermute | solution.py:25
  40.8 11.4 %collective-permute-start.12 = (bf16[20,32,128]{2,1,0:T(8,128)(2,1)S(1)}, bf16[20,32,128]{2,1,0:T(8,128)(2,1)S(1)}, u32[]{:S(2)}, u32[]{:S(2)}) collective-permute-start(bf16[20,32,128]{2,1,0:T(8,128)(2,1)S(1)} %collective-permute-done.10.near_ref), channel_id=1, source_target_pairs={{0,4},{4,0},{8,12},{12,8},{16,20},{20,16},{24,28},{28,24},{32,36},... | collective-permute-start | bytes 491528 | tf_op jit(solution)/shard_map/ppermute | solution.py:25
  45.3 6.9 %collective-permute-start.13 = (bf16[12,32,128]{2,1,0:T(8,128)(2,1)S(1)}, bf16[12,32,128]{2,1,0:T(8,128)(2,1)S(1)}, u32[]{:S(2)}, u32[]{:S(2)}) collective-permute-start(bf16[12,32,128]{2,1,0:T(8,128)(2,1)S(1)} %collective-permute-done.11.far_ref), channel_id=1, source_target_pairs={{0,4},{4,0},{8,12},{12,8},{16,20},{20,16},{24,28},{28,24},{32,36},... | collective-permute-start | bytes 294920 | tf_op jit(solution)/shard_map/ppermute | solution.py:25

commit v3 on v2

--- a/solution.py
+++ b/solution.py
@@ -47,47 +47,20 @@
     return sums
 
 
-def own_kernel(chunk, jitter_ref, incident_hbm, response_hbm, sums_ref, response_ref, incident_ref, wave_sem, panel_sems):
-    domains = response_ref.shape[0]
-    wave_copy = pltpu.make_async_copy(incident_hbm, incident_ref, wave_sem)
-    wave_copy.start()
-    copies = []
-    for c in range(domains // chunk):
-        at = pl.ds(c * chunk, chunk)
-        copies.append(pltpu.make_async_copy(response_hbm.at[at], response_ref.at[at], panel_sems.at[c]))
-        copies[-1].start()
-    wave_copy.wait()
-    for copy in copies:
-        copy.wait()
-    sums = placed_sums(jitter_ref, [incident_ref], response_ref)
-    for b, block in enumerate(sums):
-        sums_ref[b] = block
-
-
-def respond_own(jitter, incident, response):
-    domains, _, depth, cols = response.shape
-    angles = incident.shape[2]
-    chunk = domains // 4
-    hbm = pl.BlockSpec(memory_space=pltpu.HBM)
-    return pl.pallas_call(
-        functools.partial(own_kernel, chunk),
-        out_shape=[
-            jax.ShapeDtypeStruct((domains // 2 + 1, 2 * angles, LANES), jnp.float32),
-            jax.ShapeDtypeStruct(response.shape, response.dtype),
-        ],
-        in_specs=[SMEM, hbm, hbm],
-        out_specs=[VMEM, VMEM],
-        scratch_shapes=[
-            pltpu.VMEM(incident.shape, incident.dtype),
-            pltpu.SemaphoreType.DMA,
-            pltpu.SemaphoreType.DMA((domains // chunk,)),
-        ],
-        compiler_params=pltpu.CompilerParams(vmem_limit_bytes=16 * 2**20),
-        cost_estimate=pl.CostEstimate(
-            flops=domains * 8 * angles * depth * cols, bytes_accessed=4 * response.size, transcendentals=0
-        ),
-        name="respond_own",
-    )(jitter, incident, response)
+def gate_kernel(held_ref, after_ref, out_ref):
+    pass
+
+
+def gate(held, after):
+    return pl.pallas_call(
+        gate_kernel,
+        out_shape=jax.ShapeDtypeStruct(held.shape, held.dtype),
+        in_specs=[VMEM, VMEM],
+        out_specs=VMEM,
+        input_output_aliases={0: 0},
+        compiler_params=pltpu.CompilerParams(vmem_limit_bytes=2**20),
+        name="gate",
+    )(held, after)
 
 
 def respond_kernel(groups, halves, *refs):
@@ -100,11 +73,11 @@
             outputs[g][b] = block.astype(outputs[g].dtype)
 
 
-def respond(jitter, response, groups):
+def respond(jitter, response, groups, kind=jnp.bfloat16):
     domains, _, depth, cols = response.shape
     halves = len(groups[0])
     angles = groups[0][0].shape[2]
-    sums = jax.ShapeDtypeStruct((domains // 2 + 1, 2 * angles, LANES), jnp.bfloat16)
+    sums = jax.ShapeDtypeStruct((domains // 2 + 1, 2 * angles, LANES), kind)
     return pl.pallas_call(
         functools.partial(respond_kernel, len(groups), halves),
         out_shape=[sums] * len(groups),
@@ -153,11 +126,11 @@
 
     @pl.when(odd)
     def _():
-        fill(other_ref, mine_ref, blocks)
+        fill(other_ref, mine_ref, 0)
 
     @pl.when(jnp.logical_not(odd))
     def _():
-        fill(mine_ref, other_ref, 0)
+        fill(mine_ref, other_ref, blocks)
 
 
 def pack(mine, other):
@@ -253,15 +226,16 @@
     low, high = incident[:half], incident[half:]
     before_low, after_high = ring(low, 1), ring(high, -1)
     before_high, after_low = ring(high, 1), ring(low, -1)
+    (own,) = respond(jitter, response, [(low, high)], jnp.float32)
+    before_low, after_high = gate(before_low, own), gate(after_high, own)
     across_low, across_high = ring(before_low, 1), ring(after_high, -1)
 
-    own, panels = respond_own(jitter, incident, response)
-    before, after = respond(jitter, panels, [(before_low, before_high), (after_low, after_high)])
-    (across,) = respond(jitter, panels, [(across_low, across_high)])
+    before, after = respond(jitter, response, [(before_low, before_high), (after_low, after_high)])
+    (across,) = respond(jitter, response, [(across_low, across_high)])
     mine = stitch([own, ring(before, -1), ring(across, 2), ring(after, 1)])
 
     chip, far = pack(mine, facing(mine, 1))
-    near_in, far_in = facing(chip, -1), facing(far, -3)
+    far_in, near_in = facing(far, 4), facing(chip, 2)
     return couple(
         block_cols, block_counts, green_blocks, chip, near_in, far_in, facing(near_in, 1), facing(far_in, 1)
     )

time: 54.9 us -> 53.4 us (0.973)
  starting transfers between devices: 33.1 us -> 25.3 us
  waiting for transfers between devices: 8.97 us -> 16.7 us
  local copies, waits for them, and re-layouts: 4.97 us -> 3.93 us
    ppermute x9, waiting for transfers between devices: 6.94 us -> 12 us  [ring(): lax.ppermute(block, 'ang', [(i, (i + distance) % size) for i in range(siz...]
    ppermute x5, starting transfers between devices: 21.6 us -> 16.6 us  [facing(): lax.ppermute(block, 'dom', [(s, t) for s, t in route if 0 <= t < doms])]
    ppermute x9, starting transfers between devices: 11.6 us -> 8.7 us  [ring(): lax.ppermute(block, 'ang', [(i, (i + distance) % size) for i in range(siz...]
    ppermute x5, waiting for transfers between devices: 2.02 us -> 4.69 us  [facing(): lax.ppermute(block, 'dom', [(s, t) for s, t in route if 0 <= t < doms])]
    pallas_call x1 -> x2, Pallas kernels: 1.73 us -> 0.01 us  [gate(): pl.pallas_call(gate_kernel, out_shape=jax.ShapeDtypeStruct(held.shape, he...]
    pallas_call x2 -> x3, Pallas kernels: 3.23 us -> 4.56 us  [respond(): pl.pallas_call(functools.partial(respond_kernel, len(groups), halves), ou...]
    unnamed x14 -> x12, local copies, waits for them, and re-layouts: 3.91 us -> 2.87 us
  transfers between devices with their start and end apart: 14 -> 14, of which waited for: 4 -> 7; matrix products, arithmetic and copies ran while one was open for 0% -> 0% of each run, Pallas kernels for 9% -> 9%
where the time goes in v3:
time: 53.4 us; the launch traced here: 53.2 us
  starting transfers between devices  25.3 us (47%)
  waiting for transfers between devices  16.7 us (31%)
  Pallas kernels  7.1 us (13%)
  local copies, waits for them, and re-layouts  3.93 us (7%)
    ppermute x5, starting transfers between devices, facing(): lax.ppermute(block, 'dom', [(s, t) for s, t in route if 0 <= t < doms])  16.6 us
    ppermute x9, waiting for transfers between devices, ring(): lax.ppermute(block, 'ang', [(i, (i + distance) % size) for i in range(siz...  12 us
    ppermute x9, starting transfers between devices, ring(): lax.ppermute(block, 'ang', [(i, (i + distance) % size) for i in range(siz...  8.7 us
    ppermute x5, waiting for transfers between devices, facing(): lax.ppermute(block, 'dom', [(s, t) for s, t in route if 0 <= t < doms])  4.69 us
    pallas_call x3, Pallas kernels, respond(): pl.pallas_call(functools.partial(respond_kernel, len(groups), halves), ou...  4.56 us
    unnamed x12, local copies, waits for them, and re-layouts  2.87 us
    pallas_call x1, Pallas kernels, couple(): pl.pallas_call(couple_kernel, out_shape=jax.ShapeDtypeStruct((2, rows //...  2.44 us
  transfers between devices with their start and end apart: 14, of which 7 were waited for; matrix products, arithmetic and copies ran while one was open for 0% of the time, Pallas kernels for 9%

profile of v3, /device:TPU:7, one launch (start us, length us, event | category | flops | bytes accessed | tf_op | source)
XLA Modules:
  0.0 53.2 jit_solution(3557667860929373860)
XLA Ops:
  0.0 1.1 %fusion = (bf16[8,2,16,512]{3,2,1,0:T(8,128)(2,1)S(1)}, bf16[8,2,16,512]{3,2,1,0:T(8,128)(2,1)S(1)}) fusion(bf16[16,2,16,512]{3,2,1,0:T(8,128)(2,1)} %param.6), kind=kLoop, calls=%fused_computation | loop fusion | bytes 1048576 | tf_op jit(solution)/shard_map/slice | solution.py:226
  1.1 2.8 %collective-permute-start.3 = (bf16[8,2,16,512]{3,2,1,0:T(8,128)(2,1)S(1)}, bf16[8,2,16,512]{3,2,1,0:T(8,128)(2,1)S(1)}, u32[]{:S(2)}, u32[]{:S(2)}) collective-permute-start(bf16[8,2,16,512]{3,2,1,0:T(8,128)(2,1)S(1)} %get-tuple-element.13.refs_3_), channel_id=1, source_target_pairs={{0,3},{1,0},{2,1},{3,2},{4,7},{5,4},{6,5},{7,6},{8,11},{9,8},{10,9... | collective-permute-start | bytes 786440 | tf_op jit(solution)/shard_map/ppermute | solution.py:19
  3.9 0.0 collective-permute-start
  3.9 0.0 collective-permute-start.1
  3.9 2.7 %collective-permute-start.2 = (bf16[8,2,16,512]{3,2,1,0:T(8,128)(2,1)S(1)}, bf16[8,2,16,512]{3,2,1,0:T(8,128)(2,1)S(1)}, u32[]{:S(2)}, u32[]{:S(2)}) collective-permute-start(bf16[8,2,16,512]{3,2,1,0:T(8,128)(2,1)S(1)} %get-tuple-element.14.refs_2_), channel_id=1, source_target_pairs={{0,3},{1,0},{2,1},{3,2},{4,7},{5,4},{6,5},{7,6},{8,11},{9,8},{10,9... | collective-permute-start | bytes 786440 | tf_op jit(solution)/shard_map/ppermute | solution.py:19
  6.6 0.0 copy-start
  6.6 2.2 %copy-done = bf16[16,2,512,128]{3,2,1,0:T(8,128)(2,1)S(1)} copy-done((bf16[16,2,512,128]{3,2,1,0:T(8,128)(2,1)S(1)}, bf16[16,2,512,128]{3,2,1,0:T(8,128)(2,1)}, u32[]{:S(2)}) %copy-start) | copy-done | bytes 4194328
  8.8 0.0 copy-start.1
  8.8 0.7 %copy-done.1 = s32[16]{0:T(128)S(1)} copy-done((s32[16]{0:T(128)S(1)}, s32[16]{0:T(128)}, u32[]{:S(2)}) %copy-start.1) | copy-done | bytes 88
  9.4 1.3 %respond.3.after_ref.refs_0_ = f32[9,32,128]{2,1,0:T(8,128)S(1)} custom-call(s32[16]{0:T(128)S(1)} %copy-done.1, bf16[16,2,512,128]{3,2,1,0:T(8,128)(2,1)S(1)} %copy-done, bf16[8,2,16,512]{3,2,1,0:T(8,128)(2,1)S(1)} %get-tuple-element.14.refs_2_, bf16[8,2,16,512]{3,2,1,0:T(8,128)(2,1)S(1)} %get-tuple-element.13.refs_3_), custom_call_target="tpu_custom_call" | custom-call | flops 134217728 | bytes 4194304 | tf_op jit(solution)/shard_map/respond/pallas_call | solution.py:81
  10.8 0.0 slice-start
  10.8 0.0 copy-start.2
  10.8 0.0 copy-start.3
  10.8 0.0 collective-permute-done.3.held_ref
  10.8 1.5 %collective-permute-start.6 = (bf16[8,2,16,512]{3,2,1,0:T(8,128)(2,1)S(1)}, bf16[8,2,16,512]{3,2,1,0:T(8,128)(2,1)S(1)}, u32[]{:S(2)}, u32[]{:S(2)}) collective-permute-start(bf16[8,2,16,512]{3,2,1,0:T(8,128)(2,1)S(1)} %gate.3.refs_5_), channel_id=1, source_target_pairs={{0,3},{1,0},{2,1},{3,2},{4,7},{5,4},{6,5},{7,6},{8,11},{9,8},{10,9... | collective-permute-start | bytes 786440 | tf_op jit(solution)/shard_map/ppermute | solution.py:19
  12.3 0.0 collective-permute-done.held_ref
  12.3 0.0 slice-start.1
  12.3 0.0 collective-permute-start.5
  12.4 5.2 %collective-permute-done.1.refs_3_ = bf16[8,2,16,512]{3,2,1,0:T(8,128)(2,1)S(1)} collective-permute-done((bf16[8,2,16,512]{3,2,1,0:T(8,128)(2,1)S(1)}, bf16[8,2,16,512]{3,2,1,0:T(8,128)(2,1)S(1)}, u32[]{:S(2)}, u32[]{:S(2)}) %collective-permute-start.1) | collective-permute-done | bytes 262176 | tf_op jit(solution)/shard_map/ppermute | solution.py:19
  17.6 0.0 collective-permute-done.2.refs_4_
  17.6 1.9 %respond.4 = (bf16[9,32,128]{2,1,0:T(8,128)(2,1)S(1)}, bf16[9,32,128]{2,1,0:T(8,128)(2,1)S(1)}) custom-call(s32[16]{0:T(128)S(1)} %copy-done.1, bf16[16,2,512,128]{3,2,1,0:T(8,128)(2,1)S(1)} %copy-done, bf16[8,2,16,512]{3,2,1,0:T(8,128)(2,1)S(1)} %gate.2.refs_2_, bf16[8,2,16,512]{3,2,1,0:T(8,128)(2,1)S(1)} %collective-permute-done.1.refs_3_, ...), custom_call_target="tpu_custom_call" | custom-call | flops 268435456 | bytes 4194304 | tf_op jit(solution)/shard_map/respond/pallas_call | solution.py:81
  19.5 0.4 collective-permute-start.4
  19.9 1.2 %collective-permute-start.8 = (bf16[9,32,128]{2,1,0:T(8,128)(2,1)S(1)}, bf16[9,32,128]{2,1,0:T(8,128)(2,1)S(1)}, u32[]{:S(2)}, u32[]{:S(2)}) collective-permute-start(bf16[9,32,128]{2,1,0:T(8,128)(2,1)S(1)} %get-tuple-element.10), channel_id=1, source_target_pairs={{0,1},{1,2},{2,3},{3,0},{4,5},{5,6},{6,7},{7,4},{8,9},{9,10},{10,1... | collective-permute-start | bytes 221192 | tf_op jit(solution)/shard_map/ppermute | solution.py:19
  21.0 0.0 collective-permute-done.6.refs_3_
  21.0 2.2 %collective-permute-done.5.refs_2_ = bf16[8,2,16,512]{3,2,1,0:T(8,128)(2,1)S(1)} collective-permute-done((bf16[8,2,16,512]{3,2,1,0:T(8,128)(2,1)S(1)}, bf16[8,2,16,512]{3,2,1,0:T(8,128)(2,1)S(1)}, u32[]{:S(2)}, u32[]{:S(2)}) %collective-permute-start.5) | collective-permute-done | bytes 262176 | tf_op jit(solution)/shard_map/ppermute | solution.py:19
  23.2 1.3 %respond.5 = bf16[9,32,128]{2,1,0:T(8,128)(2,1)S(1)} custom-call(s32[16]{0:T(128)S(1)} %copy-done.1, bf16[16,2,512,128]{3,2,1,0:T(8,128)(2,1)S(1)} %copy-done, bf16[8,2,16,512]{3,2,1,0:T(8,128)(2,1)S(1)} %collective-permute-done.5.refs_2_, bf16[8,2,16,512]{3,2,1,0:T(8,128)(2,1)S(1)} %collective-permute-done.6.refs_3_), custom_call_target="tpu_custom_call" | custom-call | flops 134217728 | bytes 4194304 | tf_op jit(solution)/shard_map/respond/pallas_call | solution.py:81
  24.5 0.1 collective-permute-start.7
  24.6 0.0 collective-permute-done.4.refs_1_
  24.6 0.8 %collective-permute-done.8.refs_3_ = bf16[9,32,128]{2,1,0:T(8,128)(2,1)S(1)} collective-permute-done((bf16[9,32,128]{2,1,0:T(8,128)(2,1)S(1)}, bf16[9,32,128]{2,1,0:T(8,128)(2,1)S(1)}, u32[]{:S(2)}, u32[]{:S(2)}) %collective-permute-start.8) | collective-permute-done | bytes 73760 | tf_op jit(solution)/shard_map/ppermute | solution.py:19
  25.4 3.9 %collective-permute-done.7.refs_2_ = bf16[9,32,128]{2,1,0:T(8,128)(2,1)S(1)} collective-permute-done((bf16[9,32,128]{2,1,0:T(8,128)(2,1)S(1)}, bf16[9,32,128]{2,1,0:T(8,128)(2,1)S(1)}, u32[]{:S(2)}, u32[]{:S(2)}) %collective-permute-start.7) | collective-permute-done | bytes 73760 | tf_op jit(solution)/shard_map/ppermute | solution.py:19
  29.3 0.1 stitch.1.mine_ref
  29.4 3.9 %collective-permute-start.9 = (f32[12,32,128]{2,1,0:T(8,128)S(1)}, f32[12,32,128]{2,1,0:T(8,128)S(1)}, u32[]{:S(2)}, u32[]{:S(2)}) collective-permute-start(f32[12,32,128]{2,1,0:T(8,128)S(1)} %stitch.1.mine_ref), channel_id=1, source_target_pairs={{0,4},{4,0},{8,12},{12,8},{16,20},{20,16},{24,28},{28,24},{32,36},... | collective-permute-start | bytes 589832 | tf_op jit(solution)/shard_map/ppermute | solution.py:25
  33.3 1.1 %collective-permute-done.9.other_ref = f32[12,32,128]{2,1,0:T(8,128)S(1)} collective-permute-done((f32[12,32,128]{2,1,0:T(8,128)S(1)}, f32[12,32,128]{2,1,0:T(8,128)S(1)}, u32[]{:S(2)}, u32[]{:S(2)}) %collective-permute-start.9) | collective-permute-done | bytes 196640 | tf_op jit(solution)/shard_map/ppermute | solution.py:25
  34.4 7.7 %collective-permute-start.10 = (bf16[20,32,128]{2,1,0:T(8,128)(2,1)S(1)}, bf16[20,32,128]{2,1,0:T(8,128)(2,1)S(1)}, u32[]{:S(2)}, u32[]{:S(2)}) collective-permute-start(bf16[20,32,128]{2,1,0:T(8,128)(2,1)S(1)} %get-tuple-element.11.chip_ref), channel_id=1, source_target_pairs={{0,8},{8,16},{12,4},{16,24},{20,12},{24,32},{28,20},{32,40},{36,28... | collective-permute-start | bytes 491528 | tf_op jit(solution)/shard_map/ppermute | solution.py:25
  42.1 3.1 %collective-permute-start.11 = (bf16[12,32,128]{2,1,0:T(8,128)(2,1)S(1)}, bf16[12,32,128]{2,1,0:T(8,128)(2,1)S(1)}, u32[]{:S(2)}, u32[]{:S(2)}) collective-permute-start(bf16[12,32,128]{2,1,0:T(8,128)(2,1)S(1)} %get-tuple-element.12), channel_id=1, source_target_pairs={{0,16},{8,24},{16,32},{20,4},{24,40},{28,12},{32,48},{36,20},{40,5... | collective-permute-start | bytes 294920 | tf_op jit(solution)/shard_map/ppermute | solution.py:25
  45.2 0.0 collective-permute-done.10.near_ref
  45.2 0.8 %collective-permute-start.12 = (bf16[20,32,128]{2,1,0:T(8,128)(2,1)S(1)}, bf16[20,32,128]{2,1,0:T(8,128)(2,1)S(1)}, u32[]{:S(2)}, u32[]{:S(2)}) collective-permute-start(bf16[20,32,128]{2,1,0:T(8,128)(2,1)S(1)} %collective-permute-done.10.near_ref), channel_id=1, source_target_pairs={{0,4},{4,0},{8,12},{12,8},{16,20},{20,16},{24,28},{28,24},{32,36},... | collective-permute-start | bytes 491528 | tf_op jit(solution)/shard_map/ppermute | solution.py:25
  46.1 2.7 %collective-permute-done.11.far_ref = bf16[12,32,128]{2,1,0:T(8,128)(2,1)S(1)} collective-permute-done((bf16[12,32,128]{2,1,0:T(8,128)(2,1)S(1)}, bf16[12,32,128]{2,1,0:T(8,128)(2,1)S(1)}, u32[]{:S(2)}, u32[]{:S(2)}) %collective-permute-start.11) | collective-permute-done | bytes 98336 | tf_op jit(solution)/shard_map/ppermute | solution.py:25
  48.7 1.1 %collective-permute-start.13 = (bf16[12,32,128]{2,1,0:T(8,128)(2,1)S(1)}, bf16[12,32,128]{2,1,0:T(8,128)(2,1)S(1)}, u32[]{:S(2)}, u32[]{:S(2)}) collective-permute-start(bf16[12,32,128]{2,1,0:T(8,128)(2,1)S(1)} %collective-permute-done.11.far_ref), channel_id=1, source_target_pairs={{0,4},{4,0},{8,12},{12,8},{16,20},{20,16},{24,28},{28,24},{32,36},... | collective-permute-start | bytes 294920 | tf_op jit(solution)/shard_map/ppermute | solution.py:25
  49.8 0.9 %collective-permute-done.13.swap_far_ref = bf16[12,32,128]{2,1,0:T(8,128)(2,1)S(1)} collective-permute-done((bf16[12,32,128]{2,1,0:T(8,128)(2,1)S(1)}, bf16[12,32,128]{2,1,0:T(8,128)(2,1)S(1)}, u32[]{:S(2)}, u32[]{:S(2)}) %collective-permute-start.13) | collective-permute-done | bytes 98336 | tf_op jit(solution)/shard_map/ppermute | solution.py:25
  50.7 0.0 collective-permute-done.12.swap_near_ref
  50.7 0.0 slice-done
  50.7 0.0 copy-done.2
  50.8 0.0 copy-done.3
  50.8 0.0 slice-done.1
  50.8 2.4 %couple.1 = f32[2,16,1024]{2,1,0:T(8,128)} custom-call(s32[8,12]{1,0:T(8,128)S(1)} %copy-done.2, s32[8]{0:T(128)S(1)} %copy-done.3, bf16[8,12,2,128,128]{4,3,2,1,0:T(8,128)(2,1)S(1)} %bitcast.1, bf16[20,32,128]{2,1,0:T(8,128)(2,1)S(1)} %get-tuple-element.11.chip_ref, bf16[20,32,128]{2,1,0:T(8,128)(2,1)S(1)} %collective-permute-done.10.near_ref, ...), custom_call_target="tpu_custom_call" | custom-call | flops 201326592 | bytes 6291456 | tf_op jit(solution)/shard_map/couple/pallas_call | solution.py:212
  (4 shorter events, 0.0 us)
Async XLA Ops:
  1.1 9.7 %collective-permute-start.3 = (bf16[8,2,16,512]{3,2,1,0:T(8,128)(2,1)S(1)}, bf16[8,2,16,512]{3,2,1,0:T(8,128)(2,1)S(1)}, u32[]{:S(2)}, u32[]{:S(2)}) collective-permute-start(bf16[8,2,16,512]{3,2,1,0:T(8,128)(2,1)S(1)} %get-tuple-element.13.refs_3_), channel_id=1, source_target_pairs={{0,3},{1,0},{2,1},{3,2},{4,7},{5,4},{6,5},{7,6},{8,11},{9,8},{10,9... | collective-permute-start | bytes 786440 | tf_op jit(solution)/shard_map/ppermute | solution.py:19
  3.9 8.5 %collective-permute-start = (bf16[8,2,16,512]{3,2,1,0:T(8,128)(2,1)S(1)}, bf16[8,2,16,512]{3,2,1,0:T(8,128)(2,1)S(1)}, u32[]{:S(2)}, u32[]{:S(2)}) collective-permute-start(bf16[8,2,16,512]{3,2,1,0:T(8,128)(2,1)S(1)} %get-tuple-element.14.refs_2_), channel_id=1, source_target_pairs={{0,1},{1,2},{2,3},{3,0},{4,5},{5,6},{6,7},{7,4},{8,9},{9,10},{10,1... | collective-permute-start | bytes 786440 | tf_op jit(solution)/shard_map/ppermute | solution.py:19
  3.9 13.7 %collective-permute-start.1 = (bf16[8,2,16,512]{3,2,1,0:T(8,128)(2,1)S(1)}, bf16[8,2,16,512]{3,2,1,0:T(8,128)(2,1)S(1)}, u32[]{:S(2)}, u32[]{:S(2)}) collective-permute-start(bf16[8,2,16,512]{3,2,1,0:T(8,128)(2,1)S(1)} %get-tuple-element.13.refs_3_), channel_id=1, source_target_pairs={{0,1},{1,2},{2,3},{3,0},{4,5},{5,6},{6,7},{7,4},{8,9},{9,10},{10,1... | collective-permute-start | bytes 786440 | tf_op jit(solution)/shard_map/ppermute | solution.py:19
  3.9 13.7 %collective-permute-start.2 = (bf16[8,2,16,512]{3,2,1,0:T(8,128)(2,1)S(1)}, bf16[8,2,16,512]{3,2,1,0:T(8,128)(2,1)S(1)}, u32[]{:S(2)}, u32[]{:S(2)}) collective-permute-start(bf16[8,2,16,512]{3,2,1,0:T(8,128)(2,1)S(1)} %get-tuple-element.14.refs_2_), channel_id=1, source_target_pairs={{0,3},{1,0},{2,1},{3,2},{4,7},{5,4},{6,5},{7,6},{8,11},{9,8},{10,9... | collective-permute-start | bytes 786440 | tf_op jit(solution)/shard_map/ppermute | solution.py:19
  6.6 2.2 %copy-start = (bf16[16,2,512,128]{3,2,1,0:T(8,128)(2,1)S(1)}, bf16[16,2,512,128]{3,2,1,0:T(8,128)(2,1)}, u32[]{:S(2)}) copy-start(bf16[16,2,512,128]{3,2,1,0:T(8,128)(2,1)} %refs_1_.5) | copy-start | bytes 12582916
  8.8 0.7 %copy-start.1 = (s32[16]{0:T(128)S(1)}, s32[16]{0:T(128)}, u32[]{:S(2)}) copy-start(s32[16]{0:T(128)} %refs_0_.5) | copy-start | bytes 196
  10.8 40.0 %slice-start = ((s8[6291456]{0:T(1024)(128)(4,1)}), s8[4194304]{0:T(1024)(128)(4,1)S(1)}, s32[]{:S(2)}) async-start(s8[6291456]{0:T(1024)(128)(4,1)} %bitcast), calls=%async_computation | async-start | bytes 8388608
  10.8 40.0 %copy-start.2 = (s32[8,12]{1,0:T(8,128)S(1)}, s32[8,12]{1,0:T(8,128)}, u32[]{:S(2)}) copy-start(s32[8,12]{1,0:T(8,128)} %cols_ref.1) | copy-start | bytes 1156
  10.8 40.0 %copy-start.3 = (s32[8]{0:T(128)S(1)}, s32[8]{0:T(128)}, u32[]{:S(2)}) copy-start(s32[8]{0:T(128)} %counts_ref.1) | copy-start | bytes 100
  10.8 10.2 %collective-permute-start.6 = (bf16[8,2,16,512]{3,2,1,0:T(8,128)(2,1)S(1)}, bf16[8,2,16,512]{3,2,1,0:T(8,128)(2,1)S(1)}, u32[]{:S(2)}, u32[]{:S(2)}) collective-permute-start(bf16[8,2,16,512]{3,2,1,0:T(8,128)(2,1)S(1)} %gate.3.refs_5_), channel_id=1, source_target_pairs={{0,3},{1,0},{2,1},{3,2},{4,7},{5,4},{6,5},{7,6},{8,11},{9,8},{10,9... | collective-permute-start | bytes 786440 | tf_op jit(solution)/shard_map/ppermute | solution.py:19
  12.3 38.4 %slice-start.1 = ((s8[6291456]{0:T(1024)(128)(4,1)}), s8[2097152]{0:T(1024)(128)(4,1)S(1)}, s32[]{:S(2)}) async-start(s8[6291456]{0:T(1024)(128)(4,1)} %bitcast), calls=%async_computation.1 | async-start | bytes 4194304
  12.3 10.8 %collective-permute-start.5 = (bf16[8,2,16,512]{3,2,1,0:T(8,128)(2,1)S(1)}, bf16[8,2,16,512]{3,2,1,0:T(8,128)(2,1)S(1)}, u32[]{:S(2)}, u32[]{:S(2)}) collective-permute-start(bf16[8,2,16,512]{3,2,1,0:T(8,128)(2,1)S(1)} %gate.2.refs_2_), channel_id=1, source_target_pairs={{0,1},{1,2},{2,3},{3,0},{4,5},{5,6},{6,7},{7,4},{8,9},{9,10},{10,1... | collective-permute-start | bytes 786440 | tf_op jit(solution)/shard_map/ppermute | solution.py:19
  19.5 5.1 %collective-permute-start.4 = (bf16[9,32,128]{2,1,0:T(8,128)(2,1)S(1)}, bf16[9,32,128]{2,1,0:T(8,128)(2,1)S(1)}, u32[]{:S(2)}, u32[]{:S(2)}) collective-permute-start(bf16[9,32,128]{2,1,0:T(8,128)(2,1)S(1)} %get-tuple-element.9), channel_id=1, source_target_pairs={{0,3},{1,0},{2,1},{3,2},{4,7},{5,4},{6,5},{7,6},{8,11},{9,8},{10,9... | collective-permute-start | bytes 221192 | tf_op jit(solution)/shard_map/ppermute | solution.py:19
  19.9 5.6 %collective-permute-start.8 = (bf16[9,32,128]{2,1,0:T(8,128)(2,1)S(1)}, bf16[9,32,128]{2,1,0:T(8,128)(2,1)S(1)}, u32[]{:S(2)}, u32[]{:S(2)}) collective-permute-start(bf16[9,32,128]{2,1,0:T(8,128)(2,1)S(1)} %get-tuple-element.10), channel_id=1, source_target_pairs={{0,1},{1,2},{2,3},{3,0},{4,5},{5,6},{6,7},{7,4},{8,9},{9,10},{10,1... | collective-permute-start | bytes 221192 | tf_op jit(solution)/shard_map/ppermute | solution.py:19
  24.5 4.8 %collective-permute-start.7 = (bf16[9,32,128]{2,1,0:T(8,128)(2,1)S(1)}, bf16[9,32,128]{2,1,0:T(8,128)(2,1)S(1)}, u32[]{:S(2)}, u32[]{:S(2)}) collective-permute-start(bf16[9,32,128]{2,1,0:T(8,128)(2,1)S(1)} %respond.5), channel_id=1, source_target_pairs={{0,2},{1,3},{2,0},{3,1},{4,6},{5,7},{6,4},{7,5},{8,10},{9,11},{10,... | collective-permute-start | bytes 221192 | tf_op jit(solution)/shard_map/ppermute | solution.py:19
  29.4 5.0 %collective-permute-start.9 = (f32[12,32,128]{2,1,0:T(8,128)S(1)}, f32[12,32,128]{2,1,0:T(8,128)S(1)}, u32[]{:S(2)}, u32[]{:S(2)}) collective-permute-start(f32[12,32,128]{2,1,0:T(8,128)S(1)} %stitch.1.mine_ref), channel_id=1, source_target_pairs={{0,4},{4,0},{8,12},{12,8},{16,20},{20,16},{24,28},{28,24},{32,36},... | collective-permute-start | bytes 589832 | tf_op jit(solution)/shard_map/ppermute | solution.py:25
  34.4 10.8 %collective-permute-start.10 = (bf16[20,32,128]{2,1,0:T(8,128)(2,1)S(1)}, bf16[20,32,128]{2,1,0:T(8,128)(2,1)S(1)}, u32[]{:S(2)}, u32[]{:S(2)}) collective-permute-start(bf16[20,32,128]{2,1,0:T(8,128)(2,1)S(1)} %get-tuple-element.11.chip_ref), channel_id=1, source_target_pairs={{0,8},{8,16},{12,4},{16,24},{20,12},{24,32},{28,20},{32,40},{36,28... | collective-permute-start | bytes 491528 | tf_op jit(solution)/shard_map/ppermute | solution.py:25
  42.1 6.6 %collective-permute-start.11 = (bf16[12,32,128]{2,1,0:T(8,128)(2,1)S(1)}, bf16[12,32,128]{2,1,0:T(8,128)(2,1)S(1)}, u32[]{:S(2)}, u32[]{:S(2)}) collective-permute-start(bf16[12,32,128]{2,1,0:T(8,128)(2,1)S(1)} %get-tuple-element.12), channel_id=1, source_target_pairs={{0,16},{8,24},{16,32},{20,4},{24,40},{28,12},{32,48},{36,20},{40,5... | collective-permute-start | bytes 294920 | tf_op jit(solution)/shard_map/ppermute | solution.py:25
  45.2 5.5 %collective-permute-start.12 = (bf16[20,32,128]{2,1,0:T(8,128)(2,1)S(1)}, bf16[20,32,128]{2,1,0:T(8,128)(2,1)S(1)}, u32[]{:S(2)}, u32[]{:S(2)}) collective-permute-start(bf16[20,32,128]{2,1,0:T(8,128)(2,1)S(1)} %collective-permute-done.10.near_ref), channel_id=1, source_target_pairs={{0,4},{4,0},{8,12},{12,8},{16,20},{20,16},{24,28},{28,24},{32,36},... | collective-permute-start | bytes 491528 | tf_op jit(solution)/shard_map/ppermute | solution.py:25
  48.7 2.0 %collective-permute-start.13 = (bf16[12,32,128]{2,1,0:T(8,128)(2,1)S(1)}, bf16[12,32,128]{2,1,0:T(8,128)(2,1)S(1)}, u32[]{:S(2)}, u32[]{:S(2)}) collective-permute-start(bf16[12,32,128]{2,1,0:T(8,128)(2,1)S(1)} %collective-permute-done.11.far_ref), channel_id=1, source_target_pairs={{0,4},{4,0},{8,12},{12,8},{16,20},{20,16},{24,28},{28,24},{32,36},... | collective-permute-start | bytes 294920 | tf_op jit(solution)/shard_map/ppermute | solution.py:25

commit v4 on v3

--- a/solution.py
+++ b/solution.py
@@ -14,15 +14,32 @@
 SMEM = pl.BlockSpec(memory_space=pltpu.SMEM)
 
 
-def ring(block, distance):
+def angle_pairs(block, shift):
     size = lax.axis_size("ang")
-    return lax.ppermute(block, "ang", [(i, (i + distance) % size) for i in range(size)])
-
-
-def facing(block, even_step):
+    if shift == 2:
+        return lax.ppermute(block, "ang", [(a, (a + 2) % size) for a in range(size)])
+    return lax.ppermute(block, "ang", [(a, (((a + shift) ^ 1) - shift) % size) for a in range(size)])
+
+
+def other_core(block):
     doms = lax.axis_size("dom")
-    route = [(i, i + (even_step if i % 2 == 0 else -even_step)) for i in range(doms)]
-    return lax.ppermute(block, "dom", [(s, t) for s, t in route if 0 <= t < doms])
+    return lax.ppermute(block, "dom", [(i, i ^ 1) for i in range(doms)])
+
+
+def pairs(block, distance):
+    chips = lax.axis_size("dom") // 2
+    route = []
+    for i in range(2 * chips):
+        chip, core = i // 2, i % 2
+        partner = chip ^ distance if core == distance - 1 else ((chip + distance) ^ distance) - distance
+        if 0 <= partner < chips:
+            route.append((i, 2 * partner + core))
+    return lax.ppermute(block, "dom", route)
+
+
+def ahead(distance):
+    me = lax.axis_index("dom")
+    return lax.rem(me + distance - 1, 2) == lax.rem(me // (2 * distance), 2)
 
 
 def placed_sums(jitter_ref, pieces, response_ref):
@@ -95,8 +112,8 @@
     sources, plane = refs[:4], refs[4]
     me = lax.axis_index("ang")
     plane[...] = jnp.zeros_like(plane)
-    for step in range(4):
-        owner = lax.rem(me + step, 4)
+    side = jnp.where(lax.rem(me, 2) == 0, 1, 3)
+    for step, owner in enumerate((me, lax.rem(me + side, 4), lax.rem(me + 4 - side, 4), lax.rem(me + 2, 4))):
         plane[pl.ds(owner, sources[step].shape[0])] += sources[step][...].astype(jnp.float32)
 
 
@@ -116,21 +133,22 @@
     odd = lax.rem(lax.axis_index("dom"), 2) == 1
     blocks = mine_ref.shape[0] - HALO
 
-    def fill(even_ref, odd_ref, first):
+    def fill(even_ref, odd_ref):
         chip_ref[pl.ds(0, blocks)] = even_ref[pl.ds(0, blocks)].astype(chip_ref.dtype)
         joined = odd_ref[pl.ds(0, HALO)] + even_ref[pl.ds(blocks, HALO)]
         chip_ref[pl.ds(blocks, HALO)] = joined.astype(chip_ref.dtype)
         rest = odd_ref[pl.ds(HALO, blocks)]
         chip_ref[pl.ds(blocks + HALO, blocks)] = rest.astype(chip_ref.dtype)
-        far_ref[...] = chip_ref[pl.ds(first, blocks + HALO)]
 
     @pl.when(odd)
     def _():
-        fill(other_ref, mine_ref, 0)
+        fill(other_ref, mine_ref)
 
     @pl.when(jnp.logical_not(odd))
     def _():
-        fill(mine_ref, other_ref, blocks)
+        fill(mine_ref, other_ref)
+
+    far_ref[...] = chip_ref[pl.ds(jnp.where(ahead(2), blocks, 0), blocks + HALO)]
 
 
 def pack(mine, other):
@@ -155,7 +173,6 @@
     angles = rows // 2
     entries = green_ref.shape[1]
     me = lax.axis_index("dom")
-    odd = lax.rem(me, 2) == 1
 
     def put(slot, ref, first, halo_ref=None, halo_first=None):
         at = slot * blocks
@@ -167,23 +184,22 @@
         window[pl.ds(at, HALO)] = (low + halo).astype(window.dtype)
         window[pl.ds(at + HALO, blocks - HALO)] = ref[pl.ds(first + HALO, blocks - HALO)]
 
-    def fill(left_ref, right_ref, left_far_ref):
+    def fill(left_ref, right_ref, left_far_ref, right_far_ref):
+        put(0, left_far_ref, 0)
         put(1, left_ref, 0, left_far_ref, blocks)
         put(2, left_ref, blocks)
         put(3, chip_ref, 0, left_ref, 2 * blocks)
         put(4, chip_ref, blocks)
         put(5, right_ref, 0, chip_ref, 2 * blocks)
         put(6, right_ref, blocks)
-
-    @pl.when(odd)
-    def _():
-        fill(swap_near_ref, near_ref, swap_far_ref)
-        put(7, far_ref, 0, near_ref, 2 * blocks)
-
-    @pl.when(jnp.logical_not(odd))
-    def _():
-        fill(near_ref, swap_near_ref, far_ref)
-        put(0, far_ref, 0)
+        put(7, right_far_ref, 0, right_ref, 2 * blocks)
+
+    for near_ahead, sides in ((True, (swap_near_ref, near_ref)), (False, (near_ref, swap_near_ref))):
+        for far_ahead, far_sides in ((True, (swap_far_ref, far_ref)), (False, (far_ref, swap_far_ref))):
+
+            @pl.when(jnp.logical_and(ahead(1) == near_ahead, ahead(2) == far_ahead))
+            def _(sides=sides, far_sides=far_sides):
+                fill(*sides, *far_sides)
 
     dead = 8 * blocks
     window[dead] = jnp.zeros((rows, lanes), window.dtype)
@@ -224,20 +240,20 @@
 def per_device(incident, response, jitter, block_cols, block_counts, green_blocks):
     half = incident.shape[0] // 2
     low, high = incident[:half], incident[half:]
-    before_low, after_high = ring(low, 1), ring(high, -1)
-    before_high, after_low = ring(high, 1), ring(low, -1)
+    one_low, two_high = angle_pairs(low, 0), angle_pairs(high, 1)
+    one_high, two_low = angle_pairs(high, 0), angle_pairs(low, 1)
     (own,) = respond(jitter, response, [(low, high)], jnp.float32)
-    before_low, after_high = gate(before_low, own), gate(after_high, own)
-    across_low, across_high = ring(before_low, 1), ring(after_high, -1)
-
-    before, after = respond(jitter, response, [(before_low, before_high), (after_low, after_high)])
+    one_low, two_high = gate(one_low, own), gate(two_high, own)
+    across_low, across_high = angle_pairs(one_low, 1), angle_pairs(two_high, 0)
+
+    one, two = respond(jitter, response, [(one_low, one_high), (two_low, two_high)])
     (across,) = respond(jitter, response, [(across_low, across_high)])
-    mine = stitch([own, ring(before, -1), ring(across, 2), ring(after, 1)])
-
-    chip, far = pack(mine, facing(mine, 1))
-    far_in, near_in = facing(far, 4), facing(chip, 2)
+    mine = stitch([own, angle_pairs(one, 0), angle_pairs(two, 1), angle_pairs(across, 2)])
+
+    chip, far = pack(mine, other_core(mine))
+    near_in, far_in = pairs(chip, 1), pairs(far, 2)
     return couple(
-        block_cols, block_counts, green_blocks, chip, near_in, far_in, facing(near_in, 1), facing(far_in, 1)
+        block_cols, block_counts, green_blocks, chip, near_in, far_in, other_core(near_in), other_core(far_in)
     )
 
 

time: 53.4 us -> 52.2 us (0.978)
  starting transfers between devices: 25.3 us -> 24.4 us
    ppermute x14, starting transfers between devices: 25.3 us -> 24.4 us  [the longest x2 9.67 us: pairs(): return lax.ppermute(block, 'dom', route)]
  transfers between devices with their start and end apart: 14 -> 14, of which waited for: 7 -> 8; matrix products, arithmetic and copies ran while one was open for 0% -> 0% of each run, Pallas kernels for 9% -> 9%
where the time goes in v4:
time: 52.2 us; the launch traced here: 52.1 us
  starting transfers between devices  24.4 us (47%)
  waiting for transfers between devices  16.5 us (32%)
  Pallas kernels  7.13 us (14%)
  local copies, waits for them, and re-layouts  3.93 us (8%)
    ppermute x2, starting transfers between devices, pairs(): return lax.ppermute(block, 'dom', route)  9.67 us
    ppermute x8, starting transfers between devices, angle_pairs(): lax.ppermute(block, 'ang', [(a, ((a + shift ^ 1) - shift) % size) for a i...  7.93 us
    ppermute x8, waiting for transfers between devices, angle_pairs(): lax.ppermute(block, 'ang', [(a, ((a + shift ^ 1) - shift) % size) for a i...  6.85 us
    ppermute x3, starting transfers between devices, other_core(): return lax.ppermute(block, 'dom', [(i, i ^ 1) for i in range(doms)])  6.38 us
    pallas_call x3, Pallas kernels, respond(): pl.pallas_call(functools.partial(respond_kernel, len(groups), halves), ou...  4.56 us
    ppermute x1, waiting for transfers between devices, angle_pairs(): lax.ppermute(block, 'ang', [(a, (a + 2) % size) for a in range(size)])  4.35 us
    ppermute x2, waiting for transfers between devices, pairs(): return lax.ppermute(block, 'dom', route)  3.24 us
    unnamed x12, local copies, waits for them, and re-layouts  2.87 us
  transfers between devices with their start and end apart: 14, of which 8 were waited for; matrix products, arithmetic and copies ran while one was open for 0% of the time, Pallas kernels for 9%

profile of v4, /device:TPU:7, one launch (start us, length us, event | category | flops | bytes accessed | tf_op | source)
XLA Modules:
  0.0 52.1 jit_solution(15298663410907882)
XLA Ops:
  0.0 1.1 %fusion = (bf16[8,2,16,512]{3,2,1,0:T(8,128)(2,1)S(1)}, bf16[8,2,16,512]{3,2,1,0:T(8,128)(2,1)S(1)}) fusion(bf16[16,2,16,512]{3,2,1,0:T(8,128)(2,1)} %param.6), kind=kLoop, calls=%fused_computation | loop fusion | bytes 1048576 | tf_op jit(solution)/shard_map/slice | solution.py:242
  1.1 2.8 %collective-permute-start.3 = (bf16[8,2,16,512]{3,2,1,0:T(8,128)(2,1)S(1)}, bf16[8,2,16,512]{3,2,1,0:T(8,128)(2,1)S(1)}, u32[]{:S(2)}, u32[]{:S(2)}) collective-permute-start(bf16[8,2,16,512]{3,2,1,0:T(8,128)(2,1)S(1)} %get-tuple-element.13.refs_3_), channel_id=1, source_target_pairs={{0,3},{1,2},{2,1},{3,0},{4,7},{5,6},{6,5},{7,4},{8,11},{9,10},{10,... | collective-permute-start | bytes 786440 | tf_op jit(solution)/shard_map/ppermute | solution.py:21
  3.9 0.0 collective-permute-start
  3.9 1.5 %collective-permute-start.1 = (bf16[8,2,16,512]{3,2,1,0:T(8,128)(2,1)S(1)}, bf16[8,2,16,512]{3,2,1,0:T(8,128)(2,1)S(1)}, u32[]{:S(2)}, u32[]{:S(2)}) collective-permute-start(bf16[8,2,16,512]{3,2,1,0:T(8,128)(2,1)S(1)} %get-tuple-element.13.refs_3_), channel_id=1, source_target_pairs={{0,1},{1,0},{2,3},{3,2},{4,5},{5,4},{6,7},{7,6},{8,9},{9,8},{10,11... | collective-permute-start | bytes 786440 | tf_op jit(solution)/shard_map/ppermute | solution.py:21
  5.4 0.1 collective-permute-start.2
  5.5 0.0 copy-start
  5.5 2.2 %copy-done = bf16[16,2,512,128]{3,2,1,0:T(8,128)(2,1)S(1)} copy-done((bf16[16,2,512,128]{3,2,1,0:T(8,128)(2,1)S(1)}, bf16[16,2,512,128]{3,2,1,0:T(8,128)(2,1)}, u32[]{:S(2)}) %copy-start) | copy-done | bytes 4194328
  7.6 0.0 copy-start.1
  7.6 0.7 %copy-done.1 = s32[16]{0:T(128)S(1)} copy-done((s32[16]{0:T(128)S(1)}, s32[16]{0:T(128)}, u32[]{:S(2)}) %copy-start.1) | copy-done | bytes 88
  8.3 1.3 %respond.3.after_ref.refs_0_ = f32[9,32,128]{2,1,0:T(8,128)S(1)} custom-call(s32[16]{0:T(128)S(1)} %copy-done.1, bf16[16,2,512,128]{3,2,1,0:T(8,128)(2,1)S(1)} %copy-done, bf16[8,2,16,512]{3,2,1,0:T(8,128)(2,1)S(1)} %get-tuple-element.14.refs_2_, bf16[8,2,16,512]{3,2,1,0:T(8,128)(2,1)S(1)} %get-tuple-element.13.refs_3_), custom_call_target="tpu_custom_call" | custom-call | flops 134217728 | bytes 4194304 | tf_op jit(solution)/shard_map/respond/pallas_call | solution.py:98
  9.6 0.0 slice-start
  9.6 0.0 copy-start.2
  9.7 0.0 copy-start.3
  9.7 0.0 collective-permute-done.3.held_ref
  9.7 0.1 collective-permute-start.7
  9.8 1.0 %collective-permute-done.held_ref = bf16[8,2,16,512]{3,2,1,0:T(8,128)(2,1)S(1)} collective-permute-done((bf16[8,2,16,512]{3,2,1,0:T(8,128)(2,1)S(1)}, bf16[8,2,16,512]{3,2,1,0:T(8,128)(2,1)S(1)}, u32[]{:S(2)}, u32[]{:S(2)}) %collective-permute-start) | collective-permute-done | bytes 262176 | tf_op jit(solution)/shard_map/ppermute | solution.py:21
  10.7 0.0 slice-start.1
  10.7 1.7 %collective-permute-start.6 = (bf16[8,2,16,512]{3,2,1,0:T(8,128)(2,1)S(1)}, bf16[8,2,16,512]{3,2,1,0:T(8,128)(2,1)S(1)}, u32[]{:S(2)}, u32[]{:S(2)}) collective-permute-start(bf16[8,2,16,512]{3,2,1,0:T(8,128)(2,1)S(1)} %gate.2.refs_2_), channel_id=1, source_target_pairs={{0,3},{1,2},{2,1},{3,0},{4,7},{5,6},{6,5},{7,4},{8,11},{9,10},{10,... | collective-permute-start | bytes 786440 | tf_op jit(solution)/shard_map/ppermute | solution.py:21
  12.5 3.9 %collective-permute-done.1.refs_3_ = bf16[8,2,16,512]{3,2,1,0:T(8,128)(2,1)S(1)} collective-permute-done((bf16[8,2,16,512]{3,2,1,0:T(8,128)(2,1)S(1)}, bf16[8,2,16,512]{3,2,1,0:T(8,128)(2,1)S(1)}, u32[]{:S(2)}, u32[]{:S(2)}) %collective-permute-start.1) | collective-permute-done | bytes 262176 | tf_op jit(solution)/shard_map/ppermute | solution.py:21
  16.4 0.0 collective-permute-done.2.refs_4_
  16.4 1.9 %respond.4 = (bf16[9,32,128]{2,1,0:T(8,128)(2,1)S(1)}, bf16[9,32,128]{2,1,0:T(8,128)(2,1)S(1)}) custom-call(s32[16]{0:T(128)S(1)} %copy-done.1, bf16[16,2,512,128]{3,2,1,0:T(8,128)(2,1)S(1)} %copy-done, bf16[8,2,16,512]{3,2,1,0:T(8,128)(2,1)S(1)} %gate.2.refs_2_, bf16[8,2,16,512]{3,2,1,0:T(8,128)(2,1)S(1)} %collective-permute-done.1.refs_3_, ...), custom_call_target="tpu_custom_call" | custom-call | flops 268435456 | bytes 4194304 | tf_op jit(solution)/shard_map/respond/pallas_call | solution.py:98
  18.3 0.2 collective-permute-start.4
  18.5 1.5 %collective-permute-start.5 = (bf16[9,32,128]{2,1,0:T(8,128)(2,1)S(1)}, bf16[9,32,128]{2,1,0:T(8,128)(2,1)S(1)}, u32[]{:S(2)}, u32[]{:S(2)}) collective-permute-start(bf16[9,32,128]{2,1,0:T(8,128)(2,1)S(1)} %get-tuple-element.10), channel_id=1, source_target_pairs={{0,3},{1,2},{2,1},{3,0},{4,7},{5,6},{6,5},{7,4},{8,11},{9,10},{10,... | collective-permute-start | bytes 221192 | tf_op jit(solution)/shard_map/ppermute | solution.py:21
  20.0 2.0 %collective-permute-done.7.refs_3_ = bf16[8,2,16,512]{3,2,1,0:T(8,128)(2,1)S(1)} collective-permute-done((bf16[8,2,16,512]{3,2,1,0:T(8,128)(2,1)S(1)}, bf16[8,2,16,512]{3,2,1,0:T(8,128)(2,1)S(1)}, u32[]{:S(2)}, u32[]{:S(2)}) %collective-permute-start.7) | collective-permute-done | bytes 262176 | tf_op jit(solution)/shard_map/ppermute | solution.py:21
  22.0 0.0 collective-permute-done.6.refs_2_
  22.0 1.3 %respond.5 = bf16[9,32,128]{2,1,0:T(8,128)(2,1)S(1)} custom-call(s32[16]{0:T(128)S(1)} %copy-done.1, bf16[16,2,512,128]{3,2,1,0:T(8,128)(2,1)S(1)} %copy-done, bf16[8,2,16,512]{3,2,1,0:T(8,128)(2,1)S(1)} %collective-permute-done.6.refs_2_, bf16[8,2,16,512]{3,2,1,0:T(8,128)(2,1)S(1)} %collective-permute-done.7.refs_3_), custom_call_target="tpu_custom_call" | custom-call | flops 134217728 | bytes 4194304 | tf_op jit(solution)/shard_map/respond/pallas_call | solution.py:98
  23.3 0.4 collective-permute-start.8
  23.8 0.0 collective-permute-done.4.refs_1_
  23.8 0.0 collective-permute-done.5.refs_2_
  23.8 4.4 %collective-permute-done.8.refs_3_ = bf16[9,32,128]{2,1,0:T(8,128)(2,1)S(1)} collective-permute-done((bf16[9,32,128]{2,1,0:T(8,128)(2,1)S(1)}, bf16[9,32,128]{2,1,0:T(8,128)(2,1)S(1)}, u32[]{:S(2)}, u32[]{:S(2)}) %collective-permute-start.8) | collective-permute-done | bytes 73760 | tf_op jit(solution)/shard_map/ppermute | solution.py:20
  28.1 0.1 stitch.1.mine_ref
  28.2 3.9 %collective-permute-start.9 = (f32[12,32,128]{2,1,0:T(8,128)S(1)}, f32[12,32,128]{2,1,0:T(8,128)S(1)}, u32[]{:S(2)}, u32[]{:S(2)}) collective-permute-start(f32[12,32,128]{2,1,0:T(8,128)S(1)} %stitch.1.mine_ref), channel_id=1, source_target_pairs={{0,4},{4,0},{8,12},{12,8},{16,20},{20,16},{24,28},{28,24},{32,36},... | collective-permute-start | bytes 589832 | tf_op jit(solution)/shard_map/ppermute | solution.py:26
  32.1 1.1 %collective-permute-done.9.other_ref = f32[12,32,128]{2,1,0:T(8,128)S(1)} collective-permute-done((f32[12,32,128]{2,1,0:T(8,128)S(1)}, f32[12,32,128]{2,1,0:T(8,128)S(1)}, u32[]{:S(2)}, u32[]{:S(2)}) %collective-permute-start.9) | collective-permute-done | bytes 196640 | tf_op jit(solution)/shard_map/ppermute | solution.py:26
  33.2 7.7 %collective-permute-start.10 = (bf16[20,32,128]{2,1,0:T(8,128)(2,1)S(1)}, bf16[20,32,128]{2,1,0:T(8,128)(2,1)S(1)}, u32[]{:S(2)}, u32[]{:S(2)}) collective-permute-start(bf16[20,32,128]{2,1,0:T(8,128)(2,1)S(1)} %get-tuple-element.11.chip_ref), channel_id=1, source_target_pairs={{0,8},{8,0},{12,20},{16,24},{20,12},{24,16},{28,36},{32,40},{36,28... | collective-permute-start | bytes 491528 | tf_op jit(solution)/shard_map/ppermute | solution.py:37
  41.0 1.9 %collective-permute-start.11 = (bf16[12,32,128]{2,1,0:T(8,128)(2,1)S(1)}, bf16[12,32,128]{2,1,0:T(8,128)(2,1)S(1)}, u32[]{:S(2)}, u32[]{:S(2)}) collective-permute-start(bf16[12,32,128]{2,1,0:T(8,128)(2,1)S(1)} %get-tuple-element.12), channel_id=1, source_target_pairs={{4,20},{12,28},{16,32},{20,4},{24,40},{28,12},{32,16},{36,52},{40,... | collective-permute-start | bytes 294920 | tf_op jit(solution)/shard_map/ppermute | solution.py:37
  42.9 0.8 %collective-permute-done.10.near_ref = bf16[20,32,128]{2,1,0:T(8,128)(2,1)S(1)} collective-permute-done((bf16[20,32,128]{2,1,0:T(8,128)(2,1)S(1)}, bf16[20,32,128]{2,1,0:T(8,128)(2,1)S(1)}, u32[]{:S(2)}, u32[]{:S(2)}) %collective-permute-start.10) | collective-permute-done | bytes 163872 | tf_op jit(solution)/shard_map/ppermute | solution.py:37
  43.6 1.4 %collective-permute-start.12 = (bf16[20,32,128]{2,1,0:T(8,128)(2,1)S(1)}, bf16[20,32,128]{2,1,0:T(8,128)(2,1)S(1)}, u32[]{:S(2)}, u32[]{:S(2)}) collective-permute-start(bf16[20,32,128]{2,1,0:T(8,128)(2,1)S(1)} %collective-permute-done.10.near_ref), channel_id=1, source_target_pairs={{0,4},{4,0},{8,12},{12,8},{16,20},{20,16},{24,28},{28,24},{32,36},... | collective-permute-start | bytes 491528 | tf_op jit(solution)/shard_map/ppermute | solution.py:26
  45.1 2.5 %collective-permute-done.11.far_ref = bf16[12,32,128]{2,1,0:T(8,128)(2,1)S(1)} collective-permute-done((bf16[12,32,128]{2,1,0:T(8,128)(2,1)S(1)}, bf16[12,32,128]{2,1,0:T(8,128)(2,1)S(1)}, u32[]{:S(2)}, u32[]{:S(2)}) %collective-permute-start.11) | collective-permute-done | bytes 98336 | tf_op jit(solution)/shard_map/ppermute | solution.py:37
  47.6 1.1 %collective-permute-start.13 = (bf16[12,32,128]{2,1,0:T(8,128)(2,1)S(1)}, bf16[12,32,128]{2,1,0:T(8,128)(2,1)S(1)}, u32[]{:S(2)}, u32[]{:S(2)}) collective-permute-start(bf16[12,32,128]{2,1,0:T(8,128)(2,1)S(1)} %collective-permute-done.11.far_ref), channel_id=1, source_target_pairs={{0,4},{4,0},{8,12},{12,8},{16,20},{20,16},{24,28},{28,24},{32,36},... | collective-permute-start | bytes 294920 | tf_op jit(solution)/shard_map/ppermute | solution.py:26
  48.6 0.9 %collective-permute-done.13.swap_far_ref = bf16[12,32,128]{2,1,0:T(8,128)(2,1)S(1)} collective-permute-done((bf16[12,32,128]{2,1,0:T(8,128)(2,1)S(1)}, bf16[12,32,128]{2,1,0:T(8,128)(2,1)S(1)}, u32[]{:S(2)}, u32[]{:S(2)}) %collective-permute-start.13) | collective-permute-done | bytes 98336 | tf_op jit(solution)/shard_map/ppermute | solution.py:26
  49.6 0.0 collective-permute-done.12.swap_near_ref
  49.6 0.0 slice-done
  49.6 0.0 copy-done.2
  49.6 0.0 copy-done.3
  49.6 0.0 slice-done.1
  49.6 2.5 %couple.1 = f32[2,16,1024]{2,1,0:T(8,128)} custom-call(s32[8,12]{1,0:T(8,128)S(1)} %copy-done.2, s32[8]{0:T(128)S(1)} %copy-done.3, bf16[8,12,2,128,128]{4,3,2,1,0:T(8,128)(2,1)S(1)} %bitcast.1, bf16[20,32,128]{2,1,0:T(8,128)(2,1)S(1)} %get-tuple-element.11.chip_ref, bf16[20,32,128]{2,1,0:T(8,128)(2,1)S(1)} %collective-permute-done.10.near_ref, ...), custom_call_target="tpu_custom_call" | custom-call | flops 201326592 | bytes 6291456 | tf_op jit(solution)/shard_map/couple/pallas_call | solution.py:228
  (4 shorter events, 0.0 us)
Async XLA Ops:
  1.1 8.6 %collective-permute-start.3 = (bf16[8,2,16,512]{3,2,1,0:T(8,128)(2,1)S(1)}, bf16[8,2,16,512]{3,2,1,0:T(8,128)(2,1)S(1)}, u32[]{:S(2)}, u32[]{:S(2)}) collective-permute-start(bf16[8,2,16,512]{3,2,1,0:T(8,128)(2,1)S(1)} %get-tuple-element.13.refs_3_), channel_id=1, source_target_pairs={{0,3},{1,2},{2,1},{3,0},{4,7},{5,6},{6,5},{7,4},{8,11},{9,10},{10,... | collective-permute-start | bytes 786440 | tf_op jit(solution)/shard_map/ppermute | solution.py:21
  3.9 6.9 %collective-permute-start = (bf16[8,2,16,512]{3,2,1,0:T(8,128)(2,1)S(1)}, bf16[8,2,16,512]{3,2,1,0:T(8,128)(2,1)S(1)}, u32[]{:S(2)}, u32[]{:S(2)}) collective-permute-start(bf16[8,2,16,512]{3,2,1,0:T(8,128)(2,1)S(1)} %get-tuple-element.14.refs_2_), channel_id=1, source_target_pairs={{0,1},{1,0},{2,3},{3,2},{4,5},{5,4},{6,7},{7,6},{8,9},{9,8},{10,11... | collective-permute-start | bytes 786440 | tf_op jit(solution)/shard_map/ppermute | solution.py:21
  3.9 12.5 %collective-permute-start.1 = (bf16[8,2,16,512]{3,2,1,0:T(8,128)(2,1)S(1)}, bf16[8,2,16,512]{3,2,1,0:T(8,128)(2,1)S(1)}, u32[]{:S(2)}, u32[]{:S(2)}) collective-permute-start(bf16[8,2,16,512]{3,2,1,0:T(8,128)(2,1)S(1)} %get-tuple-element.13.refs_3_), channel_id=1, source_target_pairs={{0,1},{1,0},{2,3},{3,2},{4,5},{5,4},{6,7},{7,6},{8,9},{9,8},{10,11... | collective-permute-start | bytes 786440 | tf_op jit(solution)/shard_map/ppermute | solution.py:21
  5.4 11.0 %collective-permute-start.2 = (bf16[8,2,16,512]{3,2,1,0:T(8,128)(2,1)S(1)}, bf16[8,2,16,512]{3,2,1,0:T(8,128)(2,1)S(1)}, u32[]{:S(2)}, u32[]{:S(2)}) collective-permute-start(bf16[8,2,16,512]{3,2,1,0:T(8,128)(2,1)S(1)} %get-tuple-element.14.refs_2_), channel_id=1, source_target_pairs={{0,3},{1,2},{2,1},{3,0},{4,7},{5,6},{6,5},{7,4},{8,11},{9,10},{10,... | collective-permute-start | bytes 786440 | tf_op jit(solution)/shard_map/ppermute | solution.py:21
  5.5 2.2 %copy-start = (bf16[16,2,512,128]{3,2,1,0:T(8,128)(2,1)S(1)}, bf16[16,2,512,128]{3,2,1,0:T(8,128)(2,1)}, u32[]{:S(2)}) copy-start(bf16[16,2,512,128]{3,2,1,0:T(8,128)(2,1)} %refs_1_.5) | copy-start | bytes 12582916
  7.6 0.7 %copy-start.1 = (s32[16]{0:T(128)S(1)}, s32[16]{0:T(128)}, u32[]{:S(2)}) copy-start(s32[16]{0:T(128)} %refs_0_.5) | copy-start | bytes 196
  9.6 39.9 %slice-start = ((s8[6291456]{0:T(1024)(128)(4,1)}), s8[4194304]{0:T(1024)(128)(4,1)S(1)}, s32[]{:S(2)}) async-start(s8[6291456]{0:T(1024)(128)(4,1)} %bitcast), calls=%async_computation | async-start | bytes 8388608
  9.6 39.9 %copy-start.2 = (s32[8,12]{1,0:T(8,128)S(1)}, s32[8,12]{1,0:T(8,128)}, u32[]{:S(2)}) copy-start(s32[8,12]{1,0:T(8,128)} %cols_ref.1) | copy-start | bytes 1156
  9.7 39.9 %copy-start.3 = (s32[8]{0:T(128)S(1)}, s32[8]{0:T(128)}, u32[]{:S(2)}) copy-start(s32[8]{0:T(128)} %counts_ref.1) | copy-start | bytes 100
  9.7 12.3 %collective-permute-start.7 = (bf16[8,2,16,512]{3,2,1,0:T(8,128)(2,1)S(1)}, bf16[8,2,16,512]{3,2,1,0:T(8,128)(2,1)S(1)}, u32[]{:S(2)}, u32[]{:S(2)}) collective-permute-start(bf16[8,2,16,512]{3,2,1,0:T(8,128)(2,1)S(1)} %gate.3.refs_5_), channel_id=1, source_target_pairs={{0,1},{1,0},{2,3},{3,2},{4,5},{5,4},{6,7},{7,6},{8,9},{9,8},{10,11... | collective-permute-start | bytes 786440 | tf_op jit(solution)/shard_map/ppermute | solution.py:21
  10.7 38.8 %slice-start.1 = ((s8[6291456]{0:T(1024)(128)(4,1)}), s8[2097152]{0:T(1024)(128)(4,1)S(1)}, s32[]{:S(2)}) async-start(s8[6291456]{0:T(1024)(128)(4,1)} %bitcast), calls=%async_computation.1 | async-start | bytes 4194304
  10.7 11.2 %collective-permute-start.6 = (bf16[8,2,16,512]{3,2,1,0:T(8,128)(2,1)S(1)}, bf16[8,2,16,512]{3,2,1,0:T(8,128)(2,1)S(1)}, u32[]{:S(2)}, u32[]{:S(2)}) collective-permute-start(bf16[8,2,16,512]{3,2,1,0:T(8,128)(2,1)S(1)} %gate.2.refs_2_), channel_id=1, source_target_pairs={{0,3},{1,2},{2,1},{3,0},{4,7},{5,6},{6,5},{7,4},{8,11},{9,10},{10,... | collective-permute-start | bytes 786440 | tf_op jit(solution)/shard_map/ppermute | solution.py:21
  18.3 5.5 %collective-permute-start.4 = (bf16[9,32,128]{2,1,0:T(8,128)(2,1)S(1)}, bf16[9,32,128]{2,1,0:T(8,128)(2,1)S(1)}, u32[]{:S(2)}, u32[]{:S(2)}) collective-permute-start(bf16[9,32,128]{2,1,0:T(8,128)(2,1)S(1)} %get-tuple-element.9), channel_id=1, source_target_pairs={{0,1},{1,0},{2,3},{3,2},{4,5},{5,4},{6,7},{7,6},{8,9},{9,8},{10,11... | collective-permute-start | bytes 221192 | tf_op jit(solution)/shard_map/ppermute | solution.py:21
  18.5 5.2 %collective-permute-start.5 = (bf16[9,32,128]{2,1,0:T(8,128)(2,1)S(1)}, bf16[9,32,128]{2,1,0:T(8,128)(2,1)S(1)}, u32[]{:S(2)}, u32[]{:S(2)}) collective-permute-start(bf16[9,32,128]{2,1,0:T(8,128)(2,1)S(1)} %get-tuple-element.10), channel_id=1, source_target_pairs={{0,3},{1,2},{2,1},{3,0},{4,7},{5,6},{6,5},{7,4},{8,11},{9,10},{10,... | collective-permute-start | bytes 221192 | tf_op jit(solution)/shard_map/ppermute | solution.py:21
  23.3 4.8 %collective-permute-start.8 = (bf16[9,32,128]{2,1,0:T(8,128)(2,1)S(1)}, bf16[9,32,128]{2,1,0:T(8,128)(2,1)S(1)}, u32[]{:S(2)}, u32[]{:S(2)}) collective-permute-start(bf16[9,32,128]{2,1,0:T(8,128)(2,1)S(1)} %respond.5), channel_id=1, source_target_pairs={{0,2},{1,3},{2,0},{3,1},{4,6},{5,7},{6,4},{7,5},{8,10},{9,11},{10,... | collective-permute-start | bytes 221192 | tf_op jit(solution)/shard_map/ppermute | solution.py:20
  28.2 5.0 %collective-permute-start.9 = (f32[12,32,128]{2,1,0:T(8,128)S(1)}, f32[12,32,128]{2,1,0:T(8,128)S(1)}, u32[]{:S(2)}, u32[]{:S(2)}) collective-permute-start(f32[12,32,128]{2,1,0:T(8,128)S(1)} %stitch.1.mine_ref), channel_id=1, source_target_pairs={{0,4},{4,0},{8,12},{12,8},{16,20},{20,16},{24,28},{28,24},{32,36},... | collective-permute-start | bytes 589832 | tf_op jit(solution)/shard_map/ppermute | solution.py:26
  33.2 10.4 %collective-permute-start.10 = (bf16[20,32,128]{2,1,0:T(8,128)(2,1)S(1)}, bf16[20,32,128]{2,1,0:T(8,128)(2,1)S(1)}, u32[]{:S(2)}, u32[]{:S(2)}) collective-permute-start(bf16[20,32,128]{2,1,0:T(8,128)(2,1)S(1)} %get-tuple-element.11.chip_ref), channel_id=1, source_target_pairs={{0,8},{8,0},{12,20},{16,24},{20,12},{24,16},{28,36},{32,40},{36,28... | collective-permute-start | bytes 491528 | tf_op jit(solution)/shard_map/ppermute | solution.py:37
  41.0 6.6 %collective-permute-start.11 = (bf16[12,32,128]{2,1,0:T(8,128)(2,1)S(1)}, bf16[12,32,128]{2,1,0:T(8,128)(2,1)S(1)}, u32[]{:S(2)}, u32[]{:S(2)}) collective-permute-start(bf16[12,32,128]{2,1,0:T(8,128)(2,1)S(1)} %get-tuple-element.12), channel_id=1, source_target_pairs={{4,20},{12,28},{16,32},{20,4},{24,40},{28,12},{32,16},{36,52},{40,... | collective-permute-start | bytes 294920 | tf_op jit(solution)/shard_map/ppermute | solution.py:37
  43.6 5.9 %collective-permute-start.12 = (bf16[20,32,128]{2,1,0:T(8,128)(2,1)S(1)}, bf16[20,32,128]{2,1,0:T(8,128)(2,1)S(1)}, u32[]{:S(2)}, u32[]{:S(2)}) collective-permute-start(bf16[20,32,128]{2,1,0:T(8,128)(2,1)S(1)} %collective-permute-done.10.near_ref), channel_id=1, source_target_pairs={{0,4},{4,0},{8,12},{12,8},{16,20},{20,16},{24,28},{28,24},{32,36},... | collective-permute-start | bytes 491528 | tf_op jit(solution)/shard_map/ppermute | solution.py:26
  47.6 2.0 %collective-permute-start.13 = (bf16[12,32,128]{2,1,0:T(8,128)(2,1)S(1)}, bf16[12,32,128]{2,1,0:T(8,128)(2,1)S(1)}, u32[]{:S(2)}, u32[]{:S(2)}) collective-permute-start(bf16[12,32,128]{2,1,0:T(8,128)(2,1)S(1)} %collective-permute-done.11.far_ref), channel_id=1, source_target_pairs={{0,4},{4,0},{8,12},{12,8},{16,20},{20,16},{24,28},{28,24},{32,36},... | collective-permute-start | bytes 294920 | tf_op jit(solution)/shard_map/ppermute | solution.py:26

commit v5 on v4

--- a/solution.py
+++ b/solution.py
@@ -43,6 +43,7 @@
 
 
 def placed_sums(jitter_ref, pieces, response_ref):
+    jitter = jitter_ref[...]
     domains = response_ref.shape[0]
     per_piece = domains // len(pieces)
     angles = pieces[0].shape[2]
@@ -54,7 +55,7 @@
         real = product[:angles, :LANES] - product[angles:, LANES:]
         imag = product[:angles, LANES:] + product[angles:, :LANES]
         field = jnp.concatenate([real, imag], axis=0).astype(jnp.bfloat16).astype(jnp.float32)
-        start = (d % 2) * (LANES // 2) + jitter_ref[d]
+        start = (d % 2) * (LANES // 2) + jitter[0, d]
         turned = pltpu.roll(field, start, 1)
         lane = lax.broadcasted_iota(jnp.int32, turned.shape, 1)
         here = jnp.where(lane >= start, turned, 0.0)
@@ -98,14 +99,14 @@
     return pl.pallas_call(
         functools.partial(respond_kernel, len(groups), halves),
         out_shape=[sums] * len(groups),
-        in_specs=[SMEM, VMEM] + [VMEM] * (len(groups) * halves),
+        in_specs=[VMEM, VMEM] + [VMEM] * (len(groups) * halves),
         out_specs=[VMEM] * len(groups),
         compiler_params=pltpu.CompilerParams(vmem_limit_bytes=16 * 2**20),
         cost_estimate=pl.CostEstimate(
             flops=len(groups) * domains * 8 * angles * depth * cols, bytes_accessed=2 * response.size, transcendentals=0
         ),
         name="respond",
-    )(jitter, response, *[piece for group in groups for piece in group])
+    )(jitter[None], response, *[piece for group in groups for piece in group])
 
 
 def stitch_kernel(*refs):
@@ -168,6 +169,7 @@
 
 
 def couple_kernel(cols_ref, counts_ref, green_ref, chip_ref, near_ref, far_ref, swap_near_ref, swap_far_ref, out_ref, window):
+    cols, counts = cols_ref[...], counts_ref[...]
     rows, lanes = chip_ref.shape[1:]
     blocks = far_ref.shape[0] - HALO
     angles = rows // 2
@@ -207,8 +209,7 @@
     for r in range(green_ref.shape[0]):
         picked = []
         for k in range(entries):
-            index = jnp.where(k < counts_ref[r], cols_ref[r, k] - first_col, dead)
-            picked.append(window[index])
+            picked.append(window[jnp.where(k < counts[0, r], cols[r, k] - first_col, dead)])
         wave = jnp.concatenate(picked, axis=1)
         green = jnp.concatenate(
             [green_ref[r, :, 0].reshape(entries * lanes, lanes), green_ref[r, :, 1].reshape(entries * lanes, lanes)],
@@ -228,13 +229,13 @@
     return pl.pallas_call(
         couple_kernel,
         out_shape=jax.ShapeDtypeStruct((2, rows // 2, rows_here * lanes), jnp.float32),
-        in_specs=[SMEM, SMEM] + [VMEM] * 6,
+        in_specs=[VMEM] * 8,
         out_specs=VMEM,
         scratch_shapes=[pltpu.VMEM((8 * blocks + 8, rows, lanes), jnp.bfloat16)],
         compiler_params=pltpu.CompilerParams(vmem_limit_bytes=24 * 2**20),
         cost_estimate=pl.CostEstimate(flops=flops, bytes_accessed=green.size * 2, transcendentals=0),
         name="couple",
-    )(block_cols, block_counts, green, chip, near, far, swap_near, swap_far)
+    )(block_cols, block_counts[None], green, chip, near, far, swap_near, swap_far)
 
 
 def per_device(incident, response, jitter, block_cols, block_counts, green_blocks):

time: 52.2 us -> 51 us (0.977)
  Pallas kernels: 7.13 us -> 4.88 us
  waiting for transfers between devices: 16.5 us -> 17.8 us
    ppermute x8, waiting for transfers between devices: 6.85 us -> 8.49 us  [angle_pairs(): lax.ppermute(block, 'ang', [(a, ((a + shift ^ 1) - shift) % size) for a i...]
    pallas_call x3, Pallas kernels: 4.56 us -> 2.97 us  [respond(): pl.pallas_call(functools.partial(respond_kernel, len(groups), halves), ou...]
    pallas_call x1, Pallas kernels: 2.46 us -> 1.8 us  [couple(): pl.pallas_call(couple_kernel, out_shape=jax.ShapeDtypeStruct((2, rows //...]
  transfers between devices with their start and end apart: 14 -> 14, of which waited for: 8 -> 10; matrix products, arithmetic and copies ran while one was open for 0% -> 0% of each run, Pallas kernels for 9% -> 6%
where the time goes in v5:
time: 51 us; the launch traced here: 50.9 us
  starting transfers between devices  24.2 us (47%)
  waiting for transfers between devices  17.8 us (35%)
  Pallas kernels  4.88 us (10%)
  local copies, waits for them, and re-layouts  3.93 us (8%)
    ppermute x2, starting transfers between devices, pairs(): return lax.ppermute(block, 'dom', route)  9.67 us
    ppermute x8, waiting for transfers between devices, angle_pairs(): lax.ppermute(block, 'ang', [(a, ((a + shift ^ 1) - shift) % size) for a i...  8.49 us
    ppermute x8, starting transfers between devices, angle_pairs(): lax.ppermute(block, 'ang', [(a, ((a + shift ^ 1) - shift) % size) for a i...  7.72 us
    ppermute x3, starting transfers between devices, other_core(): return lax.ppermute(block, 'dom', [(i, i ^ 1) for i in range(doms)])  6.38 us
    ppermute x1, waiting for transfers between devices, angle_pairs(): lax.ppermute(block, 'ang', [(a, (a + 2) % size) for a in range(size)])  4 us
    ppermute x2, waiting for transfers between devices, pairs(): return lax.ppermute(block, 'dom', route)  3.25 us
    pallas_call x3, Pallas kernels, respond(): pl.pallas_call(functools.partial(respond_kernel, len(groups), halves), ou...  2.97 us
    unnamed x12, local copies, waits for them, and re-layouts  2.86 us
  transfers between devices with their start and end apart: 14, of which 10 were waited for; matrix products, arithmetic and copies ran while one was open for 0% of the time, Pallas kernels for 6%

profile of v5, /device:TPU:7, one launch (start us, length us, event | category | flops | bytes accessed | tf_op | source)
XLA Modules:
  0.0 50.9 jit_solution(13062538164042964525)
XLA Ops:
  0.0 1.1 %fusion = (bf16[8,2,16,512]{3,2,1,0:T(8,128)(2,1)S(1)}, bf16[8,2,16,512]{3,2,1,0:T(8,128)(2,1)S(1)}) fusion(bf16[16,2,16,512]{3,2,1,0:T(8,128)(2,1)} %param.6), kind=kLoop, calls=%fused_computation | loop fusion | bytes 1048576 | tf_op jit(solution)/shard_map/slice | solution.py:243
  1.1 2.8 %collective-permute-start.3 = (bf16[8,2,16,512]{3,2,1,0:T(8,128)(2,1)S(1)}, bf16[8,2,16,512]{3,2,1,0:T(8,128)(2,1)S(1)}, u32[]{:S(2)}, u32[]{:S(2)}) collective-permute-start(bf16[8,2,16,512]{3,2,1,0:T(8,128)(2,1)S(1)} %get-tuple-element.13.refs_3_), channel_id=1, source_target_pairs={{0,3},{1,2},{2,1},{3,0},{4,7},{5,6},{6,5},{7,4},{8,11},{9,10},{10,... | collective-permute-start | bytes 786440 | tf_op jit(solution)/shard_map/ppermute | solution.py:21
  3.9 0.0 collective-permute-start
  3.9 1.5 %collective-permute-start.1 = (bf16[8,2,16,512]{3,2,1,0:T(8,128)(2,1)S(1)}, bf16[8,2,16,512]{3,2,1,0:T(8,128)(2,1)S(1)}, u32[]{:S(2)}, u32[]{:S(2)}) collective-permute-start(bf16[8,2,16,512]{3,2,1,0:T(8,128)(2,1)S(1)} %get-tuple-element.13.refs_3_), channel_id=1, source_target_pairs={{0,1},{1,0},{2,3},{3,2},{4,5},{5,4},{6,7},{7,6},{8,9},{9,8},{10,11... | collective-permute-start | bytes 786440 | tf_op jit(solution)/shard_map/ppermute | solution.py:21
  5.4 0.1 collective-permute-start.2
  5.5 0.0 copy-start
  5.5 2.2 %copy-done = bf16[16,2,512,128]{3,2,1,0:T(8,128)(2,1)S(1)} copy-done((bf16[16,2,512,128]{3,2,1,0:T(8,128)(2,1)S(1)}, bf16[16,2,512,128]{3,2,1,0:T(8,128)(2,1)}, u32[]{:S(2)}) %copy-start) | copy-done | bytes 4194328
  7.6 0.0 copy-start.1
  7.6 0.7 %copy-done.1 = s32[16]{0:T(128)S(1)} copy-done((s32[16]{0:T(128)S(1)}, s32[16]{0:T(128)}, u32[]{:S(2)}) %copy-start.1) | copy-done | bytes 88
  8.3 0.8 %respond.3.after_ref.refs_0_ = f32[9,32,128]{2,1,0:T(8,128)S(1)} custom-call(s32[1,16]{1,0:T(1,128)S(1)} %bitcast.4, bf16[16,2,512,128]{3,2,1,0:T(8,128)(2,1)S(1)} %copy-done, bf16[8,2,16,512]{3,2,1,0:T(8,128)(2,1)S(1)} %get-tuple-element.14.refs_2_, bf16[8,2,16,512]{3,2,1,0:T(8,128)(2,1)S(1)} %get-tuple-element.13.refs_3_), custom_call_target="tpu_custom_call" | custom-call | flops 134217728 | bytes 4194304 | tf_op jit(solution)/shard_map/respond/pallas_call | solution.py:99
  9.1 0.0 slice-start
  9.1 0.0 copy-start.2
  9.1 0.0 copy-start.3
  9.1 0.5 %collective-permute-done.3.held_ref = bf16[8,2,16,512]{3,2,1,0:T(8,128)(2,1)S(1)} collective-permute-done((bf16[8,2,16,512]{3,2,1,0:T(8,128)(2,1)S(1)}, bf16[8,2,16,512]{3,2,1,0:T(8,128)(2,1)S(1)}, u32[]{:S(2)}, u32[]{:S(2)}) %collective-permute-start.3) | collective-permute-done | bytes 262176 | tf_op jit(solution)/shard_map/ppermute | solution.py:21
  9.7 0.0 collective-permute-start.7
  9.7 1.1 %collective-permute-done.held_ref = bf16[8,2,16,512]{3,2,1,0:T(8,128)(2,1)S(1)} collective-permute-done((bf16[8,2,16,512]{3,2,1,0:T(8,128)(2,1)S(1)}, bf16[8,2,16,512]{3,2,1,0:T(8,128)(2,1)S(1)}, u32[]{:S(2)}, u32[]{:S(2)}) %collective-permute-start) | collective-permute-done | bytes 262176 | tf_op jit(solution)/shard_map/ppermute | solution.py:21
  10.7 0.0 slice-start.1
  10.7 1.6 %collective-permute-start.6 = (bf16[8,2,16,512]{3,2,1,0:T(8,128)(2,1)S(1)}, bf16[8,2,16,512]{3,2,1,0:T(8,128)(2,1)S(1)}, u32[]{:S(2)}, u32[]{:S(2)}) collective-permute-start(bf16[8,2,16,512]{3,2,1,0:T(8,128)(2,1)S(1)} %gate.2.refs_2_), channel_id=1, source_target_pairs={{0,3},{1,2},{2,1},{3,0},{4,7},{5,6},{6,5},{7,4},{8,11},{9,10},{10,... | collective-permute-start | bytes 786440 | tf_op jit(solution)/shard_map/ppermute | solution.py:21
  12.4 4.0 %collective-permute-done.1.refs_3_ = bf16[8,2,16,512]{3,2,1,0:T(8,128)(2,1)S(1)} collective-permute-done((bf16[8,2,16,512]{3,2,1,0:T(8,128)(2,1)S(1)}, bf16[8,2,16,512]{3,2,1,0:T(8,128)(2,1)S(1)}, u32[]{:S(2)}, u32[]{:S(2)}) %collective-permute-start.1) | collective-permute-done | bytes 262176 | tf_op jit(solution)/shard_map/ppermute | solution.py:21
  16.4 0.0 collective-permute-done.2.refs_4_
  16.4 1.4 %respond.4 = (bf16[9,32,128]{2,1,0:T(8,128)(2,1)S(1)}, bf16[9,32,128]{2,1,0:T(8,128)(2,1)S(1)}) custom-call(s32[1,16]{1,0:T(1,128)S(1)} %bitcast.5, bf16[16,2,512,128]{3,2,1,0:T(8,128)(2,1)S(1)} %copy-done, bf16[8,2,16,512]{3,2,1,0:T(8,128)(2,1)S(1)} %gate.2.refs_2_, bf16[8,2,16,512]{3,2,1,0:T(8,128)(2,1)S(1)} %collective-permute-done.1.refs_3_, ...), custom_call_target="tpu_custom_call" | custom-call | flops 268435456 | bytes 4194304 | tf_op jit(solution)/shard_map/respond/pallas_call | solution.py:99
  17.7 0.2 collective-permute-start.4
  18.0 1.5 %collective-permute-start.5 = (bf16[9,32,128]{2,1,0:T(8,128)(2,1)S(1)}, bf16[9,32,128]{2,1,0:T(8,128)(2,1)S(1)}, u32[]{:S(2)}, u32[]{:S(2)}) collective-permute-start(bf16[9,32,128]{2,1,0:T(8,128)(2,1)S(1)} %get-tuple-element.10), channel_id=1, source_target_pairs={{0,3},{1,2},{2,1},{3,0},{4,7},{5,6},{6,5},{7,4},{8,11},{9,10},{10,... | collective-permute-start | bytes 221192 | tf_op jit(solution)/shard_map/ppermute | solution.py:21
  19.4 2.6 %collective-permute-done.7.refs_3_ = bf16[8,2,16,512]{3,2,1,0:T(8,128)(2,1)S(1)} collective-permute-done((bf16[8,2,16,512]{3,2,1,0:T(8,128)(2,1)S(1)}, bf16[8,2,16,512]{3,2,1,0:T(8,128)(2,1)S(1)}, u32[]{:S(2)}, u32[]{:S(2)}) %collective-permute-start.7) | collective-permute-done | bytes 262176 | tf_op jit(solution)/shard_map/ppermute | solution.py:21
  22.0 0.0 collective-permute-done.6.refs_2_
  22.0 0.8 %respond.5 = bf16[9,32,128]{2,1,0:T(8,128)(2,1)S(1)} custom-call(s32[1,16]{1,0:T(1,128)S(1)} %bitcast.6, bf16[16,2,512,128]{3,2,1,0:T(8,128)(2,1)S(1)} %copy-done, bf16[8,2,16,512]{3,2,1,0:T(8,128)(2,1)S(1)} %collective-permute-done.6.refs_2_, bf16[8,2,16,512]{3,2,1,0:T(8,128)(2,1)S(1)} %collective-permute-done.7.refs_3_), custom_call_target="tpu_custom_call" | custom-call | flops 134217728 | bytes 4194304 | tf_op jit(solution)/shard_map/respond/pallas_call | solution.py:99
  22.8 0.4 collective-permute-start.8
  23.2 0.3 collective-permute-done.4.refs_1_
  23.6 0.0 collective-permute-done.5.refs_2_
  23.6 4.0 %collective-permute-done.8.refs_3_ = bf16[9,32,128]{2,1,0:T(8,128)(2,1)S(1)} collective-permute-done((bf16[9,32,128]{2,1,0:T(8,128)(2,1)S(1)}, bf16[9,32,128]{2,1,0:T(8,128)(2,1)S(1)}, u32[]{:S(2)}, u32[]{:S(2)}) %collective-permute-start.8) | collective-permute-done | bytes 73760 | tf_op jit(solution)/shard_map/ppermute | solution.py:20
  27.6 0.1 stitch.1.mine_ref
  27.6 3.9 %collective-permute-start.9 = (f32[12,32,128]{2,1,0:T(8,128)S(1)}, f32[12,32,128]{2,1,0:T(8,128)S(1)}, u32[]{:S(2)}, u32[]{:S(2)}) collective-permute-start(f32[12,32,128]{2,1,0:T(8,128)S(1)} %stitch.1.mine_ref), channel_id=1, source_target_pairs={{0,4},{4,0},{8,12},{12,8},{16,20},{20,16},{24,28},{28,24},{32,36},... | collective-permute-start | bytes 589832 | tf_op jit(solution)/shard_map/ppermute | solution.py:26
  31.5 1.1 %collective-permute-done.9.other_ref = f32[12,32,128]{2,1,0:T(8,128)S(1)} collective-permute-done((f32[12,32,128]{2,1,0:T(8,128)S(1)}, f32[12,32,128]{2,1,0:T(8,128)S(1)}, u32[]{:S(2)}, u32[]{:S(2)}) %collective-permute-start.9) | collective-permute-done | bytes 196640 | tf_op jit(solution)/shard_map/ppermute | solution.py:26
  32.7 7.7 %collective-permute-start.10 = (bf16[20,32,128]{2,1,0:T(8,128)(2,1)S(1)}, bf16[20,32,128]{2,1,0:T(8,128)(2,1)S(1)}, u32[]{:S(2)}, u32[]{:S(2)}) collective-permute-start(bf16[20,32,128]{2,1,0:T(8,128)(2,1)S(1)} %get-tuple-element.11.chip_ref), channel_id=1, source_target_pairs={{0,8},{8,0},{12,20},{16,24},{20,12},{24,16},{28,36},{32,40},{36,28... | collective-permute-start | bytes 491528 | tf_op jit(solution)/shard_map/ppermute | solution.py:37
  40.4 1.9 %collective-permute-start.11 = (bf16[12,32,128]{2,1,0:T(8,128)(2,1)S(1)}, bf16[12,32,128]{2,1,0:T(8,128)(2,1)S(1)}, u32[]{:S(2)}, u32[]{:S(2)}) collective-permute-start(bf16[12,32,128]{2,1,0:T(8,128)(2,1)S(1)} %get-tuple-element.12), channel_id=1, source_target_pairs={{4,20},{12,28},{16,32},{20,4},{24,40},{28,12},{32,16},{36,52},{40,... | collective-permute-start | bytes 294920 | tf_op jit(solution)/shard_map/ppermute | solution.py:37
  42.3 0.8 %collective-permute-done.10.near_ref = bf16[20,32,128]{2,1,0:T(8,128)(2,1)S(1)} collective-permute-done((bf16[20,32,128]{2,1,0:T(8,128)(2,1)S(1)}, bf16[20,32,128]{2,1,0:T(8,128)(2,1)S(1)}, u32[]{:S(2)}, u32[]{:S(2)}) %collective-permute-start.10) | collective-permute-done | bytes 163872 | tf_op jit(solution)/shard_map/ppermute | solution.py:37
  43.1 1.4 %collective-permute-start.12 = (bf16[20,32,128]{2,1,0:T(8,128)(2,1)S(1)}, bf16[20,32,128]{2,1,0:T(8,128)(2,1)S(1)}, u32[]{:S(2)}, u32[]{:S(2)}) collective-permute-start(bf16[20,32,128]{2,1,0:T(8,128)(2,1)S(1)} %collective-permute-done.10.near_ref), channel_id=1, source_target_pairs={{0,4},{4,0},{8,12},{12,8},{16,20},{20,16},{24,28},{28,24},{32,36},... | collective-permute-start | bytes 491528 | tf_op jit(solution)/shard_map/ppermute | solution.py:26
  44.5 2.5 %collective-permute-done.11.far_ref = bf16[12,32,128]{2,1,0:T(8,128)(2,1)S(1)} collective-permute-done((bf16[12,32,128]{2,1,0:T(8,128)(2,1)S(1)}, bf16[12,32,128]{2,1,0:T(8,128)(2,1)S(1)}, u32[]{:S(2)}, u32[]{:S(2)}) %collective-permute-start.11) | collective-permute-done | bytes 98336 | tf_op jit(solution)/shard_map/ppermute | solution.py:37
  47.0 1.1 %collective-permute-start.13 = (bf16[12,32,128]{2,1,0:T(8,128)(2,1)S(1)}, bf16[12,32,128]{2,1,0:T(8,128)(2,1)S(1)}, u32[]{:S(2)}, u32[]{:S(2)}) collective-permute-start(bf16[12,32,128]{2,1,0:T(8,128)(2,1)S(1)} %collective-permute-done.11.far_ref), channel_id=1, source_target_pairs={{0,4},{4,0},{8,12},{12,8},{16,20},{20,16},{24,28},{28,24},{32,36},... | collective-permute-start | bytes 294920 | tf_op jit(solution)/shard_map/ppermute | solution.py:26
  48.1 0.9 %collective-permute-done.13.swap_far_ref = bf16[12,32,128]{2,1,0:T(8,128)(2,1)S(1)} collective-permute-done((bf16[12,32,128]{2,1,0:T(8,128)(2,1)S(1)}, bf16[12,32,128]{2,1,0:T(8,128)(2,1)S(1)}, u32[]{:S(2)}, u32[]{:S(2)}) %collective-permute-start.13) | collective-permute-done | bytes 98336 | tf_op jit(solution)/shard_map/ppermute | solution.py:26
  49.0 0.0 collective-permute-done.12.swap_near_ref
  49.0 0.0 slice-done
  49.0 0.0 copy-done.2
  49.0 0.0 copy-done.3
  49.0 0.0 slice-done.1
  49.1 1.8 %couple.1 = f32[2,16,1024]{2,1,0:T(8,128)} custom-call(s32[8,12]{1,0:T(8,128)S(1)} %copy-done.2, s32[1,8]{1,0:T(1,128)S(1)} %bitcast.7, bf16[8,12,2,128,128]{4,3,2,1,0:T(8,128)(2,1)S(1)} %bitcast.3, bf16[20,32,128]{2,1,0:T(8,128)(2,1)S(1)} %get-tuple-element.11.chip_ref, bf16[20,32,128]{2,1,0:T(8,128)(2,1)S(1)} %collective-permute-done.10.near_ref, ...), custom_call_target="tpu_custom_call" | custom-call | flops 201326592 | bytes 6291456 | tf_op jit(solution)/shard_map/couple/pallas_call | solution.py:229
  (4 shorter events, 0.0 us)
Async XLA Ops:
  1.1 8.6 %collective-permute-start.3 = (bf16[8,2,16,512]{3,2,1,0:T(8,128)(2,1)S(1)}, bf16[8,2,16,512]{3,2,1,0:T(8,128)(2,1)S(1)}, u32[]{:S(2)}, u32[]{:S(2)}) collective-permute-start(bf16[8,2,16,512]{3,2,1,0:T(8,128)(2,1)S(1)} %get-tuple-element.13.refs_3_), channel_id=1, source_target_pairs={{0,3},{1,2},{2,1},{3,0},{4,7},{5,6},{6,5},{7,4},{8,11},{9,10},{10,... | collective-permute-start | bytes 786440 | tf_op jit(solution)/shard_map/ppermute | solution.py:21
  3.9 6.9 %collective-permute-start = (bf16[8,2,16,512]{3,2,1,0:T(8,128)(2,1)S(1)}, bf16[8,2,16,512]{3,2,1,0:T(8,128)(2,1)S(1)}, u32[]{:S(2)}, u32[]{:S(2)}) collective-permute-start(bf16[8,2,16,512]{3,2,1,0:T(8,128)(2,1)S(1)} %get-tuple-element.14.refs_2_), channel_id=1, source_target_pairs={{0,1},{1,0},{2,3},{3,2},{4,5},{5,4},{6,7},{7,6},{8,9},{9,8},{10,11... | collective-permute-start | bytes 786440 | tf_op jit(solution)/shard_map/ppermute | solution.py:21
  3.9 12.5 %collective-permute-start.1 = (bf16[8,2,16,512]{3,2,1,0:T(8,128)(2,1)S(1)}, bf16[8,2,16,512]{3,2,1,0:T(8,128)(2,1)S(1)}, u32[]{:S(2)}, u32[]{:S(2)}) collective-permute-start(bf16[8,2,16,512]{3,2,1,0:T(8,128)(2,1)S(1)} %get-tuple-element.13.refs_3_), channel_id=1, source_target_pairs={{0,1},{1,0},{2,3},{3,2},{4,5},{5,4},{6,7},{7,6},{8,9},{9,8},{10,11... | collective-permute-start | bytes 786440 | tf_op jit(solution)/shard_map/ppermute | solution.py:21
  5.4 11.0 %collective-permute-start.2 = (bf16[8,2,16,512]{3,2,1,0:T(8,128)(2,1)S(1)}, bf16[8,2,16,512]{3,2,1,0:T(8,128)(2,1)S(1)}, u32[]{:S(2)}, u32[]{:S(2)}) collective-permute-start(bf16[8,2,16,512]{3,2,1,0:T(8,128)(2,1)S(1)} %get-tuple-element.14.refs_2_), channel_id=1, source_target_pairs={{0,3},{1,2},{2,1},{3,0},{4,7},{5,6},{6,5},{7,4},{8,11},{9,10},{10,... | collective-permute-start | bytes 786440 | tf_op jit(solution)/shard_map/ppermute | solution.py:21
  5.5 2.2 %copy-start = (bf16[16,2,512,128]{3,2,1,0:T(8,128)(2,1)S(1)}, bf16[16,2,512,128]{3,2,1,0:T(8,128)(2,1)}, u32[]{:S(2)}) copy-start(bf16[16,2,512,128]{3,2,1,0:T(8,128)(2,1)} %refs_1_.5) | copy-start | bytes 12582916
  7.6 0.7 %copy-start.1 = (s32[16]{0:T(128)S(1)}, s32[16]{0:T(128)}, u32[]{:S(2)}) copy-start(s32[16]{0:T(128)} %param.8) | copy-start | bytes 196
  9.1 39.9 %slice-start = ((s8[6291456]{0:T(1024)(128)(4,1)}), s8[4194304]{0:T(1024)(128)(4,1)S(1)}, s32[]{:S(2)}) async-start(s8[6291456]{0:T(1024)(128)(4,1)} %bitcast.2), calls=%async_computation | async-start | bytes 8388608
  9.1 39.9 %copy-start.2 = (s32[8,12]{1,0:T(8,128)S(1)}, s32[8,12]{1,0:T(8,128)}, u32[]{:S(2)}) copy-start(s32[8,12]{1,0:T(8,128)} %cols_ref.1) | copy-start | bytes 1156
  9.1 39.9 %copy-start.3 = (s32[8]{0:T(128)S(1)}, s32[8]{0:T(128)}, u32[]{:S(2)}) copy-start(s32[8]{0:T(128)} %param.10) | copy-start | bytes 100
  9.7 12.3 %collective-permute-start.7 = (bf16[8,2,16,512]{3,2,1,0:T(8,128)(2,1)S(1)}, bf16[8,2,16,512]{3,2,1,0:T(8,128)(2,1)S(1)}, u32[]{:S(2)}, u32[]{:S(2)}) collective-permute-start(bf16[8,2,16,512]{3,2,1,0:T(8,128)(2,1)S(1)} %gate.3.refs_5_), channel_id=1, source_target_pairs={{0,1},{1,0},{2,3},{3,2},{4,5},{5,4},{6,7},{7,6},{8,9},{9,8},{10,11... | collective-permute-start | bytes 786440 | tf_op jit(solution)/shard_map/ppermute | solution.py:21
  10.7 38.3 %slice-start.1 = ((s8[6291456]{0:T(1024)(128)(4,1)}), s8[2097152]{0:T(1024)(128)(4,1)S(1)}, s32[]{:S(2)}) async-start(s8[6291456]{0:T(1024)(128)(4,1)} %bitcast.2), calls=%async_computation.1 | async-start | bytes 4194304
  10.7 11.2 %collective-permute-start.6 = (bf16[8,2,16,512]{3,2,1,0:T(8,128)(2,1)S(1)}, bf16[8,2,16,512]{3,2,1,0:T(8,128)(2,1)S(1)}, u32[]{:S(2)}, u32[]{:S(2)}) collective-permute-start(bf16[8,2,16,512]{3,2,1,0:T(8,128)(2,1)S(1)} %gate.2.refs_2_), channel_id=1, source_target_pairs={{0,3},{1,2},{2,1},{3,0},{4,7},{5,6},{6,5},{7,4},{8,11},{9,10},{10,... | collective-permute-start | bytes 786440 | tf_op jit(solution)/shard_map/ppermute | solution.py:21
  17.7 5.8 %collective-permute-start.4 = (bf16[9,32,128]{2,1,0:T(8,128)(2,1)S(1)}, bf16[9,32,128]{2,1,0:T(8,128)(2,1)S(1)}, u32[]{:S(2)}, u32[]{:S(2)}) collective-permute-start(bf16[9,32,128]{2,1,0:T(8,128)(2,1)S(1)} %get-tuple-element.9), channel_id=1, source_target_pairs={{0,1},{1,0},{2,3},{3,2},{4,5},{5,4},{6,7},{7,6},{8,9},{9,8},{10,11... | collective-permute-start | bytes 221192 | tf_op jit(solution)/shard_map/ppermute | solution.py:21
  18.0 5.6 %collective-permute-start.5 = (bf16[9,32,128]{2,1,0:T(8,128)(2,1)S(1)}, bf16[9,32,128]{2,1,0:T(8,128)(2,1)S(1)}, u32[]{:S(2)}, u32[]{:S(2)}) collective-permute-start(bf16[9,32,128]{2,1,0:T(8,128)(2,1)S(1)} %get-tuple-element.10), channel_id=1, source_target_pairs={{0,3},{1,2},{2,1},{3,0},{4,7},{5,6},{6,5},{7,4},{8,11},{9,10},{10,... | collective-permute-start | bytes 221192 | tf_op jit(solution)/shard_map/ppermute | solution.py:21
  22.8 4.8 %collective-permute-start.8 = (bf16[9,32,128]{2,1,0:T(8,128)(2,1)S(1)}, bf16[9,32,128]{2,1,0:T(8,128)(2,1)S(1)}, u32[]{:S(2)}, u32[]{:S(2)}) collective-permute-start(bf16[9,32,128]{2,1,0:T(8,128)(2,1)S(1)} %respond.5), channel_id=1, source_target_pairs={{0,2},{1,3},{2,0},{3,1},{4,6},{5,7},{6,4},{7,5},{8,10},{9,11},{10,... | collective-permute-start | bytes 221192 | tf_op jit(solution)/shard_map/ppermute | solution.py:20
  27.6 5.0 %collective-permute-start.9 = (f32[12,32,128]{2,1,0:T(8,128)S(1)}, f32[12,32,128]{2,1,0:T(8,128)S(1)}, u32[]{:S(2)}, u32[]{:S(2)}) collective-permute-start(f32[12,32,128]{2,1,0:T(8,128)S(1)} %stitch.1.mine_ref), channel_id=1, source_target_pairs={{0,4},{4,0},{8,12},{12,8},{16,20},{20,16},{24,28},{28,24},{32,36},... | collective-permute-start | bytes 589832 | tf_op jit(solution)/shard_map/ppermute | solution.py:26
  32.7 10.4 %collective-permute-start.10 = (bf16[20,32,128]{2,1,0:T(8,128)(2,1)S(1)}, bf16[20,32,128]{2,1,0:T(8,128)(2,1)S(1)}, u32[]{:S(2)}, u32[]{:S(2)}) collective-permute-start(bf16[20,32,128]{2,1,0:T(8,128)(2,1)S(1)} %get-tuple-element.11.chip_ref), channel_id=1, source_target_pairs={{0,8},{8,0},{12,20},{16,24},{20,12},{24,16},{28,36},{32,40},{36,28... | collective-permute-start | bytes 491528 | tf_op jit(solution)/shard_map/ppermute | solution.py:37
  40.4 6.6 %collective-permute-start.11 = (bf16[12,32,128]{2,1,0:T(8,128)(2,1)S(1)}, bf16[12,32,128]{2,1,0:T(8,128)(2,1)S(1)}, u32[]{:S(2)}, u32[]{:S(2)}) collective-permute-start(bf16[12,32,128]{2,1,0:T(8,128)(2,1)S(1)} %get-tuple-element.12), channel_id=1, source_target_pairs={{4,20},{12,28},{16,32},{20,4},{24,40},{28,12},{32,16},{36,52},{40,... | collective-permute-start | bytes 294920 | tf_op jit(solution)/shard_map/ppermute | solution.py:37
  43.1 5.9 %collective-permute-start.12 = (bf16[20,32,128]{2,1,0:T(8,128)(2,1)S(1)}, bf16[20,32,128]{2,1,0:T(8,128)(2,1)S(1)}, u32[]{:S(2)}, u32[]{:S(2)}) collective-permute-start(bf16[20,32,128]{2,1,0:T(8,128)(2,1)S(1)} %collective-permute-done.10.near_ref), channel_id=1, source_target_pairs={{0,4},{4,0},{8,12},{12,8},{16,20},{20,16},{24,28},{28,24},{32,36},... | collective-permute-start | bytes 491528 | tf_op jit(solution)/shard_map/ppermute | solution.py:26
  47.0 2.0 %collective-permute-start.13 = (bf16[12,32,128]{2,1,0:T(8,128)(2,1)S(1)}, bf16[12,32,128]{2,1,0:T(8,128)(2,1)S(1)}, u32[]{:S(2)}, u32[]{:S(2)}) collective-permute-start(bf16[12,32,128]{2,1,0:T(8,128)(2,1)S(1)} %collective-permute-done.11.far_ref), channel_id=1, source_target_pairs={{0,4},{4,0},{8,12},{12,8},{16,20},{20,16},{24,28},{28,24},{32,36},... | collective-permute-start | bytes 294920 | tf_op jit(solution)/shard_map/ppermute | solution.py:26

commit v6 on v5

--- a/solution.py
+++ b/solution.py
@@ -247,7 +247,8 @@
     one_low, two_high = gate(one_low, own), gate(two_high, own)
     across_low, across_high = angle_pairs(one_low, 1), angle_pairs(two_high, 0)
 
-    one, two = respond(jitter, response, [(one_low, one_high), (two_low, two_high)])
+    (one,) = respond(jitter, response, [(one_low, one_high)])
+    (two,) = respond(jitter, response, [(two_low, two_high)])
     (across,) = respond(jitter, response, [(across_low, across_high)])
     mine = stitch([own, angle_pairs(one, 0), angle_pairs(two, 1), angle_pairs(across, 2)])
 

time: 51 us -> 50.8 us (level)
  waiting for transfers between devices: 17.8 us -> 14.1 us
  starting transfers between devices: 24.2 us -> 27.3 us
    ppermute x8, waiting for transfers between devices: 8.49 us -> 5.57 us  [angle_pairs(): lax.ppermute(block, 'ang', [(a, ((a + shift ^ 1) - shift) % size) for a i...]
    ppermute x8, starting transfers between devices: 7.72 us -> 9.8 us  [angle_pairs(): lax.ppermute(block, 'ang', [(a, ((a + shift ^ 1) - shift) % size) for a i...]
    ppermute x1, starting transfers between devices: 0.42 us -> 1.48 us  [angle_pairs(): lax.ppermute(block, 'ang', [(a, (a + 2) % size) for a in range(size)])]
    ppermute x1, waiting for transfers between devices: 4 us -> 3.29 us  [angle_pairs(): lax.ppermute(block, 'ang', [(a, (a + 2) % size) for a in range(size)])]
    pallas_call x3 -> x4, Pallas kernels: 2.97 us -> 3.22 us  [respond(): pl.pallas_call(functools.partial(respond_kernel, len(groups), halves), ou...]
  transfers between devices with their start and end apart: 14 -> 14, of which waited for: 10 -> 7; matrix products, arithmetic and copies ran while one was open for 0% -> 0% of each run, Pallas kernels for 6% -> 6%
where the time goes in v6:
time: 50.8 us; the launch traced here: 50.6 us
  starting transfers between devices  27.3 us (54%)
  waiting for transfers between devices  14.1 us (28%)
  Pallas kernels  5.14 us (10%)
  local copies, waits for them, and re-layouts  3.93 us (8%)
    ppermute x8, starting transfers between devices, angle_pairs(): lax.ppermute(block, 'ang', [(a, ((a + shift ^ 1) - shift) % size) for a i...  9.8 us
    ppermute x2, starting transfers between devices, pairs(): return lax.ppermute(block, 'dom', route)  9.67 us
    ppermute x3, starting transfers between devices, other_core(): return lax.ppermute(block, 'dom', [(i, i ^ 1) for i in range(doms)])  6.36 us
    ppermute x8, waiting for transfers between devices, angle_pairs(): lax.ppermute(block, 'ang', [(a, ((a + shift ^ 1) - shift) % size) for a i...  5.57 us
    ppermute x1, waiting for transfers between devices, angle_pairs(): lax.ppermute(block, 'ang', [(a, (a + 2) % size) for a in range(size)])  3.29 us
    ppermute x2, waiting for transfers between devices, pairs(): return lax.ppermute(block, 'dom', route)  3.26 us
    pallas_call x4, Pallas kernels, respond(): pl.pallas_call(functools.partial(respond_kernel, len(groups), halves), ou...  3.22 us
    unnamed x12, local copies, waits for them, and re-layouts  2.87 us
  transfers between devices with their start and end apart: 14, of which 7 were waited for; matrix products, arithmetic and copies ran while one was open for 0% of the time, Pallas kernels for 6%

profile of v6, /device:TPU:7, one launch (start us, length us, event | category | flops | bytes accessed | tf_op | source)
XLA Modules:
  0.0 50.6 jit_solution(15075386457749078580)
XLA Ops:
  0.0 1.1 %fusion = (bf16[8,2,16,512]{3,2,1,0:T(8,128)(2,1)S(1)}, bf16[8,2,16,512]{3,2,1,0:T(8,128)(2,1)S(1)}) fusion(bf16[16,2,16,512]{3,2,1,0:T(8,128)(2,1)} %param.6), kind=kLoop, calls=%fused_computation | loop fusion | bytes 1048576 | tf_op jit(solution)/shard_map/slice | solution.py:243
  1.1 1.4 %collective-permute-start = (bf16[8,2,16,512]{3,2,1,0:T(8,128)(2,1)S(1)}, bf16[8,2,16,512]{3,2,1,0:T(8,128)(2,1)S(1)}, u32[]{:S(2)}, u32[]{:S(2)}) collective-permute-start(bf16[8,2,16,512]{3,2,1,0:T(8,128)(2,1)S(1)} %get-tuple-element.10.refs_2_), channel_id=1, source_target_pairs={{0,1},{1,0},{2,3},{3,2},{4,5},{5,4},{6,7},{7,6},{8,9},{9,8},{10,11... | collective-permute-start | bytes 786440 | tf_op jit(solution)/shard_map/ppermute | solution.py:21
  2.5 1.9 %collective-permute-start.4 = (bf16[8,2,16,512]{3,2,1,0:T(8,128)(2,1)S(1)}, bf16[8,2,16,512]{3,2,1,0:T(8,128)(2,1)S(1)}, u32[]{:S(2)}, u32[]{:S(2)}) collective-permute-start(bf16[8,2,16,512]{3,2,1,0:T(8,128)(2,1)S(1)} %get-tuple-element.9.refs_3_), channel_id=1, source_target_pairs={{0,3},{1,2},{2,1},{3,0},{4,7},{5,6},{6,5},{7,4},{8,11},{9,10},{10,... | collective-permute-start | bytes 786440 | tf_op jit(solution)/shard_map/ppermute | solution.py:21
  4.4 0.4 collective-permute-start.1
  4.8 0.6 %collective-permute-start.3 = (bf16[8,2,16,512]{3,2,1,0:T(8,128)(2,1)S(1)}, bf16[8,2,16,512]{3,2,1,0:T(8,128)(2,1)S(1)}, u32[]{:S(2)}, u32[]{:S(2)}) collective-permute-start(bf16[8,2,16,512]{3,2,1,0:T(8,128)(2,1)S(1)} %get-tuple-element.10.refs_2_), channel_id=1, source_target_pairs={{0,3},{1,2},{2,1},{3,0},{4,7},{5,6},{6,5},{7,4},{8,11},{9,10},{10,... | collective-permute-start | bytes 786440 | tf_op jit(solution)/shard_map/ppermute | solution.py:21
  5.4 0.0 copy-start
  5.4 2.2 %copy-done = bf16[16,2,512,128]{3,2,1,0:T(8,128)(2,1)S(1)} copy-done((bf16[16,2,512,128]{3,2,1,0:T(8,128)(2,1)S(1)}, bf16[16,2,512,128]{3,2,1,0:T(8,128)(2,1)}, u32[]{:S(2)}) %copy-start) | copy-done | bytes 4194328
  7.5 0.0 copy-start.1
  7.5 0.7 %copy-done.1 = s32[16]{0:T(128)S(1)} copy-done((s32[16]{0:T(128)S(1)}, s32[16]{0:T(128)}, u32[]{:S(2)}) %copy-start.1) | copy-done | bytes 88
  8.2 0.8 %respond.4.after_ref.refs_0_ = f32[9,32,128]{2,1,0:T(8,128)S(1)} custom-call(s32[1,16]{1,0:T(1,128)S(1)} %bitcast.4, bf16[16,2,512,128]{3,2,1,0:T(8,128)(2,1)S(1)} %copy-done, bf16[8,2,16,512]{3,2,1,0:T(8,128)(2,1)S(1)} %get-tuple-element.10.refs_2_, bf16[8,2,16,512]{3,2,1,0:T(8,128)(2,1)S(1)} %get-tuple-element.9.refs_3_), custom_call_target="tpu_custom_call" | custom-call | flops 134217728 | bytes 4194304 | tf_op jit(solution)/shard_map/respond/pallas_call | solution.py:99
  9.0 0.0 collective-permute-done.held_ref
  9.0 2.2 %collective-permute-start.6 = (bf16[8,2,16,512]{3,2,1,0:T(8,128)(2,1)S(1)}, bf16[8,2,16,512]{3,2,1,0:T(8,128)(2,1)S(1)}, u32[]{:S(2)}, u32[]{:S(2)}) collective-permute-start(bf16[8,2,16,512]{3,2,1,0:T(8,128)(2,1)S(1)} %gate.2.refs_2_), channel_id=1, source_target_pairs={{0,3},{1,2},{2,1},{3,0},{4,7},{5,6},{6,5},{7,4},{8,11},{9,10},{10,... | collective-permute-start | bytes 786440 | tf_op jit(solution)/shard_map/ppermute | solution.py:21
  11.2 0.0 collective-permute-done.4.held_ref
  11.2 0.0 collective-permute-start.7
  11.2 2.8 %collective-permute-done.1.refs_3_ = bf16[8,2,16,512]{3,2,1,0:T(8,128)(2,1)S(1)} collective-permute-done((bf16[8,2,16,512]{3,2,1,0:T(8,128)(2,1)S(1)}, bf16[8,2,16,512]{3,2,1,0:T(8,128)(2,1)S(1)}, u32[]{:S(2)}, u32[]{:S(2)}) %collective-permute-start.1) | collective-permute-done | bytes 262176 | tf_op jit(solution)/shard_map/ppermute | solution.py:21
  13.9 0.0 slice-start
  13.9 0.8 %respond.5 = bf16[9,32,128]{2,1,0:T(8,128)(2,1)S(1)} custom-call(s32[1,16]{1,0:T(1,128)S(1)} %bitcast.5, bf16[16,2,512,128]{3,2,1,0:T(8,128)(2,1)S(1)} %copy-done, bf16[8,2,16,512]{3,2,1,0:T(8,128)(2,1)S(1)} %gate.2.refs_2_, bf16[8,2,16,512]{3,2,1,0:T(8,128)(2,1)S(1)} %collective-permute-done.1.refs_3_), custom_call_target="tpu_custom_call" | custom-call | flops 134217728 | bytes 4194304 | tf_op jit(solution)/shard_map/respond/pallas_call | solution.py:99
  14.8 0.0 slice-start.1
  14.8 0.0 copy-start.2
  14.8 0.0 copy-start.3
  14.8 1.4 %collective-permute-start.2 = (bf16[9,32,128]{2,1,0:T(8,128)(2,1)S(1)}, bf16[9,32,128]{2,1,0:T(8,128)(2,1)S(1)}, u32[]{:S(2)}, u32[]{:S(2)}) collective-permute-start(bf16[9,32,128]{2,1,0:T(8,128)(2,1)S(1)} %respond.5), channel_id=1, source_target_pairs={{0,1},{1,0},{2,3},{3,2},{4,5},{5,4},{6,7},{7,6},{8,9},{9,8},{10,11... | collective-permute-start | bytes 221192 | tf_op jit(solution)/shard_map/ppermute | solution.py:21
  16.2 0.0 collective-permute-done.3.refs_2_
  16.2 0.8 %respond.6 = bf16[9,32,128]{2,1,0:T(8,128)(2,1)S(1)} custom-call(s32[1,16]{1,0:T(1,128)S(1)} %bitcast.6, bf16[16,2,512,128]{3,2,1,0:T(8,128)(2,1)S(1)} %copy-done, bf16[8,2,16,512]{3,2,1,0:T(8,128)(2,1)S(1)} %collective-permute-done.3.refs_2_, bf16[8,2,16,512]{3,2,1,0:T(8,128)(2,1)S(1)} %gate.3.refs_3_), custom_call_target="tpu_custom_call" | custom-call | flops 134217728 | bytes 4194304 | tf_op jit(solution)/shard_map/respond/pallas_call | solution.py:99
  17.0 2.0 %collective-permute-start.5 = (bf16[9,32,128]{2,1,0:T(8,128)(2,1)S(1)}, bf16[9,32,128]{2,1,0:T(8,128)(2,1)S(1)}, u32[]{:S(2)}, u32[]{:S(2)}) collective-permute-start(bf16[9,32,128]{2,1,0:T(8,128)(2,1)S(1)} %respond.6), channel_id=1, source_target_pairs={{0,3},{1,2},{2,1},{3,0},{4,7},{5,6},{6,5},{7,4},{8,11},{9,10},{10,... | collective-permute-start | bytes 221192 | tf_op jit(solution)/shard_map/ppermute | solution.py:21
  19.0 2.8 %collective-permute-done.6.refs_2_ = bf16[8,2,16,512]{3,2,1,0:T(8,128)(2,1)S(1)} collective-permute-done((bf16[8,2,16,512]{3,2,1,0:T(8,128)(2,1)S(1)}, bf16[8,2,16,512]{3,2,1,0:T(8,128)(2,1)S(1)}, u32[]{:S(2)}, u32[]{:S(2)}) %collective-permute-start.6) | collective-permute-done | bytes 262176 | tf_op jit(solution)/shard_map/ppermute | solution.py:21
  21.8 0.0 collective-permute-done.7.refs_3_
  21.8 0.8 %respond.7 = bf16[9,32,128]{2,1,0:T(8,128)(2,1)S(1)} custom-call(s32[1,16]{1,0:T(1,128)S(1)} %bitcast.7, bf16[16,2,512,128]{3,2,1,0:T(8,128)(2,1)S(1)} %copy-done, bf16[8,2,16,512]{3,2,1,0:T(8,128)(2,1)S(1)} %collective-permute-done.6.refs_2_, bf16[8,2,16,512]{3,2,1,0:T(8,128)(2,1)S(1)} %collective-permute-done.7.refs_3_), custom_call_target="tpu_custom_call" | custom-call | flops 134217728 | bytes 4194304 | tf_op jit(solution)/shard_map/respond/pallas_call | solution.py:99
  22.6 1.5 %collective-permute-start.8 = (bf16[9,32,128]{2,1,0:T(8,128)(2,1)S(1)}, bf16[9,32,128]{2,1,0:T(8,128)(2,1)S(1)}, u32[]{:S(2)}, u32[]{:S(2)}) collective-permute-start(bf16[9,32,128]{2,1,0:T(8,128)(2,1)S(1)} %respond.7), channel_id=1, source_target_pairs={{0,2},{1,3},{2,0},{3,1},{4,6},{5,7},{6,4},{7,5},{8,10},{9,11},{10,... | collective-permute-start | bytes 221192 | tf_op jit(solution)/shard_map/ppermute | solution.py:20
  24.0 0.0 collective-permute-done.2.refs_1_
  24.0 0.0 collective-permute-done.5.refs_2_
  24.1 3.3 %collective-permute-done.8.refs_3_ = bf16[9,32,128]{2,1,0:T(8,128)(2,1)S(1)} collective-permute-done((bf16[9,32,128]{2,1,0:T(8,128)(2,1)S(1)}, bf16[9,32,128]{2,1,0:T(8,128)(2,1)S(1)}, u32[]{:S(2)}, u32[]{:S(2)}) %collective-permute-start.8) | collective-permute-done | bytes 73760 | tf_op jit(solution)/shard_map/ppermute | solution.py:20
  27.3 0.1 stitch.1.mine_ref
  27.4 3.9 %collective-permute-start.9 = (f32[12,32,128]{2,1,0:T(8,128)S(1)}, f32[12,32,128]{2,1,0:T(8,128)S(1)}, u32[]{:S(2)}, u32[]{:S(2)}) collective-permute-start(f32[12,32,128]{2,1,0:T(8,128)S(1)} %stitch.1.mine_ref), channel_id=1, source_target_pairs={{0,4},{4,0},{8,12},{12,8},{16,20},{20,16},{24,28},{28,24},{32,36},... | collective-permute-start | bytes 589832 | tf_op jit(solution)/shard_map/ppermute | solution.py:26
  31.3 1.1 %collective-permute-done.9.other_ref = f32[12,32,128]{2,1,0:T(8,128)S(1)} collective-permute-done((f32[12,32,128]{2,1,0:T(8,128)S(1)}, f32[12,32,128]{2,1,0:T(8,128)S(1)}, u32[]{:S(2)}, u32[]{:S(2)}) %collective-permute-start.9) | collective-permute-done | bytes 196640 | tf_op jit(solution)/shard_map/ppermute | solution.py:26
  32.4 7.7 %collective-permute-start.10 = (bf16[20,32,128]{2,1,0:T(8,128)(2,1)S(1)}, bf16[20,32,128]{2,1,0:T(8,128)(2,1)S(1)}, u32[]{:S(2)}, u32[]{:S(2)}) collective-permute-start(bf16[20,32,128]{2,1,0:T(8,128)(2,1)S(1)} %get-tuple-element.7.chip_ref), channel_id=1, source_target_pairs={{0,8},{8,0},{12,20},{16,24},{20,12},{24,16},{28,36},{32,40},{36,28... | collective-permute-start | bytes 491528 | tf_op jit(solution)/shard_map/ppermute | solution.py:37
  40.2 1.9 %collective-permute-start.11 = (bf16[12,32,128]{2,1,0:T(8,128)(2,1)S(1)}, bf16[12,32,128]{2,1,0:T(8,128)(2,1)S(1)}, u32[]{:S(2)}, u32[]{:S(2)}) collective-permute-start(bf16[12,32,128]{2,1,0:T(8,128)(2,1)S(1)} %get-tuple-element.8), channel_id=1, source_target_pairs={{4,20},{12,28},{16,32},{20,4},{24,40},{28,12},{32,16},{36,52},{40,... | collective-permute-start | bytes 294920 | tf_op jit(solution)/shard_map/ppermute | solution.py:37
  42.1 0.8 %collective-permute-done.10.near_ref = bf16[20,32,128]{2,1,0:T(8,128)(2,1)S(1)} collective-permute-done((bf16[20,32,128]{2,1,0:T(8,128)(2,1)S(1)}, bf16[20,32,128]{2,1,0:T(8,128)(2,1)S(1)}, u32[]{:S(2)}, u32[]{:S(2)}) %collective-permute-start.10) | collective-permute-done | bytes 163872 | tf_op jit(solution)/shard_map/ppermute | solution.py:37
  42.9 1.4 %collective-permute-start.12 = (bf16[20,32,128]{2,1,0:T(8,128)(2,1)S(1)}, bf16[20,32,128]{2,1,0:T(8,128)(2,1)S(1)}, u32[]{:S(2)}, u32[]{:S(2)}) collective-permute-start(bf16[20,32,128]{2,1,0:T(8,128)(2,1)S(1)} %collective-permute-done.10.near_ref), channel_id=1, source_target_pairs={{0,4},{4,0},{8,12},{12,8},{16,20},{20,16},{24,28},{28,24},{32,36},... | collective-permute-start | bytes 491528 | tf_op jit(solution)/shard_map/ppermute | solution.py:26
  44.3 2.5 %collective-permute-done.11.far_ref = bf16[12,32,128]{2,1,0:T(8,128)(2,1)S(1)} collective-permute-done((bf16[12,32,128]{2,1,0:T(8,128)(2,1)S(1)}, bf16[12,32,128]{2,1,0:T(8,128)(2,1)S(1)}, u32[]{:S(2)}, u32[]{:S(2)}) %collective-permute-start.11) | collective-permute-done | bytes 98336 | tf_op jit(solution)/shard_map/ppermute | solution.py:37
  46.8 1.0 %collective-permute-start.13 = (bf16[12,32,128]{2,1,0:T(8,128)(2,1)S(1)}, bf16[12,32,128]{2,1,0:T(8,128)(2,1)S(1)}, u32[]{:S(2)}, u32[]{:S(2)}) collective-permute-start(bf16[12,32,128]{2,1,0:T(8,128)(2,1)S(1)} %collective-permute-done.11.far_ref), channel_id=1, source_target_pairs={{0,4},{4,0},{8,12},{12,8},{16,20},{20,16},{24,28},{28,24},{32,36},... | collective-permute-start | bytes 294920 | tf_op jit(solution)/shard_map/ppermute | solution.py:26
  47.8 0.9 %collective-permute-done.13.swap_far_ref = bf16[12,32,128]{2,1,0:T(8,128)(2,1)S(1)} collective-permute-done((bf16[12,32,128]{2,1,0:T(8,128)(2,1)S(1)}, bf16[12,32,128]{2,1,0:T(8,128)(2,1)S(1)}, u32[]{:S(2)}, u32[]{:S(2)}) %collective-permute-start.13) | collective-permute-done | bytes 98336 | tf_op jit(solution)/shard_map/ppermute | solution.py:26
  48.8 0.0 collective-permute-done.12.swap_near_ref
  48.8 0.0 slice-done
  48.8 0.0 slice-done.1
  48.8 0.0 copy-done.2
  48.8 0.0 copy-done.3
  48.8 1.8 %couple.1 = f32[2,16,1024]{2,1,0:T(8,128)} custom-call(s32[8,12]{1,0:T(8,128)S(1)} %copy-done.2, s32[1,8]{1,0:T(1,128)S(1)} %bitcast.8, bf16[8,12,2,128,128]{4,3,2,1,0:T(8,128)(2,1)S(1)} %bitcast.3, bf16[20,32,128]{2,1,0:T(8,128)(2,1)S(1)} %get-tuple-element.7.chip_ref, bf16[20,32,128]{2,1,0:T(8,128)(2,1)S(1)} %collective-permute-done.10.near_ref, ...), custom_call_target="tpu_custom_call" | custom-call | flops 201326592 | bytes 6291456 | tf_op jit(solution)/shard_map/couple/pallas_call | solution.py:229
  (4 shorter events, 0.0 us)
Async XLA Ops:
  1.1 7.9 %collective-permute-start = (bf16[8,2,16,512]{3,2,1,0:T(8,128)(2,1)S(1)}, bf16[8,2,16,512]{3,2,1,0:T(8,128)(2,1)S(1)}, u32[]{:S(2)}, u32[]{:S(2)}) collective-permute-start(bf16[8,2,16,512]{3,2,1,0:T(8,128)(2,1)S(1)} %get-tuple-element.10.refs_2_), channel_id=1, source_target_pairs={{0,1},{1,0},{2,3},{3,2},{4,5},{5,4},{6,7},{7,6},{8,9},{9,8},{10,11... | collective-permute-start | bytes 786440 | tf_op jit(solution)/shard_map/ppermute | solution.py:21
  2.5 8.7 %collective-permute-start.4 = (bf16[8,2,16,512]{3,2,1,0:T(8,128)(2,1)S(1)}, bf16[8,2,16,512]{3,2,1,0:T(8,128)(2,1)S(1)}, u32[]{:S(2)}, u32[]{:S(2)}) collective-permute-start(bf16[8,2,16,512]{3,2,1,0:T(8,128)(2,1)S(1)} %get-tuple-element.9.refs_3_), channel_id=1, source_target_pairs={{0,3},{1,2},{2,1},{3,0},{4,7},{5,6},{6,5},{7,4},{8,11},{9,10},{10,... | collective-permute-start | bytes 786440 | tf_op jit(solution)/shard_map/ppermute | solution.py:21
  4.4 9.6 %collective-permute-start.1 = (bf16[8,2,16,512]{3,2,1,0:T(8,128)(2,1)S(1)}, bf16[8,2,16,512]{3,2,1,0:T(8,128)(2,1)S(1)}, u32[]{:S(2)}, u32[]{:S(2)}) collective-permute-start(bf16[8,2,16,512]{3,2,1,0:T(8,128)(2,1)S(1)} %get-tuple-element.9.refs_3_), channel_id=1, source_target_pairs={{0,1},{1,0},{2,3},{3,2},{4,5},{5,4},{6,7},{7,6},{8,9},{9,8},{10,11... | collective-permute-start | bytes 786440 | tf_op jit(solution)/shard_map/ppermute | solution.py:21
  4.8 11.4 %collective-permute-start.3 = (bf16[8,2,16,512]{3,2,1,0:T(8,128)(2,1)S(1)}, bf16[8,2,16,512]{3,2,1,0:T(8,128)(2,1)S(1)}, u32[]{:S(2)}, u32[]{:S(2)}) collective-permute-start(bf16[8,2,16,512]{3,2,1,0:T(8,128)(2,1)S(1)} %get-tuple-element.10.refs_2_), channel_id=1, source_target_pairs={{0,3},{1,2},{2,1},{3,0},{4,7},{5,6},{6,5},{7,4},{8,11},{9,10},{10,... | collective-permute-start | bytes 786440 | tf_op jit(solution)/shard_map/ppermute | solution.py:21
  5.4 2.2 %copy-start = (bf16[16,2,512,128]{3,2,1,0:T(8,128)(2,1)S(1)}, bf16[16,2,512,128]{3,2,1,0:T(8,128)(2,1)}, u32[]{:S(2)}) copy-start(bf16[16,2,512,128]{3,2,1,0:T(8,128)(2,1)} %refs_1_.7) | copy-start | bytes 12582916
  7.5 0.7 %copy-start.1 = (s32[16]{0:T(128)S(1)}, s32[16]{0:T(128)}, u32[]{:S(2)}) copy-start(s32[16]{0:T(128)} %param.8) | copy-start | bytes 196
  9.0 12.7 %collective-permute-start.6 = (bf16[8,2,16,512]{3,2,1,0:T(8,128)(2,1)S(1)}, bf16[8,2,16,512]{3,2,1,0:T(8,128)(2,1)S(1)}, u32[]{:S(2)}, u32[]{:S(2)}) collective-permute-start(bf16[8,2,16,512]{3,2,1,0:T(8,128)(2,1)S(1)} %gate.2.refs_2_), channel_id=1, source_target_pairs={{0,3},{1,2},{2,1},{3,0},{4,7},{5,6},{6,5},{7,4},{8,11},{9,10},{10,... | collective-permute-start | bytes 786440 | tf_op jit(solution)/shard_map/ppermute | solution.py:21
  11.2 10.6 %collective-permute-start.7 = (bf16[8,2,16,512]{3,2,1,0:T(8,128)(2,1)S(1)}, bf16[8,2,16,512]{3,2,1,0:T(8,128)(2,1)S(1)}, u32[]{:S(2)}, u32[]{:S(2)}) collective-permute-start(bf16[8,2,16,512]{3,2,1,0:T(8,128)(2,1)S(1)} %gate.3.refs_3_), channel_id=1, source_target_pairs={{0,1},{1,0},{2,3},{3,2},{4,5},{5,4},{6,7},{7,6},{8,9},{9,8},{10,11... | collective-permute-start | bytes 786440 | tf_op jit(solution)/shard_map/ppermute | solution.py:21
  13.9 34.8 %slice-start = ((s8[6291456]{0:T(1024)(128)(4,1)}), s8[4194304]{0:T(1024)(128)(4,1)S(1)}, s32[]{:S(2)}) async-start(s8[6291456]{0:T(1024)(128)(4,1)} %bitcast.2), calls=%async_computation | async-start | bytes 8388608
  14.8 34.0 %slice-start.1 = ((s8[6291456]{0:T(1024)(128)(4,1)}), s8[2097152]{0:T(1024)(128)(4,1)S(1)}, s32[]{:S(2)}) async-start(s8[6291456]{0:T(1024)(128)(4,1)} %bitcast.2), calls=%async_computation.1 | async-start | bytes 4194304
  14.8 34.0 %copy-start.2 = (s32[8,12]{1,0:T(8,128)S(1)}, s32[8,12]{1,0:T(8,128)}, u32[]{:S(2)}) copy-start(s32[8,12]{1,0:T(8,128)} %cols_ref.1) | copy-start | bytes 1156
  14.8 34.0 %copy-start.3 = (s32[8]{0:T(128)S(1)}, s32[8]{0:T(128)}, u32[]{:S(2)}) copy-start(s32[8]{0:T(128)} %param.10) | copy-start | bytes 100
  14.8 9.3 %collective-permute-start.2 = (bf16[9,32,128]{2,1,0:T(8,128)(2,1)S(1)}, bf16[9,32,128]{2,1,0:T(8,128)(2,1)S(1)}, u32[]{:S(2)}, u32[]{:S(2)}) collective-permute-start(bf16[9,32,128]{2,1,0:T(8,128)(2,1)S(1)} %respond.5), channel_id=1, source_target_pairs={{0,1},{1,0},{2,3},{3,2},{4,5},{5,4},{6,7},{7,6},{8,9},{9,8},{10,11... | collective-permute-start | bytes 221192 | tf_op jit(solution)/shard_map/ppermute | solution.py:21
  17.0 7.1 %collective-permute-start.5 = (bf16[9,32,128]{2,1,0:T(8,128)(2,1)S(1)}, bf16[9,32,128]{2,1,0:T(8,128)(2,1)S(1)}, u32[]{:S(2)}, u32[]{:S(2)}) collective-permute-start(bf16[9,32,128]{2,1,0:T(8,128)(2,1)S(1)} %respond.6), channel_id=1, source_target_pairs={{0,3},{1,2},{2,1},{3,0},{4,7},{5,6},{6,5},{7,4},{8,11},{9,10},{10,... | collective-permute-start | bytes 221192 | tf_op jit(solution)/shard_map/ppermute | solution.py:21
  22.6 4.8 %collective-permute-start.8 = (bf16[9,32,128]{2,1,0:T(8,128)(2,1)S(1)}, bf16[9,32,128]{2,1,0:T(8,128)(2,1)S(1)}, u32[]{:S(2)}, u32[]{:S(2)}) collective-permute-start(bf16[9,32,128]{2,1,0:T(8,128)(2,1)S(1)} %respond.7), channel_id=1, source_target_pairs={{0,2},{1,3},{2,0},{3,1},{4,6},{5,7},{6,4},{7,5},{8,10},{9,11},{10,... | collective-permute-start | bytes 221192 | tf_op jit(solution)/shard_map/ppermute | solution.py:20
  27.4 5.0 %collective-permute-start.9 = (f32[12,32,128]{2,1,0:T(8,128)S(1)}, f32[12,32,128]{2,1,0:T(8,128)S(1)}, u32[]{:S(2)}, u32[]{:S(2)}) collective-permute-start(f32[12,32,128]{2,1,0:T(8,128)S(1)} %stitch.1.mine_ref), channel_id=1, source_target_pairs={{0,4},{4,0},{8,12},{12,8},{16,20},{20,16},{24,28},{28,24},{32,36},... | collective-permute-start | bytes 589832 | tf_op jit(solution)/shard_map/ppermute | solution.py:26
  32.4 10.4 %collective-permute-start.10 = (bf16[20,32,128]{2,1,0:T(8,128)(2,1)S(1)}, bf16[20,32,128]{2,1,0:T(8,128)(2,1)S(1)}, u32[]{:S(2)}, u32[]{:S(2)}) collective-permute-start(bf16[20,32,128]{2,1,0:T(8,128)(2,1)S(1)} %get-tuple-element.7.chip_ref), channel_id=1, source_target_pairs={{0,8},{8,0},{12,20},{16,24},{20,12},{24,16},{28,36},{32,40},{36,28... | collective-permute-start | bytes 491528 | tf_op jit(solution)/shard_map/ppermute | solution.py:37
  40.2 6.6 %collective-permute-start.11 = (bf16[12,32,128]{2,1,0:T(8,128)(2,1)S(1)}, bf16[12,32,128]{2,1,0:T(8,128)(2,1)S(1)}, u32[]{:S(2)}, u32[]{:S(2)}) collective-permute-start(bf16[12,32,128]{2,1,0:T(8,128)(2,1)S(1)} %get-tuple-element.8), channel_id=1, source_target_pairs={{4,20},{12,28},{16,32},{20,4},{24,40},{28,12},{32,16},{36,52},{40,... | collective-permute-start | bytes 294920 | tf_op jit(solution)/shard_map/ppermute | solution.py:37
  42.9 5.9 %collective-permute-start.12 = (bf16[20,32,128]{2,1,0:T(8,128)(2,1)S(1)}, bf16[20,32,128]{2,1,0:T(8,128)(2,1)S(1)}, u32[]{:S(2)}, u32[]{:S(2)}) collective-permute-start(bf16[20,32,128]{2,1,0:T(8,128)(2,1)S(1)} %collective-permute-done.10.near_ref), channel_id=1, source_target_pairs={{0,4},{4,0},{8,12},{12,8},{16,20},{20,16},{24,28},{28,24},{32,36},... | collective-permute-start | bytes 491528 | tf_op jit(solution)/shard_map/ppermute | solution.py:26
  46.8 2.0 %collective-permute-start.13 = (bf16[12,32,128]{2,1,0:T(8,128)(2,1)S(1)}, bf16[12,32,128]{2,1,0:T(8,128)(2,1)S(1)}, u32[]{:S(2)}, u32[]{:S(2)}) collective-permute-start(bf16[12,32,128]{2,1,0:T(8,128)(2,1)S(1)} %collective-permute-done.11.far_ref), channel_id=1, source_target_pairs={{0,4},{4,0},{8,12},{12,8},{16,20},{20,16},{24,28},{28,24},{32,36},... | collective-permute-start | bytes 294920 | tf_op jit(solution)/shard_map/ppermute | solution.py:26
